TPU v7x, 32 devices: a whole 2x2x4 slice. The times are simulated.
32 devices in a mesh: groups: 2 (over y), seq: 16 (over z, x, core).
Axes of the slice: x: 2, y: 2, z: 4, core: 2. Of those that a mesh axis runs over, the one named last changes fastest.
Arguments:
- q_lin: bfloat16 [16384, 128], P(('groups', 'seq')), parts along dimension 0, may hold values from -6 to 6
- k_lin: bfloat16 [16384, 128], P(('groups', 'seq')), parts along dimension 0, may hold values from -6 to 6
- v_lin: bfloat16 [16384, 512], P(('groups', 'seq')), parts along dimension 0, may hold values from -6 to 6
- q_win: bfloat16 [16384, 2048], P(('groups', 'seq')), parts along dimension 0, may hold values from -10 to 10
- k_win: bfloat16 [16384, 2048], P(('groups', 'seq')), parts along dimension 0, may hold values from -10 to 10
- v_win: bfloat16 [16384, 2048], P(('groups', 'seq')), parts along dimension 0, may hold values from -6 to 6
Outputs:
- lin_out: bfloat16 [16384, 512], P(('groups', 'seq')), parts along dimension 0
- win_out: bfloat16 [16384, 2048], P(('groups', 'seq')), parts along dimension 0
There are 2 independent parts, one for each index of `groups`. A program takes and returns all parts, laid end to end along the dimension named above; each array names one. Nothing has to cross between parts.
All inputs are finite; a program needn't handle non-finite values.
Results may differ from a plain program's by a relative error of at most 0.005.
Values may be sent and summed in bfloat16 or wider, within the bound.
No kernel may reach another device: no remote copies, remote signals or barrier semaphores. Data moves between devices by JAX's collectives and lax.ppermute only.
A program may use at most 192 MiB of HBM per device.

v0:
```python
import math

import jax
import jax.numpy as jnp
from jax import lax
from jax.sharding import PartitionSpec as P

HEADS = 8
KDIM = 16
VDIM = 64
WHEADS = 16
WDIM = 128
WINDOW = 64


highest = lax.Precision.HIGHEST


def prefix(part, axis, combine, identity):
    place = lax.axis_index(axis)
    gathered = jax.tree.map(lambda a: lax.all_gather(a, axis), part)
    state = jax.tree.map(lambda a, e: jnp.zeros_like(a) + jnp.asarray(e, a.dtype), part, identity)

    def one(lap, state):
        return combine(
            state, jax.tree.map(lambda a: lax.dynamic_index_in_dim(a, lap, 0, False), gathered)
        )

    return lax.fori_loop(0, place, one, state)


def from_behind(value, axis, steps):
    count = lax.axis_size(axis)
    initial, last = (max(0, -steps), min(count, count - steps))
    return lax.ppermute(value, axis, [(source, source + steps) for source in range(initial, last)])


def expand_full(scaled):
    head_count, key_width, tok_count = scaled.shape
    ones_part = jnp.ones((head_count, 1, tok_count), jnp.float32)
    square = (scaled[:, :, None, :] * scaled[:, None, :, :]).reshape(
        head_count, key_width * key_width, tok_count
    ) * (1.0 / math.sqrt(2.0))
    return jnp.concatenate([ones_part, scaled, square], axis=1)


def add_states(earlier, later):
    return (earlier[0] + later[0], earlier[1] + later[1])


def body(q_lin, k_lin, v_lin, q_win, k_win, v_win):
    tok_count = q_lin.shape[0]
    root = float(KDIM) ** 0.25
    query_scaled = q_lin.astype(jnp.float32).T.reshape(HEADS, KDIM, tok_count) / root
    key_scaled = k_lin.astype(jnp.float32).T.reshape(HEADS, KDIM, tok_count) / root
    values = v_lin.astype(jnp.float32).reshape(tok_count, HEADS, VDIM)
    query_feats = expand_full(query_scaled)
    key_feats = expand_full(key_scaled)
    feat_count = key_feats.shape[1]
    local_state = jnp.einsum("hft,thv->fhv", key_feats, values, precision=highest).reshape(
        feat_count, HEADS * VDIM
    )
    local_norm = jnp.sum(key_feats, axis=2)
    identity = (jnp.zeros_like(local_state), jnp.zeros_like(local_norm))
    carried_state, carried_norm = prefix((local_state, local_norm), "seq", add_states, identity)
    edges = from_behind((k_win[-WINDOW:], v_win[-WINDOW:]), "seq", 1)
    similar = jnp.einsum("hkt,hks->hts", query_scaled, key_scaled, precision=highest)
    position = jnp.arange(tok_count)
    causal = position[:, None] >= position[None, :]
    kernel = jnp.where(causal[None], 1.0 + similar + 0.5 * similar * similar, 0.0)
    numerator = jnp.einsum("hts,shv->thv", kernel, values, precision=highest)
    numerator = numerator + jnp.einsum(
        "hft,fhv->thv",
        query_feats,
        carried_state.reshape(feat_count, HEADS, VDIM),
        precision=highest,
    )
    denominator = jnp.sum(kernel, axis=2) + jnp.einsum(
        "hft,hf->ht", query_feats, carried_norm, precision=highest
    )
    lin_out = (
        (numerator / denominator.T[:, :, None])
        .reshape(tok_count, HEADS * VDIM)
        .astype(jnp.bfloat16)
    )
    block_count = tok_count // WINDOW
    keys_ext = jnp.concatenate([edges[0], k_win], axis=0).reshape(
        block_count + 1, WINDOW, WHEADS, WDIM
    )
    vals_ext = jnp.concatenate([edges[1], v_win], axis=0).reshape(
        block_count + 1, WINDOW, WHEADS, WDIM
    )
    keys_pair = jnp.concatenate([keys_ext[:-1], keys_ext[1:]], axis=1)
    vals_pair = jnp.concatenate([vals_ext[:-1], vals_ext[1:]], axis=1)
    queries = q_win.reshape(block_count, WINDOW, WHEADS, WDIM)
    scores = jnp.einsum(
        "bthd,bshd->bhts", queries, keys_pair, preferred_element_type=jnp.float32
    ) / math.sqrt(WDIM)
    query_pos = jnp.arange(WINDOW)[:, None]
    key_pos = jnp.arange(2 * WINDOW)[None, :]
    band = (key_pos > query_pos) & (key_pos <= query_pos + WINDOW)
    leading = lax.axis_index("seq") == 0
    first_block = (jnp.arange(block_count) == 0)[:, None, None]
    allowed = band[None] & jnp.logical_not(leading & first_block & (key_pos < WINDOW)[None])
    scores = jnp.where(allowed[:, None], scores, -jnp.inf)
    peak = jnp.max(scores, axis=3, keepdims=True)
    expo = jnp.exp(scores - peak)
    weights = (expo / jnp.sum(expo, axis=3, keepdims=True)).astype(jnp.bfloat16)
    window_sum = jnp.einsum(
        "bhts,bshd->bthd", weights, vals_pair, preferred_element_type=jnp.float32
    )
    win_out = window_sum.astype(jnp.bfloat16).reshape(tok_count, WHEADS * WDIM)
    return (lin_out, win_out)


def solution(mesh):
    in_specs = (
        P(("groups", "seq"), None),
        P(("groups", "seq"), None),
        P(("groups", "seq"), None),
        P(("groups", "seq"), None),
        P(("groups", "seq"), None),
        P(("groups", "seq"), None),
    )
    out_specs = (P(("groups", "seq"), None), P(("groups", "seq"), None))
    return jax.shard_map(body, mesh=mesh, in_specs=in_specs, out_specs=out_specs, check_vma=False)
```

profile of v0, /device:TPU:27, one launch (start us, length us, event | category | flops | bytes accessed | tf_op | source)
XLA Modules:
  0.0 136.7 jit_solution(17282133605729136626)
XLA Ops:
  8.3 2.7 %multiply_multiply_fusion.2 = f32[8,16,16,512]{3,2,1,0:T(8,128)} fusion(f32[8,16,512]{2,1,0:T(8,128)S(1)} %bitcast.89), kind=kLoop, calls=%fused_computation.22 | loop fusion | flops 2097152 | bytes 4456448 | tf_op jit(solution)/shard_map/mul | solution.py:41
  12.1 5.3 %fusion.21 = f32[8,273,64]{1,2,0:T(8,128)S(1)} fusion(bf16[512,8,64]{0,2,1:T(8,128)(2,1)} %bitcast.103, f32[8,256,512]{2,1,0:T(8,128)} %bitcast.79, f32[8,16,512]{2,1,0:T(8,128)S(1)} %bitcast.90, f32[273]{0:T(512)S(1)} %pad.11.clone), kind=kOutput, calls=%fused_computation.30 | convolution fusion | flops 861020160 | bytes 5540932 | tf_op jit(solution)/shard_map/hft,thv->fhv/dot_general | solution.py:60
  19.3 1.3 collective-permute-start.1
  20.5 1.7 %slice.26 = bf16[64,2048]{1,0:T(8,128)(2,1)} slice(bf16[512,2048]{1,0:T(8,128)(2,1)} %param.13), slice={[448:512], [0:2048]} | slice | bytes 524288 | tf_op jit(solution)/shard_map/slice | solution.py:66
  22.2 1.5 %collective-permute-start = (bf16[64,2048]{1,0:T(8,128)(2,1)}, bf16[64,2048]{1,0:T(8,128)(2,1)S(1)}, u32[]{:S(2)}, u32[]{:S(2)}) collective-permute-start(bf16[64,2048]{1,0:T(8,128)(2,1)} %slice.26), channel_id=1, source_target_pairs={{0,1},{1,2},{2,3},{3,4},{4,5},{5,6},{6,7},{7,8},{8,9},{9,10},{10,1... | collective-permute-start | bytes 786440 | tf_op jit(solution)/shard_map/ppermute | solution.py:35
  24.2 3.0 %fusion.20 = f32[8,273]{1,0:T(8,128)S(1)} fusion(f32[8,256,512]{2,1,0:T(8,128)} %bitcast.80, f32[8,16,512]{2,1,0:T(8,128)S(1)} %bitcast.91, f32[273]{0:T(512)S(1)} %pad.11.clone), kind=kLoop, calls=%fused_computation.29 | loop fusion | flops 3352440 | bytes 4466276 | tf_op jit(solution)/shard_map/reduce_sum | solution.py:63
  27.1 2.7 %multiply_multiply_fusion.1 = f32[8,16,16,512]{3,2,1,0:T(8,128)} fusion(f32[8,16,512]{2,1,0:T(8,128)S(1)} %bitcast.95), kind=kLoop, calls=%fused_computation.21 | loop fusion | flops 2097152 | bytes 4456448 | tf_op jit(solution)/shard_map/mul | solution.py:41
  29.9 8.3 %fusion.3 = (f32[8,512]{1,0:T(8,128)S(1)}, f32[8,512,512]{1,2,0:T(8,128)S(1)}) fusion(pred[512,512]{0,1:T(8,128)(4,1)S(1)} %iota_compare_fusion, f32[8,16,512]{2,1,0:T(8,128)S(1)} %bitcast.96, f32[8,16,512]{2,1,0:T(8,128)S(1)} %bitcast.92), kind=kOutput, calls=%fused_computation.6 | convolution fusion | flops 415232000 | bytes 9191424 | tf_op jit(solution)/shard_map/hkt,hks->hts/dot_general | solution.py:67
  38.2 5.9 %fusion.37 = f32[512,8,64]{0,2,1:T(8,128)} fusion(bf16[512,8,64]{0,2,1:T(8,128)(2,1)S(1)} %bitcast.104, f32[8,512,512]{1,2,0:T(8,128)S(1)} %get-tuple-element.57, pred[512,512]{0,1:T(8,128)(4,1)S(1)} %iota_compare_fusion), kind=kOutput, calls=%fused_computation.48 | convolution fusion | flops 1621098496 | bytes 10223616 | tf_op jit(solution)/shard_map/hts,shv->thv/dot_general | solution.py:71
  47.8 19.9 %all-gather = f32[128,273]{1,0:T(8,128)S(1)} all-gather(f32[8,273]{1,0:T(8,128)S(1)} %fusion.20), channel_id=2, replica_groups=mesh['groups'=2,'seq'=16] {'seq'}, dimensions={0}, use_global_device_ids=true | all-gather | bytes 148512 | tf_op jit(solution)/shard_map/all_gather | solution.py:21
  70.4 3.0 %fusion.6 = f32[8,16,128,64]{2,3,1,0:T(8,128)S(1)} fusion(bf16[8,64,16,128]{3,1,2,0:T(8,128)(2,1)S(1)} %copy.39, bf16[8,64,16,128]{3,1,2,0:T(8,128)(2,1)S(1)} %copy.38, bf16[8,64,16,128]{3,2,1,0:T(8,128)(2,1)S(1)} %bitcast.83), kind=kOutput, calls=%fused_computation.10 | convolution fusion | flops 276824064 | bytes 10485760 | tf_op jit(solution)/shard_map/bthd,bshd->bhts/dot_general | solution.py:96
  73.4 2.9 %fusion.53 = (f32[8,16,64]{2,1,0:T(8,128)S(1)}, f32[8,16,64,128]{3,2,1,0:T(8,128)S(1)}) fusion(f32[8,16,128,64]{2,3,1,0:T(8,128)S(1)} %fusion.6, pred[8,64,128]{2,1,0:T(8,128)(4,1)S(1)} %broadcast_and_fusion), kind=kOutput, calls=%fused_computation.74 | output fusion | flops 6291583 | bytes 8486912 | tf_op jit(solution)/shard_map/sub | solution.py:107
  76.2 1.9 %convert_bitcast_fusion = bf16[8,64,16,128]{3,1,2,0:T(8,128)(2,1)S(1)} fusion(bf16[8,64,16,128]{3,1,2,0:T(8,128)(2,1)S(1)} %copy.37, bf16[8,64,16,128]{3,1,2,0:T(8,128)(2,1)S(1)} %copy.36, f32[8,16,64,128]{3,2,1,0:T(8,128)S(1)} %get-tuple-element.59, f32[8,16,64]{2,1,0:T(8,128)S(1)} %get-tuple-element.58), kind=kOutput, calls=%fused_computation.41 | convolution fusion | flops 279969792 | bytes 10518528 | tf_op jit(solution)/shard_map/bhts,bshd->bthd/dot_general | solution.py:109
  78.2 1.4 copy.41
  79.5 1.9 %copy.58 = bf16[64,8,16,128]{3,1,2,0:T(8,128)(2,1)} copy(bf16[64,8,16,128]{3,2,1,0:T(8,128)(2,1)S(1)} %bitcast.86) | data formatting | bytes 4194304
  81.4 17.9 %all-gather.3.cloned.1.call-done = f32[16,273,512]{2,1,0:T(8,128)} async-done(((f32[1,273,512]{2,1,0:T(8,128)}), f32[16,273,512]{2,1,0:T(8,128)}) %all-gather.3.cloned.1.call-update) | async-done | bytes 8945680 | tf_op jit(solution)/shard_map/all_gather | solution.py:21
  99.3 19.2 %while.12 = (s32[]{:T(128)}, f32[273,512]{1,0:T(8,128)S(1)}, f32[8,273]{1,0:T(8,128)S(1)}, s32[]{:T(128)}, f32[16,273,512]{2,1,0:T(8,128)}, /*index=5*/f32[16,8,273]{2,1,0:T(8,128)S(1)}, s32[]{:T(128)}, s32[]{:T(128)}, s32[]{:T(128)}) while((s32[]{:T(128)}, f32[273,512]{1,0:T(8,128)S(1)}, f32[8,273]{1,0:T(8,128)S(1)}, s32[]{:T(128)}, ...), condition=%wide.region_2.3_spmd, body=%wide.region_1.2_spmd.sunk | while | flops 141965 | bytes 1703655 | solution.py:29
  99.4 1.2 bitcast_add_fusion.5
  100.6 1.2 bitcast_add_fusion.5
  101.9 1.2 bitcast_add_fusion.5
  103.1 1.2 bitcast_add_fusion.5
  114.5 1.2 bitcast_add_fusion.5
  118.8 5.9 %fusion.18 = f32[8,1,512]{2,1,0:T(1,128)S(1)} fusion(f32[8,256,512]{2,1,0:T(8,128)} %bitcast.93, f32[8,16,512]{2,1,0:T(8,128)S(1)} %bitcast.97, f32[273]{0:T(512)S(1)} %pad.11.clone, f32[8,273,1]{1,0,2:T(8,128)S(1)} %bitcast.106), kind=kOutput, calls=%fused_computation.27 | convolution fusion | flops 15654912 | bytes 4482660 | tf_op jit(solution)/shard_map/hft,hf->ht/dot_general | solution.py:78
  124.7 4.1 %divide_convert_fusion.4 = bf16[512,8,64]{0,2,1:T(8,128)(2,1)S(1)} fusion(f32[512,8,64]{0,2,1:T(8,128)S(1)} %copy-done.7, f32[273,8,64]{0,2,1:T(8,128)S(1)} %bitcast.101, f32[8,256,512]{2,1,0:T(8,128)S(1)} %bitcast.94, f32[8,16,512]{2,1,0:T(8,128)S(1)} %bitcast.98, f32[273]{0:T(512)S(1)} %pad.11.clone, f32[512,8]{0,1:T(8,128)S(1)} %fusion.41), kind=kOutput, calls=%fused_computation.49 | convolution fusion | flops 861806592 | bytes 6605892 | tf_op jit(solution)/shard_map/hft,fhv->thv/dot_general | solution.py:72
  (76 shorter events, 24.3 us)
Async XLA Ops:
  7.2 3.9 %copy-start.4 = (bf16[512,512]{1,0:T(8,128)(2,1)S(1)}, bf16[512,512]{1,0:T(8,128)(2,1)}, u32[]{:S(2)}) copy-start(bf16[512,512]{1,0:T(8,128)(2,1)} %param.10) | copy-start | bytes 1572868
  7.2 92.1 %all-gather.3.cloned.1.call-start = ((), (), s32[]{:S(2)}) async-start(), calls=%async_computation | async-start | bytes 9748480 | tf_op jit(solution)/shard_map/all_gather | solution.py:21
  12.1 6.5 %copy-start = (bf16[512,2048]{1,0:T(8,128)(2,1)S(1)}, bf16[512,2048]{1,0:T(8,128)(2,1)}, u32[]{:S(2)}) copy-start(bf16[512,2048]{1,0:T(8,128)(2,1)} %param.12) | copy-start | bytes 6291460
  12.1 11.6 %copy-start.6 = (bf16[512,128]{1,0:T(8,128)(2,1)S(1)}, bf16[512,128]{1,0:T(8,128)(2,1)}, u32[]{:S(2)}) copy-start(bf16[512,128]{1,0:T(8,128)(2,1)} %param.8) | copy-start | bytes 393220
  19.3 48.4 %collective-permute-start.1 = (bf16[64,2048]{1,0:T(8,128)(2,1)}, bf16[64,2048]{1,0:T(8,128)(2,1)S(1)}, u32[]{:S(2)}, u32[]{:S(2)}) collective-permute-start(bf16[64,2048]{1,0:T(8,128)(2,1)} %slice.30), channel_id=1, source_target_pairs={{0,1},{1,2},{2,3},{3,4},{4,5},{5,6},{6,7},{7,8},{8,9},{9,10},{10,1... | collective-permute-start | bytes 786440 | tf_op jit(solution)/shard_map/ppermute | solution.py:35
  22.2 46.9 %collective-permute-start = (bf16[64,2048]{1,0:T(8,128)(2,1)}, bf16[64,2048]{1,0:T(8,128)(2,1)S(1)}, u32[]{:S(2)}, u32[]{:S(2)}) collective-permute-start(bf16[64,2048]{1,0:T(8,128)(2,1)} %slice.26), channel_id=1, source_target_pairs={{0,1},{1,2},{2,3},{3,4},{4,5},{5,6},{6,7},{7,8},{8,9},{9,10},{10,1... | collective-permute-start | bytes 786440 | tf_op jit(solution)/shard_map/ppermute | solution.py:35
  29.9 8.3 %copy-start.5 = (bf16[512,512]{0,1:T(8,128)(2,1)S(1)}, bf16[512,512]{0,1:T(8,128)(2,1)}, u32[]{:S(2)}) copy-start(bf16[512,512]{0,1:T(8,128)(2,1)} %copy.32) | copy-start | bytes 1572868
  44.2 1.6 %copy-start.3 = (bf16[512,2048]{1,0:T(8,128)(2,1)S(1)}, bf16[512,2048]{1,0:T(8,128)(2,1)}, u32[]{:S(2)}) copy-start(bf16[512,2048]{1,0:T(8,128)(2,1)} %param.11) | copy-start | bytes 6291460
  44.8 1.8 %copy-start.1 = (bf16[512,2048]{1,0:T(8,128)(2,1)S(1)}, bf16[512,2048]{1,0:T(8,128)(2,1)}, u32[]{:S(2)}) copy-start(bf16[512,2048]{1,0:T(8,128)(2,1)} %param.13) | copy-start | bytes 6291460
  118.6 6.2 %copy-start.7 = (f32[512,8,64]{0,2,1:T(8,128)S(1)}, f32[512,8,64]{0,2,1:T(8,128)}, u32[]{:S(2)}) copy-start(f32[512,8,64]{0,2,1:T(8,128)} %fusion.37) | copy-start | bytes 3145732
  118.8 5.9 %copy-start.2 = (f32[8,16,16,512]{3,2,1,0:T(8,128)S(1)}, f32[8,16,16,512]{3,2,1,0:T(8,128)}, u32[]{:S(2)}) copy-start(f32[8,16,16,512]{3,2,1,0:T(8,128)} %multiply_multiply_fusion.1) | copy-start | bytes 12582916
Sparse Core Ops, SparseCore 0:
  18.7 80.5 all-gather.2
where the time goes:
time: 138 us; the launch traced here: 137 us
  matrix products  34.4 us (25%)
  other arithmetic  31.4 us (23%)
  blocking collectives  19.9 us (14%)
  waiting for transfers between devices  17.9 us (13%)
  local copies, waits for them, and re-layouts  15.2 us (11%)
  between operations  14.4 us (10%)
  starting transfers between devices  2.78 us (2%)
    all_gather x1, blocking collectives, prefix(): gathered = jax.tree.map(lambda a: lax.all_gather(a, axis), part)  19.9 us
    add x30, other arithmetic, add_states(): return (earlier[0] + later[0], earlier[1] + later[1])  18.4 us
    all_gather x1, waiting for transfers between devices, prefix(): gathered = jax.tree.map(lambda a: lax.all_gather(a, axis), part)  17.9 us
    dot_general x1, matrix products, body(): jnp.einsum('hkt,hks->hts', query_scaled, key_scaled, precision=highest)  8.33 us
    unnamed x24, local copies, waits for them, and re-layouts  7.57 us
    dot_general x1, matrix products, body(): numerator = jnp.einsum('hts,shv->thv', kernel, values, precision=highest)  5.94 us
    dot_general x1, matrix products, body(): jnp.einsum('hft,hf->ht', query_feats, carried_norm, precision=highest)  5.85 us
    mul x2, other arithmetic, expand_full(): (scaled[:, :, None, :] * scaled[:, None, :, :]).reshape(head_count, key_w...  5.46 us
  transfers between devices with their start and end apart: 3, of which 1 were waited for; matrix products, arithmetic and copies ran while one was open for 29% of the time, Pallas kernels for 0%

commit v1 on v0

v1 whole, which is shorter than its diff:
```python
import math

import jax
import jax.numpy as jnp
from jax import lax
from jax.experimental import pallas as pl
from jax.experimental.pallas import tpu as pltpu
from jax.sharding import PartitionSpec as P

HEADS = 8
KDIM = 16
VDIM = 64
WHEADS = 16
WDIM = 128
WINDOW = 64

BF = jnp.bfloat16
F32 = jnp.float32
BLOCKS = 10
PAIRS = BLOCKS // 2
MAIN = PAIRS * 64
ROWS = MAIN + 16
STEP = 256
COEF = (1 / 32,) + (1 / 16,) * 7 + (1 / 32, 1 / 4)
VMEM = pl.BlockSpec(memory_space=pltpu.VMEM)


def lanes(shape):
    return lax.broadcasted_iota(jnp.int32, shape, len(shape) - 1)


def rows_of(shape):
    return lax.broadcasted_iota(jnp.int32, shape, len(shape) - 2)


def feature(x, d):
    if d == 9:
        return x
    if d == 0:
        return x * x
    low = lanes(x.shape) % KDIM < KDIM - d
    other = jnp.where(low, pltpu.roll(x, 128 - d, 1), pltpu.roll(x, KDIM - d, 1))
    return x * other


def halves(first, second):
    left = lanes(first.shape) < 64
    return (
        jnp.where(left, first, pltpu.roll(second, 64, 1)),
        jnp.where(left, pltpu.roll(first, 64, 1), second),
    )


def put_features(x, coef, fa, fb):
    sums = []
    for p in range(PAIRS):
        blocks = [feature(x, d) * coef[d] for d in (2 * p, 2 * p + 1)]
        sums.append([jnp.sum(b, axis=0, keepdims=True) for b in blocks])
        a, b = halves(*blocks)
        fa[:, p * 128 : (p + 1) * 128] = a.astype(BF)
        fb[:, p * 128 : (p + 1) * 128] = b.astype(BF)
    return sums


def state_kernel(k_hbm, v_hbm, s_ref, fa, fb, kbuf, vbuf, sems):
    copies = [
        pltpu.make_async_copy(src, dst, sems.at[n])
        for n, (src, dst) in enumerate(((k_hbm, kbuf), (v_hbm, vbuf)))
    ]
    for copy in copies:
        copy.start()
    copies[0].wait()
    sums = put_features(kbuf[...].astype(F32), (1.0,) * BLOCKS, fa, fb)
    zs = [halves(*pair) for pair in sums]
    copies[1].wait()
    v = vbuf[...]
    vsum = jnp.sum(v.astype(F32), axis=0, keepdims=True)
    left = lanes((64, 128)) < 64
    even = (rows_of((64, 128)) // KDIM) % 2 == 0
    for half, f in ((0, fa), (1, fb)):
        r = lax.dot_general(
            f[...],
            v[:, half * 256 : (half + 1) * 256],
            (((0,), (0,)), ((), ())),
            preferred_element_type=F32,
        )
        for p in range(PAIRS):
            pieces = []
            for par in range(2):
                at = p * 128 + par * 64
                z = jnp.concatenate(
                    [r[at : at + 32, :128], r[at + 32 : at + 64, 128:]], axis=0
                )
                keep = even if par == 0 else jnp.logical_not(even)
                pieces.append(jnp.where(keep, z, pltpu.roll(z, 64, 1)))
            s_ref[half, p * 64 : (p + 1) * 64, :] = jnp.where(left, *pieces).astype(BF)
        aux = [z[half] for z in zs]
        aux += [vsum[:, half * 256 + t * 128 : half * 256 + (t + 1) * 128] for t in range(2)]
        aux.append(jnp.zeros((ROWS - MAIN - PAIRS - 2, 128), F32))
        s_ref[half, MAIN:, :] = jnp.concatenate(aux, axis=0).astype(BF)


def query_kernel(q_ref, fa, fb):
    put_features(q_ref[...].astype(F32), COEF, fa, fb)


def local_kernel(q_ref, k_ref, v_ref, num_ref, den_ref):
    tok = q_ref.shape[0]
    step = STEP
    k = k_ref[...]
    lane = lanes((step, 128))
    left = lane < 64
    left_all = lanes((tok, 128)) < 64
    causal = rows_of((step, step)) >= lanes((step, step))
    one = jnp.ones((tok, 128), BF)
    for t in range(HEADS // 2):
        vt = v_ref[:, t * 128 : (t + 1) * 128]
        aug = (jnp.where(left_all, vt, one), jnp.where(left_all, one, vt))
        for r in range(tok // step):
            q = q_ref[r * step : (r + 1) * step, :]
            outs = []
            for e in range(2):
                qm = jnp.where(lane // KDIM == 2 * t + e, q, jnp.zeros_like(q))
                end = (r + 1) * step
                u = lax.dot_general(
                    qm, k[:end, :], (((1,), (1,)), ((), ())), preferred_element_type=F32
                )
                w = u + 4.0
                w = w * w * (1 / 32) + 0.5
                diag = jnp.where(causal, w[:, r * step :], 0.0).astype(BF)
                if r:
                    w = jnp.concatenate([w[:, : r * step].astype(BF), diag], axis=1)
                else:
                    w = diag
                outs.append(jnp.dot(w, aug[e][:end, :], preferred_element_type=F32))
            num_ref[r * step : (r + 1) * step, t * 128 : (t + 1) * 128] = jnp.where(
                left, outs[0], outs[1]
            )
            den_ref[r * step : (r + 1) * step, t * 128 : (t + 1) * 128] = pltpu.roll(
                jnp.where(left, outs[1], outs[0]), 64, 1
            )


def finish_kernel(fa, fb, own_ref, other_ref, peer_ref, num_ref, den_ref, o_ref, pa, pb):
    tok = fa.shape[0]
    me = lax.axis_index("seq")
    second = me % 2 == 1
    own = own_ref[...].astype(F32)
    other = other_ref[...].astype(F32)
    left = lanes((64, 128)) < 64
    row = rows_of((64, 128)) // KDIM
    col = lanes((64, 128)) // VDIM
    span = ((rows_of((256, 256)) // KDIM) % 4 == lanes((256, 256)) // VDIM).astype(BF)
    count = (me * tok).astype(F32)
    for half, f, dst in ((0, fa, pa), (1, fb, pb)):
        state = jnp.where(second == (half == 1), own, other)
        state = state + jnp.where(second, peer_ref[half].astype(F32), 0.0)
        for p in range(PAIRS):
            c = state[p * 64 : (p + 1) * 64, :]
            turned = pltpu.roll(c, 64, 1)
            for par in range(2):
                base = jnp.where(left, c, turned) if par == 0 else jnp.where(left, turned, c)
                at = p * 128 + par * 64
                for t in range(2):
                    dst[at : at + 64, t * 128 : (t + 1) * 128] = jnp.where(
                        row == col + 2 * t, base, 0.0
                    ).astype(BF)
        cols = slice(half * 256, (half + 1) * 256)
        acc = jnp.zeros((tok, 128), F32)
        for p in range(PAIRS):
            acc = acc + f[:, p * 128 : (p + 1) * 128].astype(F32) * state[MAIN + p : MAIN + p + 1, :]
        high = acc.astype(BF)
        both = jnp.concatenate([high, (acc - high.astype(F32)).astype(BF)], axis=1)
        den = jnp.dot(both, span, preferred_element_type=F32) + den_ref[:, cols] + count
        at = MAIN + PAIRS
        vsum = jnp.concatenate([state[at : at + 1, :], state[at + 1 : at + 2, :]], axis=1)
        num = jnp.dot(f[...], dst[...], preferred_element_type=F32)
        o_ref[:, cols] = ((num + num_ref[:, cols] + vsum) / den).astype(BF)


SCALE = 1.0 / (math.sqrt(WDIM) * math.log(2.0))
QB = 2 * WINDOW


def masks():
    row, lane = rows_of((QB, QB)), lanes((QB, QB))
    earlier = (row < WINDOW) & (lane >= WINDOW)
    key = jnp.where(earlier, lane, lane + QB) - QB
    return earlier, key, (key <= row) & (key > row - WINDOW)


def attend(blocks, earlier, bias):
    s = jnp.stack(
        [
            lax.dot_general(q, k, (((1,), (1,)), ((), ())), preferred_element_type=F32)
            for q, k, v in blocks
        ]
    )
    s = jnp.where(earlier, s[:, :, :QB], s[:, :, QB:]) * SCALE + bias
    e = jnp.exp2(s - jnp.max(s, axis=2, keepdims=True))
    inverse = 1.0 / jnp.sum(e, axis=2, keepdims=True)
    e = jnp.concatenate([jnp.where(earlier, e, 0.0), jnp.where(earlier, 0.0, e)], axis=2).astype(BF)
    return [
        (jnp.dot(e[n], v, preferred_element_type=F32) * inverse[n]).astype(BF)
        for n, (q, k, v) in enumerate(blocks)
    ]


def window_kernel(q_ref, k_ref, v_ref, *refs):
    o_ref = refs[-1]
    earlier, _, allowed = masks()
    bias = jnp.where(allowed, 0.0, -jnp.inf)
    starts = range(QB, q_ref.shape[0], QB)
    for h in range(q_ref.shape[1] // WDIM):
        cols = slice(h * WDIM, (h + 1) * WDIM)
        outs = attend(
            [
                (q_ref[at : at + QB, cols], k_ref[at - QB : at + QB, cols], v_ref[at - QB : at + QB, cols])
                for at in starts
            ],
            earlier,
            bias,
        )
        for at, out in zip(starts, outs):
            o_ref[at : at + QB, cols] = out


def edge_kernel(q_ref, k_ref, v_ref, h_ref, whole_ref, o_ref):
    first = lax.axis_index("seq") == 0
    earlier, key, allowed = masks()
    bias = jnp.where(allowed & ((key >= 0) | jnp.logical_not(first)), 0.0, -jnp.inf)
    for h in range(q_ref.shape[1] // WDIM):
        cols = slice(h * WDIM, (h + 1) * WDIM)
        kh, vh = h_ref[:WINDOW, cols], h_ref[WINDOW:, cols]
        k = jnp.concatenate([kh, kh, k_ref[:, cols]], axis=0)
        v = jnp.concatenate([vh, vh, v_ref[:, cols]], axis=0)
        o_ref[:, cols] = attend([(q_ref[:, cols], k, v)], earlier, bias)[0]


def halo_kernel(k_ref, v_ref, o_ref, sems):
    tok = k_ref.shape[0]
    copies = [
        pltpu.make_async_copy(
            ref.at[pl.ds(tok - WINDOW, WINDOW)], o_ref.at[pl.ds(n * WINDOW, WINDOW)], sems.at[n]
        )
        for n, ref in enumerate((k_ref, v_ref))
    ]
    for copy in copies:
        copy.start()
    for copy in copies:
        copy.wait()


def call(kernel, out, *args, flops=0, nbytes=0, vmem=16, **kw):
    return pl.pallas_call(
        kernel,
        out_shape=out,
        cost_estimate=pl.CostEstimate(flops=flops, bytes_accessed=nbytes, transcendentals=0),
        compiler_params=pltpu.CompilerParams(vmem_limit_bytes=vmem << 20),
        **kw,
    )(*args)


def exchange(x, step):
    count = lax.axis_size("seq")
    return lax.ppermute(x, "seq", [(i, i ^ step) for i in range(count)])


def shape(*dims, dtype=BF):
    return jax.ShapeDtypeStruct(dims, dtype)


def body(q_lin, k_lin, v_lin, q_win, k_win, v_win):
    tok = q_lin.shape[0]
    count = lax.axis_size("seq")
    assert count & (count - 1) == 0 and count > 1
    me = lax.axis_index("seq")
    second = me % 2 == 1
    wide = WHEADS * WDIM
    hbm = pl.BlockSpec(memory_space=pltpu.HBM)
    feats = pltpu.VMEM((tok, PAIRS * 128), BF)

    def window(group, groups, earlier):
        cols = wide // groups
        width = 512
        block = pl.BlockSpec((tok, width), lambda i: (0, group * (cols // width) + i))
        extra = () if earlier is None else (earlier,)
        return call(
            window_kernel,
            shape(tok, wide),
            q_win,
            k_win,
            v_win,
            *extra,
            grid=(cols // width,),
            in_specs=[block] * 3 + [hbm] * len(extra),
            out_specs=block,
            input_output_aliases={3: 0} if extra else {},
            flops=(1 << 31) // groups,
            nbytes=(8 << 20) // groups,
        )

    def halo():
        edge = call(
            halo_kernel,
            shape(2 * WINDOW, wide),
            k_win,
            v_win,
            in_specs=[hbm, hbm],
            out_specs=VMEM,
            scratch_shapes=[pltpu.SemaphoreType.DMA((2,))],
            nbytes=1 << 20,
        )
        return lax.ppermute(edge, "seq", [(i, (i + 1) % count) for i in range(count)])

    def local(q, k, v):
        return call(
            local_kernel,
            (shape(tok, HEADS * VDIM, dtype=F32),) * 2,
            q,
            k,
            v,
            in_specs=[VMEM] * 3,
            out_specs=(VMEM, VMEM),
            flops=1 << 31,
            nbytes=3 << 20,
        )

    edge = halo()
    state = call(
        state_kernel,
        shape(2, ROWS, 128),
        k_lin,
        v_lin,
        in_specs=[hbm] * 2,
        out_specs=VMEM,
        scratch_shapes=[feats] * 2
        + [pltpu.VMEM(k_lin.shape, BF), pltpu.VMEM(v_lin.shape, BF), pltpu.SemaphoreType.DMA((2,))],
        flops=1 << 30,
        nbytes=1 << 20,
    )
    peer = exchange(state, 1)
    qa, qb = call(
        query_kernel,
        (shape(tok, PAIRS * 128),) * 2,
        q_lin,
        in_specs=[VMEM],
        out_specs=(VMEM, VMEM),
        flops=1 << 28,
        nbytes=1 << 20,
    )
    both = state.astype(F32) + peer.astype(F32)
    carried = jnp.where(second, both[1], both[0])
    before = jnp.zeros_like(carried)
    win = None
    step, turn = 2, 0
    lin = (q_lin, k_lin, v_lin)
    num = den = None
    while step < count:
        if turn == 0:
            carried, lin = lax.optimization_barrier((carried, lin))
        got = exchange(carried.astype(BF), step)
        if turn == 0:
            num, den = local(*lin)
            got, num, den = lax.optimization_barrier((got, num, den))
        elif turn < 3:
            win = window(turn - 1, 2, win)
            got, win = lax.optimization_barrier((got, win))
        got = got.astype(F32)
        before = before + jnp.where((me & step) != 0, got, 0.0)
        carried = carried + got
        step *= 2
        turn += 1
    own = before.astype(BF)
    other = exchange(own, 1)
    top = pl.BlockSpec((QB, wide), lambda i: (0, 0))
    win_out = call(
        edge_kernel,
        shape(tok, wide),
        q_win,
        k_win,
        v_win,
        edge,
        win,
        grid=(1,),
        in_specs=[top] * 4 + [hbm],
        out_specs=top,
        input_output_aliases={4: 0},
        flops=1 << 28,
        nbytes=1 << 20,
    )
    lin_out = call(
        finish_kernel,
        shape(tok, HEADS * VDIM),
        qa,
        qb,
        own,
        other,
        peer,
        num,
        den,
        in_specs=[VMEM] * 7,
        out_specs=VMEM,
        scratch_shapes=[pltpu.VMEM((PAIRS * 128, 256), BF)] * 2,
        flops=1 << 30,
        nbytes=3 << 20,
    )
    return (lin_out, win_out)


def solution(mesh):
    spec = P(("groups", "seq"), None)
    return jax.shard_map(
        body, mesh=mesh, in_specs=(spec,) * 6, out_specs=(spec, spec), check_vma=False
    )
```

time: 138 us -> 36.9 us (0.27)
  the two profiles are of different devices: /device:TPU:27 before, /device:TPU:0 now
where the time goes in v1:
time: 36.9 us; the launch traced here: 36.7 us
  Pallas kernels  16.6 us (45%)
  starting transfers between devices  11.7 us (32%)
  local copies, waits for them, and re-layouts  6.54 us (18%)
  waiting for transfers between devices  0.8 us (2%)
  between operations  0.74 us (2%)
    pallas_call x8, Pallas kernels, call(): pl.pallas_call(kernel, out_shape=out, cost_estimate=pl.CostEstimate(flops...  16.6 us
    ppermute x5, starting transfers between devices, exchange(): return lax.ppermute(x, 'seq', [(i, i ^ step) for i in range(count)])  11.6 us
    unnamed x18, local copies, waits for them, and re-layouts  6.54 us
    ppermute x5, waiting for transfers between devices, exchange(): return lax.ppermute(x, 'seq', [(i, i ^ step) for i in range(count)])  0.79 us
  transfers between devices with their start and end apart: 6, of which 1 were waited for; matrix products, arithmetic and copies ran while one was open for 1% of the time, Pallas kernels for 35%

profile of v1, /device:TPU:0, one launch (start us, length us, event | category | flops | bytes accessed | tf_op | source)
XLA Modules:
  0.0 36.7 jit_solution(10455980245331813812)
XLA Ops:
  0.6 0.0 copy-start.4
  0.7 1.2 %copy-done.4 = bf16[512,512]{1,0:T(8,128)(2,1)S(1)} copy-done((bf16[512,512]{1,0:T(8,128)(2,1)S(1)}, bf16[512,512]{1,0:T(8,128)(2,1)}, u32[]{:S(2)}) %copy-start.4) | copy-done | bytes 524312
  1.8 0.9 %copy-done.6 = bf16[512,128]{1,0:T(8,128)(2,1)S(1)} copy-done((bf16[512,128]{1,0:T(8,128)(2,1)S(1)}, bf16[512,128]{1,0:T(8,128)(2,1)}, u32[]{:S(2)}) %copy-start.6) | copy-done | bytes 131096
  2.7 2.0 %shard_map.78 = bf16[2,336,128]{2,1,0:T(8,128)(2,1)S(1)} custom-call(bf16[512,128]{1,0:T(8,128)(2,1)S(1)} %copy-done.6, bf16[512,512]{1,0:T(8,128)(2,1)S(1)} %copy-done.4), custom_call_target="tpu_custom_call" | custom-call | flops 1073741824 | bytes 1048576 | tf_op jit(solution)/shard_map/pallas_call | solution.py:255
  4.7 0.5 %collective-permute-start = (bf16[2,336,128]{2,1,0:T(8,128)(2,1)S(1)}, bf16[2,336,128]{2,1,0:T(8,128)(2,1)S(1)}, u32[]{:S(2)}, u32[]{:S(2)}) collective-permute-start(bf16[2,336,128]{2,1,0:T(8,128)(2,1)S(1)} %shard_map.78), channel_id=1, source_target_pairs={{0,1},{1,0},{2,3},{3,2},{4,5},{5,4},{6,7},{7,6},{8,9},{9,8},{10,11... | collective-permute-start | bytes 516104 | tf_op jit(solution)/shard_map/ppermute | solution.py:266
  5.3 1.6 %copy-done.1 = bf16[512,2048]{1,0:T(8,128)(2,1)S(1)} copy-done((bf16[512,2048]{1,0:T(8,128)(2,1)S(1)}, bf16[512,2048]{1,0:T(8,128)(2,1)}, u32[]{:S(2)}) %copy-start.1) | copy-done | bytes 2097176
  6.9 0.1 shard_map.83
  6.9 0.1 collective-permute-start.5
  7.1 3.0 %collective-permute-start.1 = (bf16[336,128]{1,0:T(8,128)(2,1)S(1)}, bf16[336,128]{1,0:T(8,128)(2,1)S(1)}, u32[]{:S(2)}, u32[]{:S(2)}) collective-permute-start(bf16[336,128]{1,0:T(8,128)(2,1)S(1)} %convert_element_type.29), channel_id=1, source_target_pairs={{0,2},{1,3},{2,0},{3,1},{4,6},{5,7},{6,4},{7,5},{8,10},{9,11},{10,... | collective-permute-start | bytes 258056 | tf_op jit(solution)/shard_map/ppermute | solution.py:266
  10.1 1.0 %copy-done.5 = bf16[512,512]{1,0:T(8,128)(2,1)S(1)} copy-done((bf16[512,512]{1,0:T(8,128)(2,1)S(1)}, bf16[512,512]{1,0:T(8,128)(2,1)}, u32[]{:S(2)}) %copy-start.5) | copy-done | bytes 524312
  11.2 0.9 %copy-done.7 = bf16[512,128]{1,0:T(8,128)(2,1)S(1)} copy-done((bf16[512,128]{1,0:T(8,128)(2,1)S(1)}, bf16[512,128]{1,0:T(8,128)(2,1)}, u32[]{:S(2)}) %copy-start.7) | copy-done | bytes 131096
  12.1 0.9 %copy-done.8 = bf16[512,128]{1,0:T(8,128)(2,1)S(1)} copy-done((bf16[512,128]{1,0:T(8,128)(2,1)S(1)}, bf16[512,128]{1,0:T(8,128)(2,1)}, u32[]{:S(2)}) %copy-start.8) | copy-done | bytes 131096
  13.0 2.6 %shard_map.79 = (f32[512,512]{1,0:T(8,128)S(1)}, f32[512,512]{1,0:T(8,128)S(1)}) custom-call(bf16[512,128]{1,0:T(8,128)(2,1)S(1)} %copy-done.8, bf16[512,128]{1,0:T(8,128)(2,1)S(1)} %copy-done.7, bf16[512,512]{1,0:T(8,128)(2,1)S(1)} %copy-done.5), custom_call_target="tpu_custom_call" | custom-call | flops 2147483648 | bytes 3145728 | tf_op jit(solution)/shard_map/pallas_call | solution.py:255
  15.6 5.4 %collective-permute-start.2 = (bf16[336,128]{1,0:T(8,128)(2,1)S(1)}, bf16[336,128]{1,0:T(8,128)(2,1)S(1)}, u32[]{:S(2)}, u32[]{:S(2)}) collective-permute-start(bf16[336,128]{1,0:T(8,128)(2,1)S(1)} %fusion.5), channel_id=1, source_target_pairs={{0,4},{1,5},{2,6},{3,7},{4,0},{5,1},{6,2},{7,3},{8,12},{9,13},{10,... | collective-permute-start | bytes 258056 | tf_op jit(solution)/shard_map/ppermute | solution.py:266
  21.0 3.6 %shard_map.80.refs_0_ = bf16[512,2048]{1,0:T(8,128)(2,1)} custom-call(bf16[512,2048]{1,0:T(8,128)(2,1)S(1)} %copy-done.3, bf16[512,2048]{1,0:T(8,128)(2,1)S(1)} %copy-done, bf16[512,2048]{1,0:T(8,128)(2,1)S(1)} %copy-done.2), custom_call_target="tpu_custom_call" | custom-call | flops 1073741824 | bytes 4194304 | tf_op jit(solution)/shard_map/pallas_call | solution.py:255
  24.6 2.7 %collective-permute-start.3 = (bf16[336,128]{1,0:T(8,128)(2,1)S(1)}, bf16[336,128]{1,0:T(8,128)(2,1)S(1)}, u32[]{:S(2)}, u32[]{:S(2)}) collective-permute-start(bf16[336,128]{1,0:T(8,128)(2,1)S(1)} %fusion.3), channel_id=1, source_target_pairs={{0,8},{1,9},{2,10},{3,11},{4,12},{5,13},{6,14},{7,15},{8,0},{9,1},... | collective-permute-start | bytes 258056 | tf_op jit(solution)/shard_map/ppermute | solution.py:266
  27.3 3.6 %shard_map.81.whole_ref = bf16[512,2048]{1,0:T(8,128)(2,1)} custom-call(bf16[512,2048]{1,0:T(8,128)(2,1)S(1)} %copy-done.3, bf16[512,2048]{1,0:T(8,128)(2,1)S(1)} %copy-done, bf16[512,2048]{1,0:T(8,128)(2,1)S(1)} %copy-done.2, bf16[512,2048]{1,0:T(8,128)(2,1)} %shard_map.80.refs_0_), custom_call_target="tpu_custom_call", output_to_operand_aliasing={{}: (3, {})} | custom-call | flops 1073741824 | bytes 4194304 | tf_op jit(solution)/shard_map/pallas_call | solution.py:255
  30.8 0.7 %collective-permute-done.3 = bf16[336,128]{1,0:T(8,128)(2,1)S(1)} collective-permute-done((bf16[336,128]{1,0:T(8,128)(2,1)S(1)}, bf16[336,128]{1,0:T(8,128)(2,1)S(1)}, u32[]{:S(2)}, u32[]{:S(2)}) %collective-permute-start.3) | collective-permute-done | bytes 86048 | tf_op jit(solution)/shard_map/ppermute | solution.py:266
  31.6 0.1 fusion.2.own_ref
  31.6 0.1 collective-permute-start.4
  31.7 1.2 %shard_map.77 = (bf16[512,640]{1,0:T(8,128)(2,1)S(1)}, bf16[512,640]{1,0:T(8,128)(2,1)S(1)}) custom-call(bf16[512,128]{1,0:T(8,128)(2,1)S(1)} %copy-done.8), custom_call_target="tpu_custom_call" | custom-call | flops 268435456 | bytes 1048576 | tf_op jit(solution)/shard_map/pallas_call | solution.py:255
  32.9 0.0 collective-permute-done.4.other_ref
  33.0 1.8 %shard_map.82 = bf16[512,512]{1,0:T(8,128)(2,1)} custom-call(bf16[512,640]{1,0:T(8,128)(2,1)S(1)} %get-tuple-element.17.fa, bf16[512,640]{1,0:T(8,128)(2,1)S(1)} %get-tuple-element.18.fb, bf16[336,128]{1,0:T(8,128)(2,1)S(1)} %fusion.2.own_ref, bf16[336,128]{1,0:T(8,128)(2,1)S(1)} %collective-permute-done.4.other_ref, ...), custom_call_target="tpu_custom_call" | custom-call | flops 1073741824 | bytes 3145728 | tf_op jit(solution)/shard_map/pallas_call | solution.py:255
  34.8 1.9 %shard_map.84 = bf16[512,2048]{1,0:T(8,128)(2,1)} custom-call(bf16[512,2048]{1,0:T(8,128)(2,1)S(1)} %copy-done.3, bf16[512,2048]{1,0:T(8,128)(2,1)S(1)} %copy-done, bf16[512,2048]{1,0:T(8,128)(2,1)S(1)} %copy-done.2, bf16[128,2048]{1,0:T(8,128)(2,1)S(1)} %collective-permute-done.5.h_ref, ...), custom_call_target="tpu_custom_call", output_to_operand_aliasing={{}: (4, {})} | custom-call | flops 268435456 | bytes 1048576 | tf_op jit(solution)/shard_map/pallas_call | solution.py:255
  (20 shorter events, 0.2 us)
Async XLA Ops:
  0.6 4.6 %copy-start = (bf16[512,2048]{1,0:T(8,128)(2,1)S(1)}, bf16[512,2048]{1,0:T(8,128)(2,1)}, u32[]{:S(2)}) copy-start(bf16[512,2048]{1,0:T(8,128)(2,1)} %k_ref.8) | copy-start | bytes 6291460
  0.6 1.2 %copy-start.4 = (bf16[512,512]{1,0:T(8,128)(2,1)S(1)}, bf16[512,512]{1,0:T(8,128)(2,1)}, u32[]{:S(2)}) copy-start(bf16[512,512]{1,0:T(8,128)(2,1)} %v_ref.4) | copy-start | bytes 1572868
  1.8 0.9 %copy-start.6 = (bf16[512,128]{1,0:T(8,128)(2,1)S(1)}, bf16[512,128]{1,0:T(8,128)(2,1)}, u32[]{:S(2)}) copy-start(bf16[512,128]{1,0:T(8,128)(2,1)} %k_ref.4) | copy-start | bytes 393220
  4.7 2.3 %collective-permute-start = (bf16[2,336,128]{2,1,0:T(8,128)(2,1)S(1)}, bf16[2,336,128]{2,1,0:T(8,128)(2,1)S(1)}, u32[]{:S(2)}, u32[]{:S(2)}) collective-permute-start(bf16[2,336,128]{2,1,0:T(8,128)(2,1)S(1)} %shard_map.78), channel_id=1, source_target_pairs={{0,1},{1,0},{2,3},{3,2},{4,5},{5,4},{6,7},{7,6},{8,9},{9,8},{10,11... | collective-permute-start | bytes 516104 | tf_op jit(solution)/shard_map/ppermute | solution.py:266
  5.3 1.6 %copy-start.1 = (bf16[512,2048]{1,0:T(8,128)(2,1)S(1)}, bf16[512,2048]{1,0:T(8,128)(2,1)}, u32[]{:S(2)}) copy-start(bf16[512,2048]{1,0:T(8,128)(2,1)} %v_ref.8) | copy-start | bytes 6291460
  6.9 27.8 %collective-permute-start.5 = (bf16[128,2048]{1,0:T(8,128)(2,1)S(1)}, bf16[128,2048]{1,0:T(8,128)(2,1)S(1)}, u32[]{:S(2)}, u32[]{:S(2)}) collective-permute-start(bf16[128,2048]{1,0:T(8,128)(2,1)S(1)} %shard_map.83), channel_id=1, source_target_pairs={{0,1},{1,2},{2,3},{3,4},{4,5},{5,6},{6,7},{7,8},{8,9},{9,10},{10,1... | collective-permute-start | bytes 1572872 | tf_op jit(solution)/shard_map/ppermute | solution.py:314
  7.1 13.9 %copy-start.2 = (bf16[512,2048]{1,0:T(8,128)(2,1)S(1)}, bf16[512,2048]{1,0:T(8,128)(2,1)}, u32[]{:S(2)}) copy-start(bf16[512,2048]{1,0:T(8,128)(2,1)} %v_ref.8) | copy-start | bytes 6291460
  7.1 13.9 %copy-start.3 = (bf16[512,2048]{1,0:T(8,128)(2,1)S(1)}, bf16[512,2048]{1,0:T(8,128)(2,1)}, u32[]{:S(2)}) copy-start(bf16[512,2048]{1,0:T(8,128)(2,1)} %q_ref.8) | copy-start | bytes 6291460
  7.1 8.4 %collective-permute-start.1 = (bf16[336,128]{1,0:T(8,128)(2,1)S(1)}, bf16[336,128]{1,0:T(8,128)(2,1)S(1)}, u32[]{:S(2)}, u32[]{:S(2)}) collective-permute-start(bf16[336,128]{1,0:T(8,128)(2,1)S(1)} %convert_element_type.29), channel_id=1, source_target_pairs={{0,2},{1,3},{2,0},{3,1},{4,6},{5,7},{6,4},{7,5},{8,10},{9,11},{10,... | collective-permute-start | bytes 258056 | tf_op jit(solution)/shard_map/ppermute | solution.py:266
  10.1 1.0 %copy-start.5 = (bf16[512,512]{1,0:T(8,128)(2,1)S(1)}, bf16[512,512]{1,0:T(8,128)(2,1)}, u32[]{:S(2)}) copy-start(bf16[512,512]{1,0:T(8,128)(2,1)} %v_ref.4) | copy-start | bytes 1572868
  11.2 0.9 %copy-start.7 = (bf16[512,128]{1,0:T(8,128)(2,1)S(1)}, bf16[512,128]{1,0:T(8,128)(2,1)}, u32[]{:S(2)}) copy-start(bf16[512,128]{1,0:T(8,128)(2,1)} %k_ref.4) | copy-start | bytes 393220
  12.1 0.9 %copy-start.8 = (bf16[512,128]{1,0:T(8,128)(2,1)S(1)}, bf16[512,128]{1,0:T(8,128)(2,1)}, u32[]{:S(2)}) copy-start(bf16[512,128]{1,0:T(8,128)(2,1)} %q_ref.5) | copy-start | bytes 393220
  15.6 8.9 %collective-permute-start.2 = (bf16[336,128]{1,0:T(8,128)(2,1)S(1)}, bf16[336,128]{1,0:T(8,128)(2,1)S(1)}, u32[]{:S(2)}, u32[]{:S(2)}) collective-permute-start(bf16[336,128]{1,0:T(8,128)(2,1)S(1)} %fusion.5), channel_id=1, source_target_pairs={{0,4},{1,5},{2,6},{3,7},{4,0},{5,1},{6,2},{7,3},{8,12},{9,13},{10,... | collective-permute-start | bytes 258056 | tf_op jit(solution)/shard_map/ppermute | solution.py:266
  24.6 7.0 %collective-permute-start.3 = (bf16[336,128]{1,0:T(8,128)(2,1)S(1)}, bf16[336,128]{1,0:T(8,128)(2,1)S(1)}, u32[]{:S(2)}, u32[]{:S(2)}) collective-permute-start(bf16[336,128]{1,0:T(8,128)(2,1)S(1)} %fusion.3), channel_id=1, source_target_pairs={{0,8},{1,9},{2,10},{3,11},{4,12},{5,13},{6,14},{7,15},{8,0},{9,1},... | collective-permute-start | bytes 258056 | tf_op jit(solution)/shard_map/ppermute | solution.py:266
  31.6 1.3 %collective-permute-start.4 = (bf16[336,128]{1,0:T(8,128)(2,1)S(1)}, bf16[336,128]{1,0:T(8,128)(2,1)S(1)}, u32[]{:S(2)}, u32[]{:S(2)}) collective-permute-start(bf16[336,128]{1,0:T(8,128)(2,1)S(1)} %fusion.2.own_ref), channel_id=1, source_target_pairs={{0,1},{1,0},{2,3},{3,2},{4,5},{5,4},{6,7},{7,6},{8,9},{9,8},{10,11... | collective-permute-start | bytes 258056 | tf_op jit(solution)/shard_map/ppermute | solution.py:266

commit v2 on v1

v2 whole, which is shorter than its diff:
```python
import math

import jax
import jax.numpy as jnp
from jax import lax
from jax.experimental import pallas as pl
from jax.experimental.pallas import tpu as pltpu
from jax.sharding import PartitionSpec as P

HEADS = 8
KDIM = 16
VDIM = 64
WHEADS = 16
WDIM = 128
WINDOW = 64

BF = jnp.bfloat16
F32 = jnp.float32
BLOCKS = 10
PAIRS = BLOCKS // 2
MAIN = PAIRS * 64
ROWS = MAIN + 16
STEP = 256
GROUP = 4
COEF = (1 / 32,) + (1 / 16,) * 7 + (1 / 32, 1 / 4)
VMEM = pl.BlockSpec(memory_space=pltpu.VMEM)


def lanes(shape):
    return lax.broadcasted_iota(jnp.int32, shape, len(shape) - 1)


def rows_of(shape):
    return lax.broadcasted_iota(jnp.int32, shape, len(shape) - 2)


def feature(x, d):
    if d == 9:
        return x
    if d == 0:
        return x * x
    low = lanes(x.shape) % KDIM < KDIM - d
    other = jnp.where(low, pltpu.roll(x, 128 - d, 1), pltpu.roll(x, KDIM - d, 1))
    return x * other


def halves(first, second):
    left = lanes(first.shape) < 64
    return (
        jnp.where(left, first, pltpu.roll(second, 64, 1)),
        jnp.where(left, pltpu.roll(first, 64, 1), second),
    )


def put_features(x, coef, fa, fb):
    sums = []
    for p in range(PAIRS):
        blocks = [feature(x, d) * coef[d] for d in (2 * p, 2 * p + 1)]
        sums.append([jnp.sum(b, axis=0, keepdims=True) for b in blocks])
        a, b = halves(*blocks)
        fa[:, p * 128 : (p + 1) * 128] = a.astype(BF)
        fb[:, p * 128 : (p + 1) * 128] = b.astype(BF)
    return sums


def load_kernel(q_hbm, k_hbm, v_hbm, kw_hbm, vw_hbm, edge_ref, q_ref, k_ref, v_ref, sems):
    last = pl.ds(kw_hbm.shape[0] - WINDOW, WINDOW)
    moves = (
        (kw_hbm.at[last], edge_ref.at[pl.ds(0, WINDOW)]),
        (vw_hbm.at[last], edge_ref.at[pl.ds(WINDOW, WINDOW)]),
        (k_hbm, k_ref),
        (v_hbm, v_ref),
        (q_hbm, q_ref),
    )
    copies = [pltpu.make_async_copy(src, dst, sems.at[n]) for n, (src, dst) in enumerate(moves)]
    for copy in copies:
        copy.start()
    for copy in copies:
        copy.wait()


def state_kernel(k_ref, v_ref, s_ref, fa, fb):
    sums = put_features(k_ref[...].astype(F32), (1.0,) * BLOCKS, fa, fb)
    zs = [halves(*pair) for pair in sums]
    v = v_ref[...]
    vsum = jnp.sum(v.astype(F32), axis=0, keepdims=True)
    left = lanes((64, 128)) < 64
    even = (rows_of((64, 128)) // KDIM) % 2 == 0
    for half, f in ((0, fa), (1, fb)):
        r = lax.dot_general(
            f[...],
            v[:, half * 256 : (half + 1) * 256],
            (((0,), (0,)), ((), ())),
            preferred_element_type=F32,
        )
        for p in range(PAIRS):
            pieces = []
            for par in range(2):
                at = p * 128 + par * 64
                z = jnp.concatenate(
                    [r[at : at + 32, :128], r[at + 32 : at + 64, 128:]], axis=0
                )
                keep = even if par == 0 else jnp.logical_not(even)
                pieces.append(jnp.where(keep, z, pltpu.roll(z, 64, 1)))
            s_ref[half, p * 64 : (p + 1) * 64, :] = jnp.where(left, *pieces).astype(BF)
        aux = [z[half] for z in zs]
        aux += [vsum[:, half * 256 + t * 128 : half * 256 + (t + 1) * 128] for t in range(2)]
        aux.append(jnp.zeros((ROWS - MAIN - PAIRS - 2, 128), F32))
        s_ref[half, MAIN:, :] = jnp.concatenate(aux, axis=0).astype(BF)


def query_kernel(q_ref, fa, fb, done):
    done[...] = jnp.zeros_like(done)
    put_features(q_ref[...].astype(F32), COEF, fa, fb)


def local_kernel(q_ref, k_ref, v_ref, num_ref, den_ref, done):
    done[...] = jnp.zeros_like(done)
    tok = q_ref.shape[0]
    step = STEP
    k = k_ref[...]
    lane = lanes((step, 128))
    left = lane < 64
    left_all = lanes((tok, 128)) < 64
    causal = rows_of((step, step)) >= lanes((step, step))
    one = jnp.ones((tok, 128), BF)
    for r in range(tok // step):
        rows, end = slice(r * step, (r + 1) * step), (r + 1) * step
        q = q_ref[rows, :]
        for t0 in range(0, HEADS // 2, 2):
            places = [(t, e) for t in (t0, t0 + 1) for e in range(2)]
            kernels = []
            for t, e in places:
                qm = jnp.where(lane // KDIM == 2 * t + e, q, jnp.zeros_like(q))
                u = lax.dot_general(
                    qm, k[:end, :], (((1,), (1,)), ((), ())), preferred_element_type=F32
                )
                kernels.append(u + 4.0)
            outs = []
            for w, (t, e) in zip(kernels, places):
                w = w * w * (1 / 32) + 0.5
                diag = jnp.where(causal, w[:, r * step :], 0.0).astype(BF)
                if r:
                    diag = jnp.concatenate([w[:, : r * step].astype(BF), diag], axis=1)
                v = v_ref[:, t * 128 : (t + 1) * 128]
                aug = jnp.where(left_all, one, v) if e else jnp.where(left_all, v, one)
                outs.append(jnp.dot(diag, aug[:end, :], preferred_element_type=F32))
            for n in range(2):
                cols = slice((t0 + n) * 128, (t0 + n + 1) * 128)
                a, b = outs[2 * n : 2 * n + 2]
                num_ref[rows, cols] = jnp.where(left, a, b)
                den_ref[rows, cols] = pltpu.roll(jnp.where(left, b, a), 64, 1)


def finish_kernel(fa, fb, own_ref, other_ref, peer_ref, num_ref, den_ref, o_ref, pa, pb):
    tok = fa.shape[0]
    me = lax.axis_index("seq")
    second = me % 2 == 1
    own = own_ref[...].astype(F32)
    other = other_ref[...].astype(F32)
    left = lanes((64, 128)) < 64
    row = rows_of((64, 128)) // KDIM
    col = lanes((64, 128)) // VDIM
    span = ((rows_of((256, 256)) // KDIM) % 4 == lanes((256, 256)) // VDIM).astype(BF)
    count = (me * tok).astype(F32)
    for half, f, dst in ((0, fa, pa), (1, fb, pb)):
        state = jnp.where(second == (half == 1), own, other)
        state = state + jnp.where(second, peer_ref[half].astype(F32), 0.0)
        for p in range(PAIRS):
            c = state[p * 64 : (p + 1) * 64, :]
            turned = pltpu.roll(c, 64, 1)
            for par in range(2):
                base = jnp.where(left, c, turned) if par == 0 else jnp.where(left, turned, c)
                at = p * 128 + par * 64
                for t in range(2):
                    dst[at : at + 64, t * 128 : (t + 1) * 128] = jnp.where(
                        row == col + 2 * t, base, 0.0
                    ).astype(BF)
        cols = slice(half * 256, (half + 1) * 256)
        acc = jnp.zeros((tok, 128), F32)
        for p in range(PAIRS):
            acc = acc + f[:, p * 128 : (p + 1) * 128].astype(F32) * state[MAIN + p : MAIN + p + 1, :]
        high = acc.astype(BF)
        both = jnp.concatenate([high, (acc - high.astype(F32)).astype(BF)], axis=1)
        den = jnp.dot(both, span, preferred_element_type=F32) + den_ref[:, cols] + count
        at = MAIN + PAIRS
        vsum = jnp.concatenate([state[at : at + 1, :], state[at + 1 : at + 2, :]], axis=1)
        num = jnp.dot(f[...], dst[...], preferred_element_type=F32)
        o_ref[:, cols] = ((num + num_ref[:, cols] + vsum) / den).astype(BF)


SCALE = 1.0 / (math.sqrt(WDIM) * math.log(2.0))
QB = 2 * WINDOW


def masks():
    row, lane = rows_of((QB, QB)), lanes((QB, QB))
    earlier = (row < WINDOW) & (lane >= WINDOW)
    key = jnp.where(earlier, lane, lane + QB) - QB
    return earlier, key, (key <= row) & (key > row - WINDOW)


def attend(blocks, earlier, bias):
    s = jnp.stack(
        [
            lax.dot_general(q, k, (((1,), (1,)), ((), ())), preferred_element_type=F32)
            for q, k, v in blocks
        ]
    )
    s = jnp.where(earlier, s[:, :, :QB], s[:, :, QB:]) * SCALE + bias
    e = jnp.exp2(s - jnp.max(s, axis=2, keepdims=True))
    inverse = 1.0 / jnp.sum(e, axis=2, keepdims=True)
    e = jnp.concatenate([jnp.where(earlier, e, 0.0), jnp.where(earlier, 0.0, e)], axis=2).astype(BF)
    return [
        (jnp.dot(e[n], v, preferred_element_type=F32) * inverse[n]).astype(BF)
        for n, (q, k, v) in enumerate(blocks)
    ]


def window_kernel(q_ref, k_ref, v_ref, o_hbm, done, obuf, sems):
    done[...] = jnp.zeros_like(done)
    earlier, _, allowed = masks()
    bias = jnp.where(allowed, 0.0, -jnp.inf)
    tok, wide = q_ref.shape
    copies = []
    for h in range(0, wide, GROUP * WDIM):
        places = [
            (at, slice(c, c + WDIM))
            for c in range(h, h + GROUP * WDIM, WDIM)
            for at in range(QB, tok, QB)
        ]
        outs = attend(
            [
                (q_ref[at : at + QB, c], k_ref[at - QB : at + QB, c], v_ref[at - QB : at + QB, c])
                for at, c in places
            ],
            earlier,
            bias,
        )
        for (at, c), out in zip(places, outs):
            obuf[at : at + QB, c] = out
        part = (pl.ds(QB, tok - QB), pl.ds(h, GROUP * WDIM))
        copies.append(
            pltpu.make_async_copy(obuf.at[part], o_hbm.at[part], sems.at[h // (GROUP * WDIM)])
        )
        copies[-1].start()
    for copy in copies:
        copy.wait()


def edge_kernel(q_ref, k_ref, v_ref, h_ref, whole_ref, o_hbm, done, obuf, sems):
    done[...] = jnp.zeros_like(done)
    first = lax.axis_index("seq") == 0
    earlier, key, allowed = masks()
    bias = jnp.where(allowed & ((key >= 0) | jnp.logical_not(first)), 0.0, -jnp.inf)
    top = slice(0, QB)
    copies = []
    for h in range(0, q_ref.shape[1], 2 * GROUP * WDIM):
        blocks = []
        for c in range(h, h + 2 * GROUP * WDIM, WDIM):
            cols = slice(c, c + WDIM)
            kh, vh = h_ref[:WINDOW, cols], h_ref[WINDOW:, cols]
            k = jnp.concatenate([kh, kh, k_ref[top, cols]], axis=0)
            v = jnp.concatenate([vh, vh, v_ref[top, cols]], axis=0)
            blocks.append((q_ref[top, cols], k, v))
        for n, out in enumerate(attend(blocks, earlier, bias)):
            obuf[:, h + n * WDIM : h + (n + 1) * WDIM] = out
        part = (pl.ds(0, QB), pl.ds(h, 2 * GROUP * WDIM))
        copies.append(
            pltpu.make_async_copy(obuf.at[part], o_hbm.at[part], sems.at[h // (2 * GROUP * WDIM)])
        )
        copies[-1].start()
    for copy in copies:
        copy.wait()


def call(kernel, out, *args, in_specs, after=(), flops=0, nbytes=0, vmem=8, **kw):
    given = len(args)

    def run(*refs):
        kernel(*refs[:given], *refs[given + len(after) :])

    return pl.pallas_call(
        run,
        out_shape=out,
        in_specs=list(in_specs) + [pl.BlockSpec(memory_space=pl.ANY)] * len(after),
        cost_estimate=pl.CostEstimate(flops=flops, bytes_accessed=nbytes, transcendentals=0),
        compiler_params=pltpu.CompilerParams(vmem_limit_bytes=vmem << 20),
        name=kernel.__name__,
        **kw,
    )(*args, *after)


def exchange(x, step):
    count = lax.axis_size("seq")
    return lax.ppermute(x, "seq", [(i, i ^ step) for i in range(count)])


def shape(*dims, dtype=BF):
    return jax.ShapeDtypeStruct(dims, dtype)


def body(q_lin, k_lin, v_lin, q_win, k_win, v_win):
    tok = q_lin.shape[0]
    count = lax.axis_size("seq")
    assert count & (count - 1) == 0 and count > 1
    me = lax.axis_index("seq")
    bits = [(me & (1 << n)) != 0 for n in range(count.bit_length() - 1)]
    bits, k_lin = lax.optimization_barrier((bits, k_lin))
    wide = WHEADS * WDIM
    hbm = pl.BlockSpec(memory_space=pltpu.HBM)
    feats = pltpu.VMEM((tok, PAIRS * 128), BF)

    edge, q_lin, k_lin, v_lin = call(
        load_kernel,
        (
            shape(2 * WINDOW, wide),
            shape(*q_lin.shape),
            shape(*k_lin.shape),
            shape(*v_lin.shape),
        ),
        *(pltpu.with_memory_space_constraint(x, pltpu.HBM) for x in (q_lin, k_lin, v_lin, k_win, v_win)),
        in_specs=[hbm] * 5,
        out_specs=(VMEM,) * 4,
        scratch_shapes=[pltpu.SemaphoreType.DMA((5,))],
        nbytes=2 << 20,
        vmem=4,
    )
    edge = lax.ppermute(edge, "seq", [(i, (i + 1) % count) for i in range(count)])
    state = call(
        state_kernel,
        shape(2, ROWS, 128),
        k_lin,
        v_lin,
        in_specs=[VMEM] * 2,
        out_specs=VMEM,
        scratch_shapes=[feats] * 2,
        flops=1 << 30,
        nbytes=1 << 20,
    )
    peer = exchange(state, 1)
    both = state.astype(F32) + peer.astype(F32)
    carried = jnp.where(bits[0], both[1], both[0])
    before = jnp.zeros_like(carried)

    token = shape(8, 128, dtype=F32)

    def local(after):
        num, den, done = call(
            local_kernel,
            (shape(tok, HEADS * VDIM, dtype=F32),) * 2 + (token,),
            q_lin,
            k_lin,
            v_lin,
            after=after,
            in_specs=[VMEM] * 3,
            out_specs=(VMEM,) * 3,
            flops=1 << 31,
            nbytes=3 << 20,
        )
        return (num, den), (done,)

    def window(after):
        win, done = call(
            window_kernel,
            (shape(tok, wide), token),
            q_win,
            k_win,
            v_win,
            after=after,
            in_specs=[VMEM] * 3,
            out_specs=(hbm, VMEM),
            scratch_shapes=[
                pltpu.VMEM((tok, wide), BF),
                pltpu.SemaphoreType.DMA((WHEADS // GROUP,)),
            ],
            flops=1 << 31,
            nbytes=8 << 20,
        )
        return win, (done,)

    def rest(after, win):
        fa, fb, first = call(
            query_kernel,
            (shape(tok, PAIRS * 128),) * 2 + (token,),
            q_lin,
            after=after,
            in_specs=[VMEM],
            out_specs=(VMEM,) * 3,
            flops=1 << 28,
            nbytes=1 << 20,
        )
        out, second = call(
            edge_kernel,
            (shape(tok, wide), token),
            q_win,
            k_win,
            v_win,
            edge,
            win,
            after=after,
            in_specs=[VMEM] * 4 + [hbm],
            out_specs=(hbm, VMEM),
            scratch_shapes=[
                pltpu.VMEM((QB, wide), BF),
                pltpu.SemaphoreType.DMA((WHEADS // (2 * GROUP),)),
            ],
            input_output_aliases={4: 0},
            flops=1 << 28,
            nbytes=1 << 20,
        )
        return (fa, fb, out), (first, second)

    step, turn = 2, 0
    sums = win = feats = None
    done = ()
    while step < count:
        send = carried.astype(BF)
        got = exchange(send, step)
        after = (send,) + done
        if turn == 0:
            sums, done = local(after)
        elif turn == 1:
            win, done = window(after)
        elif turn == 2:
            feats, done = rest(after, win)
        if turn < 3:
            got, done = lax.optimization_barrier((got, done))
        got = got.astype(F32)
        before = before + jnp.where(bits[turn + 1], got, 0.0)
        carried = carried + got
        step *= 2
        turn += 1
    assert turn >= 3
    own = before.astype(BF)
    other = exchange(own, 1)
    lin_out = call(
        finish_kernel,
        shape(tok, HEADS * VDIM),
        *feats[:2],
        own,
        other,
        peer,
        *sums,
        after=done,
        in_specs=[VMEM] * 7,
        out_specs=VMEM,
        scratch_shapes=[pltpu.VMEM((PAIRS * 128, 256), BF)] * 2,
        flops=1 << 30,
        nbytes=3 << 20,
    )
    return (lin_out, feats[2])


def solution(mesh):
    spec = P(("groups", "seq"), None)
    return jax.shard_map(
        body, mesh=mesh, in_specs=(spec,) * 6, out_specs=(spec, spec), check_vma=False
    )
```

time: 36.9 us -> 32 us (0.87)
  waiting for transfers between devices: 0.8 us -> 10.8 us
  local copies, waits for them, and re-layouts: 6.54 us -> 0.01 us
  starting transfers between devices: 11.7 us -> 7.1 us
  Pallas kernels: 16.6 us -> 13 us
    ppermute x5, waiting for transfers between devices: 0.79 us -> 10.8 us  [exchange(): return lax.ppermute(x, 'seq', [(i, i ^ step) for i in range(count)])]
    unnamed x18 -> x6, local copies, waits for them, and re-layouts: 6.54 us -> 0.01 us
    ppermute x5, starting transfers between devices: 11.6 us -> 7.03 us  [exchange(): return lax.ppermute(x, 'seq', [(i, i ^ step) for i in range(count)])]
    pallas_call x8 -> x7, Pallas kernels: 16.6 us -> 13 us  [call(): pl.pallas_call(run, out_shape=out, in_specs=list(in_specs) + [pl.BlockSpe...]
  transfers between devices with their start and end apart: 6 -> 6, of which waited for: 1 -> 5; matrix products, arithmetic and copies ran while one was open for 1% -> 0% of each run, Pallas kernels for 35% -> 25%
where the time goes in v2:
time: 32 us; the launch traced here: 31.8 us
  Pallas kernels  13 us (41%)
  waiting for transfers between devices  10.8 us (34%)
  starting transfers between devices  7.1 us (22%)
  between operations  0.73 us (2%)
    pallas_call x7, Pallas kernels, call(): pl.pallas_call(run, out_shape=out, in_specs=list(in_specs) + [pl.BlockSpe...  13 us
    ppermute x5, waiting for transfers between devices, exchange(): return lax.ppermute(x, 'seq', [(i, i ^ step) for i in range(count)])  10.8 us
    ppermute x5, starting transfers between devices, exchange(): return lax.ppermute(x, 'seq', [(i, i ^ step) for i in range(count)])  7.03 us
  transfers between devices with their start and end apart: 6, of which 5 were waited for; matrix products, arithmetic and copies ran while one was open for 0% of the time, Pallas kernels for 25%

profile of v2, /device:TPU:0, one launch (start us, length us, event | category | flops | bytes accessed | tf_op | source)
XLA Modules:
  0.0 31.8 jit_solution(5363215510107613257)
XLA Ops:
  0.6 1.3 %load_kernel.1 = (bf16[128,2048]{1,0:T(8,128)(2,1)S(1)}, bf16[512,128]{1,0:T(8,128)(2,1)S(1)}, bf16[512,128]{1,0:T(8,128)(2,1)S(1)}, bf16[512,512]{1,0:T(8,128)(2,1)S(1)}) custom-call(bf16[512,128]{1,0:T(8,128)(2,1)} %refs_0_.3, bf16[512,128]{1,0:T(8,128)(2,1)} %refs_1_.2, bf16[512,512]{1,0:T(8,128)(2,1)} %refs_2_.3, bf16[512,2048]{1,0:T(8,128)(2,1)} %refs_1_.4, ...), custom_call_target="tpu_custom_call" | custom-call | bytes 2097152 | tf_op jit(solution)/shard_map/load_kernel/pallas_call | solution.py:283
  2.0 1.9 %state_kernel.1 = bf16[2,336,128]{2,1,0:T(8,128)(2,1)S(1)} custom-call(bf16[512,128]{1,0:T(8,128)(2,1)S(1)} %get-tuple-element.31.refs_0_.refs_1_, bf16[512,512]{1,0:T(8,128)(2,1)S(1)} %get-tuple-element.32.refs_1_.refs_2_), custom_call_target="tpu_custom_call" | custom-call | flops 1073741824 | bytes 1048576 | tf_op jit(solution)/shard_map/state_kernel/pallas_call | solution.py:283
  3.8 0.5 %collective-permute-start = (bf16[2,336,128]{2,1,0:T(8,128)(2,1)S(1)}, bf16[2,336,128]{2,1,0:T(8,128)(2,1)S(1)}, u32[]{:S(2)}, u32[]{:S(2)}) collective-permute-start(bf16[2,336,128]{2,1,0:T(8,128)(2,1)S(1)} %state_kernel.1), channel_id=1, source_target_pairs={{0,1},{1,0},{2,3},{3,2},{4,5},{5,4},{6,7},{7,6},{8,9},{9,8},{10,11... | collective-permute-start | bytes 516104 | tf_op jit(solution)/shard_map/ppermute | solution.py:296
  4.3 0.1 collective-permute-start.4
  4.4 1.0 %collective-permute-done.refs_4_ = bf16[2,336,128]{2,1,0:T(8,128)(2,1)S(1)} collective-permute-done((bf16[2,336,128]{2,1,0:T(8,128)(2,1)S(1)}, bf16[2,336,128]{2,1,0:T(8,128)(2,1)S(1)}, u32[]{:S(2)}, u32[]{:S(2)}) %collective-permute-start) | collective-permute-done | bytes 172064 | tf_op jit(solution)/shard_map/ppermute | solution.py:296
  5.5 2.9 %collective-permute-start.1 = (bf16[336,128]{1,0:T(8,128)(2,1)S(1)}, bf16[336,128]{1,0:T(8,128)(2,1)S(1)}, u32[]{:S(2)}, u32[]{:S(2)}) collective-permute-start(bf16[336,128]{1,0:T(8,128)(2,1)S(1)} %get-tuple-element.54.refs_3_), channel_id=1, source_target_pairs={{0,2},{1,3},{2,0},{3,1},{4,6},{5,7},{6,4},{7,5},{8,10},{9,11},{10,... | collective-permute-start | bytes 258056 | tf_op jit(solution)/shard_map/ppermute | solution.py:296
  8.4 0.0 copy-start
  8.4 2.0 %local_kernel.1 = (f32[512,512]{1,0:T(8,128)S(1)}, f32[512,512]{1,0:T(8,128)S(1)}, f32[8,128]{1,0:T(8,128)S(1)}) custom-call(bf16[512,128]{1,0:T(8,128)(2,1)S(1)} %get-tuple-element.29.refs_0_, bf16[512,128]{1,0:T(8,128)(2,1)S(1)} %get-tuple-element.31.refs_0_.refs_1_, bf16[512,512]{1,0:T(8,128)(2,1)S(1)} %get-tuple-element.32.refs_1_.refs_2_, ...), custom_call_target="tpu_custom_call" | custom-call | flops 2147483648 | bytes 3145728 | tf_op jit(solution)/shard_map/local_kernel/pallas_call | solution.py:283
  10.4 6.8 %collective-permute-done.1 = bf16[336,128]{1,0:T(8,128)(2,1)S(1)} collective-permute-done((bf16[336,128]{1,0:T(8,128)(2,1)S(1)}, bf16[336,128]{1,0:T(8,128)(2,1)S(1)}, u32[]{:S(2)}, u32[]{:S(2)}) %collective-permute-start.1) | collective-permute-done | bytes 86048 | tf_op jit(solution)/shard_map/ppermute | solution.py:296
  17.2 1.2 %collective-permute-start.2 = (bf16[336,128]{1,0:T(8,128)(2,1)S(1)}, bf16[336,128]{1,0:T(8,128)(2,1)S(1)}, u32[]{:S(2)}, u32[]{:S(2)}) collective-permute-start(bf16[336,128]{1,0:T(8,128)(2,1)S(1)} %fusion.5.refs_3_), channel_id=1, source_target_pairs={{0,4},{1,5},{2,6},{3,7},{4,0},{5,1},{6,2},{7,3},{8,12},{9,13},{10,... | collective-permute-start | bytes 258056 | tf_op jit(solution)/shard_map/ppermute | solution.py:296
  18.4 0.0 copy-done
  18.4 0.0 copy-done.1
  18.4 0.0 copy-done.2
  18.4 3.0 %window_kernel.1 = (bf16[512,2048]{1,0:T(8,128)(2,1)}, f32[8,128]{1,0:T(8,128)S(1)}) custom-call(bf16[512,2048]{1,0:T(8,128)(2,1)S(1)} %copy-done.2, bf16[512,2048]{1,0:T(8,128)(2,1)S(1)} %copy-done, bf16[512,2048]{1,0:T(8,128)(2,1)S(1)} %copy-done.1, bf16[336,128]{1,0:T(8,128)(2,1)S(1)} %fusion.5.refs_3_, f32[8,128]{1,0:T(8,128)S(1)} %get-tuple-element.35.refs_4_), custom_call_target="tpu_custom_call" | custom-call | flops 2147483648 | bytes 8388608 | tf_op jit(solution)/shard_map/window_kernel/pallas_call | solution.py:283
  21.5 0.3 %collective-permute-done.2 = bf16[336,128]{1,0:T(8,128)(2,1)S(1)} collective-permute-done((bf16[336,128]{1,0:T(8,128)(2,1)S(1)}, bf16[336,128]{1,0:T(8,128)(2,1)S(1)}, u32[]{:S(2)}, u32[]{:S(2)}) %collective-permute-start.2) | collective-permute-done | bytes 86048 | tf_op jit(solution)/shard_map/ppermute | solution.py:296
  21.8 2.4 %collective-permute-start.3 = (bf16[336,128]{1,0:T(8,128)(2,1)S(1)}, bf16[336,128]{1,0:T(8,128)(2,1)S(1)}, u32[]{:S(2)}, u32[]{:S(2)}) collective-permute-start(bf16[336,128]{1,0:T(8,128)(2,1)S(1)} %fusion.3.refs_1_.refs_5_), channel_id=1, source_target_pairs={{0,8},{1,9},{2,10},{3,11},{4,12},{5,13},{6,14},{7,15},{8,0},{9,1},... | collective-permute-start | bytes 258056 | tf_op jit(solution)/shard_map/ppermute | solution.py:296
  24.2 1.2 %query_kernel.1 = (bf16[512,640]{1,0:T(8,128)(2,1)S(1)}, bf16[512,640]{1,0:T(8,128)(2,1)S(1)}, f32[8,128]{1,0:T(8,128)S(1)}) custom-call(bf16[512,128]{1,0:T(8,128)(2,1)S(1)} %get-tuple-element.29.refs_0_, bf16[336,128]{1,0:T(8,128)(2,1)S(1)} %fusion.3.refs_1_.refs_5_, f32[8,128]{1,0:T(8,128)S(1)} %get-tuple-element.38.refs_2_.refs_6_), custom_call_target="tpu_custom_call" | custom-call | flops 268435456 | bytes 1048576 | tf_op jit(solution)/shard_map/query_kernel/pallas_call | solution.py:283
  25.4 0.0 collective-permute-done.4.refs_3_
  25.4 1.7 %edge_kernel.1 = (bf16[512,2048]{1,0:T(8,128)(2,1)}, f32[8,128]{1,0:T(8,128)S(1)}) custom-call(bf16[512,2048]{1,0:T(8,128)(2,1)S(1)} %copy-done.2, bf16[512,2048]{1,0:T(8,128)(2,1)S(1)} %copy-done, bf16[512,2048]{1,0:T(8,128)(2,1)S(1)} %copy-done.1, bf16[128,2048]{1,0:T(8,128)(2,1)S(1)} %collective-permute-done.4.refs_3_, ...), custom_call_target="tpu_custom_call", output_to_operand_aliasing={{0}: (4, {})} | custom-call | flops 268435456 | bytes 1048576 | tf_op jit(solution)/shard_map/edge_kernel/pallas_call | solution.py:283
  27.1 1.5 %collective-permute-done.3 = bf16[336,128]{1,0:T(8,128)(2,1)S(1)} collective-permute-done((bf16[336,128]{1,0:T(8,128)(2,1)S(1)}, bf16[336,128]{1,0:T(8,128)(2,1)S(1)}, u32[]{:S(2)}, u32[]{:S(2)}) %collective-permute-start.3) | collective-permute-done | bytes 86048 | tf_op jit(solution)/shard_map/ppermute | solution.py:296
  28.5 0.1 fusion.2.refs_2_
  28.6 0.1 collective-permute-start.5
  28.7 1.3 %collective-permute-done.5.refs_3_ = bf16[336,128]{1,0:T(8,128)(2,1)S(1)} collective-permute-done((bf16[336,128]{1,0:T(8,128)(2,1)S(1)}, bf16[336,128]{1,0:T(8,128)(2,1)S(1)}, u32[]{:S(2)}, u32[]{:S(2)}) %collective-permute-start.5) | collective-permute-done | bytes 86048 | tf_op jit(solution)/shard_map/ppermute | solution.py:296
  29.9 1.9 %finish_kernel.1 = bf16[512,512]{1,0:T(8,128)(2,1)} custom-call(bf16[512,640]{1,0:T(8,128)(2,1)S(1)} %get-tuple-element.39.refs_0_, bf16[512,640]{1,0:T(8,128)(2,1)S(1)} %get-tuple-element.40.refs_1_, bf16[336,128]{1,0:T(8,128)(2,1)S(1)} %fusion.2.refs_2_, bf16[336,128]{1,0:T(8,128)(2,1)S(1)} %collective-permute-done.5.refs_3_, ...), custom_call_target="tpu_custom_call" | custom-call | flops 1073741824 | bytes 3145728 | tf_op jit(solution)/shard_map/finish_kernel/pallas_call | solution.py:283
  (6 shorter events, 0.1 us)
Async XLA Ops:
  3.8 1.6 %collective-permute-start = (bf16[2,336,128]{2,1,0:T(8,128)(2,1)S(1)}, bf16[2,336,128]{2,1,0:T(8,128)(2,1)S(1)}, u32[]{:S(2)}, u32[]{:S(2)}) collective-permute-start(bf16[2,336,128]{2,1,0:T(8,128)(2,1)S(1)} %state_kernel.1), channel_id=1, source_target_pairs={{0,1},{1,0},{2,3},{3,2},{4,5},{5,4},{6,7},{7,6},{8,9},{9,8},{10,11... | collective-permute-start | bytes 516104 | tf_op jit(solution)/shard_map/ppermute | solution.py:296
  4.3 21.1 %collective-permute-start.4 = (bf16[128,2048]{1,0:T(8,128)(2,1)S(1)}, bf16[128,2048]{1,0:T(8,128)(2,1)S(1)}, u32[]{:S(2)}, u32[]{:S(2)}) collective-permute-start(bf16[128,2048]{1,0:T(8,128)(2,1)S(1)} %get-tuple-element.45), channel_id=1, source_target_pairs={{0,1},{1,2},{2,3},{3,4},{4,5},{5,6},{6,7},{7,8},{8,9},{9,10},{10,1... | collective-permute-start | bytes 1572872 | tf_op jit(solution)/shard_map/ppermute | solution.py:329
  5.5 11.7 %collective-permute-start.1 = (bf16[336,128]{1,0:T(8,128)(2,1)S(1)}, bf16[336,128]{1,0:T(8,128)(2,1)S(1)}, u32[]{:S(2)}, u32[]{:S(2)}) collective-permute-start(bf16[336,128]{1,0:T(8,128)(2,1)S(1)} %get-tuple-element.54.refs_3_), channel_id=1, source_target_pairs={{0,2},{1,3},{2,0},{3,1},{4,6},{5,7},{6,4},{7,5},{8,10},{9,11},{10,... | collective-permute-start | bytes 258056 | tf_op jit(solution)/shard_map/ppermute | solution.py:296
  8.4 10.0 %copy-start = (bf16[512,2048]{1,0:T(8,128)(2,1)S(1)}, bf16[512,2048]{1,0:T(8,128)(2,1)}, u32[]{:S(2)}) copy-start(bf16[512,2048]{1,0:T(8,128)(2,1)} %refs_1_.4) | copy-start | bytes 6291460
  8.4 10.0 %copy-start.1 = (bf16[512,2048]{1,0:T(8,128)(2,1)S(1)}, bf16[512,2048]{1,0:T(8,128)(2,1)}, u32[]{:S(2)}) copy-start(bf16[512,2048]{1,0:T(8,128)(2,1)} %refs_2_.5) | copy-start | bytes 6291460
  8.4 10.0 %copy-start.2 = (bf16[512,2048]{1,0:T(8,128)(2,1)S(1)}, bf16[512,2048]{1,0:T(8,128)(2,1)}, u32[]{:S(2)}) copy-start(bf16[512,2048]{1,0:T(8,128)(2,1)} %refs_0_.5) | copy-start | bytes 6291460
  17.2 4.6 %collective-permute-start.2 = (bf16[336,128]{1,0:T(8,128)(2,1)S(1)}, bf16[336,128]{1,0:T(8,128)(2,1)S(1)}, u32[]{:S(2)}, u32[]{:S(2)}) collective-permute-start(bf16[336,128]{1,0:T(8,128)(2,1)S(1)} %fusion.5.refs_3_), channel_id=1, source_target_pairs={{0,4},{1,5},{2,6},{3,7},{4,0},{5,1},{6,2},{7,3},{8,12},{9,13},{10,... | collective-permute-start | bytes 258056 | tf_op jit(solution)/shard_map/ppermute | solution.py:296
  21.8 6.7 %collective-permute-start.3 = (bf16[336,128]{1,0:T(8,128)(2,1)S(1)}, bf16[336,128]{1,0:T(8,128)(2,1)S(1)}, u32[]{:S(2)}, u32[]{:S(2)}) collective-permute-start(bf16[336,128]{1,0:T(8,128)(2,1)S(1)} %fusion.3.refs_1_.refs_5_), channel_id=1, source_target_pairs={{0,8},{1,9},{2,10},{3,11},{4,12},{5,13},{6,14},{7,15},{8,0},{9,1},... | collective-permute-start | bytes 258056 | tf_op jit(solution)/shard_map/ppermute | solution.py:296
  28.6 1.3 %collective-permute-start.5 = (bf16[336,128]{1,0:T(8,128)(2,1)S(1)}, bf16[336,128]{1,0:T(8,128)(2,1)S(1)}, u32[]{:S(2)}, u32[]{:S(2)}) collective-permute-start(bf16[336,128]{1,0:T(8,128)(2,1)S(1)} %fusion.2.refs_2_), channel_id=1, source_target_pairs={{0,1},{1,0},{2,3},{3,2},{4,5},{5,4},{6,7},{7,6},{8,9},{9,8},{10,11... | collective-permute-start | bytes 258056 | tf_op jit(solution)/shard_map/ppermute | solution.py:296

commit v3 on v2

--- a/solution.py
+++ b/solution.py
@@ -63,24 +63,23 @@
     return sums
 
 
-def load_kernel(q_hbm, k_hbm, v_hbm, kw_hbm, vw_hbm, edge_ref, q_ref, k_ref, v_ref, sems):
+def state_kernel(
+    q_hbm, k_hbm, v_hbm, kw_hbm, vw_hbm, s_ref, ke_ref, ve_ref, q_ref, k_ref, v_ref, fa, fb, sems
+):
     last = pl.ds(kw_hbm.shape[0] - WINDOW, WINDOW)
     moves = (
-        (kw_hbm.at[last], edge_ref.at[pl.ds(0, WINDOW)]),
-        (vw_hbm.at[last], edge_ref.at[pl.ds(WINDOW, WINDOW)]),
         (k_hbm, k_ref),
         (v_hbm, v_ref),
+        (kw_hbm.at[last], ke_ref),
         (q_hbm, q_ref),
+        (vw_hbm.at[last], ve_ref),
     )
     copies = [pltpu.make_async_copy(src, dst, sems.at[n]) for n, (src, dst) in enumerate(moves)]
     for copy in copies:
         copy.start()
-    for copy in copies:
-        copy.wait()
-
-
-def state_kernel(k_ref, v_ref, s_ref, fa, fb):
+    copies[0].wait()
     sums = put_features(k_ref[...].astype(F32), (1.0,) * BLOCKS, fa, fb)
+    copies[1].wait()
     zs = [halves(*pair) for pair in sums]
     v = v_ref[...]
     vsum = jnp.sum(v.astype(F32), axis=0, keepdims=True)
@@ -107,11 +106,8 @@
         aux += [vsum[:, half * 256 + t * 128 : half * 256 + (t + 1) * 128] for t in range(2)]
         aux.append(jnp.zeros((ROWS - MAIN - PAIRS - 2, 128), F32))
         s_ref[half, MAIN:, :] = jnp.concatenate(aux, axis=0).astype(BF)
-
-
-def query_kernel(q_ref, fa, fb, done):
-    done[...] = jnp.zeros_like(done)
-    put_features(q_ref[...].astype(F32), COEF, fa, fb)
+    for copy in copies[2:]:
+        copy.wait()
 
 
 def local_kernel(q_ref, k_ref, v_ref, num_ref, den_ref, done):
@@ -146,47 +142,48 @@
                 aug = jnp.where(left_all, one, v) if e else jnp.where(left_all, v, one)
                 outs.append(jnp.dot(diag, aug[:end, :], preferred_element_type=F32))
             for n in range(2):
-                cols = slice((t0 + n) * 128, (t0 + n + 1) * 128)
+                half, cols = t0 // 2, slice(n * 128, (n + 1) * 128)
                 a, b = outs[2 * n : 2 * n + 2]
-                num_ref[rows, cols] = jnp.where(left, a, b)
-                den_ref[rows, cols] = pltpu.roll(jnp.where(left, b, a), 64, 1)
-
-
-def finish_kernel(fa, fb, own_ref, other_ref, peer_ref, num_ref, den_ref, o_ref, pa, pb):
-    tok = fa.shape[0]
+                num_ref[half, rows, cols] = jnp.where(left, a, b)
+                den_ref[half, rows, cols] = pltpu.roll(jnp.where(left, b, a), 64, 1)
+
+
+def finish_half(half, f_ref, e_ref, peer_ref, num_ref, den_ref, obuf, weights):
+    tok = f_ref.shape[1]
     me = lax.axis_index("seq")
-    second = me % 2 == 1
-    own = own_ref[...].astype(F32)
-    other = other_ref[...].astype(F32)
+    core = me % 2
     left = lanes((64, 128)) < 64
     row = rows_of((64, 128)) // KDIM
     col = lanes((64, 128)) // VDIM
     span = ((rows_of((256, 256)) // KDIM) % 4 == lanes((256, 256)) // VDIM).astype(BF)
     count = (me * tok).astype(F32)
-    for half, f, dst in ((0, fa, pa), (1, fb, pb)):
-        state = jnp.where(second == (half == 1), own, other)
-        state = state + jnp.where(second, peer_ref[half].astype(F32), 0.0)
+    state = e_ref[...].astype(F32) + jnp.where(core == 1, peer_ref[half].astype(F32), 0.0)
+    for p in range(PAIRS):
+        c = state[p * 64 : (p + 1) * 64, :]
+        turned = pltpu.roll(c, 64, 1)
+        for par in range(2):
+            base = jnp.where(left, c, turned) if par == 0 else jnp.where(left, turned, c)
+            at = p * 128 + par * 64
+            for t in range(2):
+                weights[at : at + 64, t * 128 : (t + 1) * 128] = jnp.where(
+                    row == col + 2 * t, base, 0.0
+                ).astype(BF)
+    at = MAIN + PAIRS
+    vsum = jnp.concatenate([state[at : at + 1, :], state[at + 1 : at + 2, :]], axis=1)
+    step = tok // 2
+    for n in range(2):
+        rows = slice(n * step, (n + 1) * step)
+        f = f_ref[half, rows, :]
+        acc = jnp.zeros((step, 128), F32)
         for p in range(PAIRS):
-            c = state[p * 64 : (p + 1) * 64, :]
-            turned = pltpu.roll(c, 64, 1)
-            for par in range(2):
-                base = jnp.where(left, c, turned) if par == 0 else jnp.where(left, turned, c)
-                at = p * 128 + par * 64
-                for t in range(2):
-                    dst[at : at + 64, t * 128 : (t + 1) * 128] = jnp.where(
-                        row == col + 2 * t, base, 0.0
-                    ).astype(BF)
-        cols = slice(half * 256, (half + 1) * 256)
-        acc = jnp.zeros((tok, 128), F32)
-        for p in range(PAIRS):
-            acc = acc + f[:, p * 128 : (p + 1) * 128].astype(F32) * state[MAIN + p : MAIN + p + 1, :]
+            z = state[MAIN + p : MAIN + p + 1, :]
+            acc = acc + f[:, p * 128 : (p + 1) * 128].astype(F32) * z
         high = acc.astype(BF)
         both = jnp.concatenate([high, (acc - high.astype(F32)).astype(BF)], axis=1)
-        den = jnp.dot(both, span, preferred_element_type=F32) + den_ref[:, cols] + count
-        at = MAIN + PAIRS
-        vsum = jnp.concatenate([state[at : at + 1, :], state[at + 1 : at + 2, :]], axis=1)
-        num = jnp.dot(f[...], dst[...], preferred_element_type=F32)
-        o_ref[:, cols] = ((num + num_ref[:, cols] + vsum) / den).astype(BF)
+        den = jnp.dot(both, span, preferred_element_type=F32) + den_ref[half, rows, :] + count
+        num = jnp.dot(f, weights[...], preferred_element_type=F32)
+        obuf[rows, :] = ((num + num_ref[half, rows, :] + vsum) / den).astype(BF)
+        yield pl.ds(n * step, step)
 
 
 SCALE = 1.0 / (math.sqrt(WDIM) * math.log(2.0))
@@ -197,7 +194,7 @@
     row, lane = rows_of((QB, QB)), lanes((QB, QB))
     earlier = (row < WINDOW) & (lane >= WINDOW)
     key = jnp.where(earlier, lane, lane + QB) - QB
-    return earlier, key, (key <= row) & (key > row - WINDOW)
+    return earlier, (key <= row) & (key > row - WINDOW)
 
 
 def attend(blocks, earlier, bias):
@@ -219,7 +216,7 @@
 
 def window_kernel(q_ref, k_ref, v_ref, o_hbm, done, obuf, sems):
     done[...] = jnp.zeros_like(done)
-    earlier, _, allowed = masks()
+    earlier, allowed = masks()
     bias = jnp.where(allowed, 0.0, -jnp.inf)
     tok, wide = q_ref.shape
     copies = []
@@ -248,28 +245,87 @@
         copy.wait()
 
 
-def edge_kernel(q_ref, k_ref, v_ref, h_ref, whole_ref, o_hbm, done, obuf, sems):
+def narrow(q_ref, first_row, k_of, v_of, bias, o_hbm, obuf, sems):
+    copies, group = [], 2 * GROUP * WDIM
+    rows = slice(first_row, first_row + WINDOW)
+    for h in range(0, q_ref.shape[1], group):
+        places = [slice(c, c + WDIM) for c in range(h, h + group, WDIM)]
+        s = jnp.stack(
+            [
+                lax.dot_general(
+                    q_ref[rows, c], k_of(c), (((1,), (1,)), ((), ())), preferred_element_type=F32
+                )
+                for c in places
+            ]
+        )
+        s = s * SCALE + bias
+        e = jnp.exp2(s - jnp.max(s, axis=2, keepdims=True))
+        inverse = 1.0 / jnp.sum(e, axis=2, keepdims=True)
+        e = e.astype(BF)
+        for n, c in enumerate(places):
+            o = jnp.dot(e[n], v_of(c), preferred_element_type=F32) * inverse[n]
+            obuf[:, c] = o.astype(BF)
+        cols = pl.ds(h, group)
+        copies.append(
+            pltpu.make_async_copy(
+                obuf.at[:, cols], o_hbm.at[pl.ds(first_row, WINDOW), cols], sems.at[h // group]
+            )
+        )
+        copies[-1].start()
+    return copies
+
+
+def band():
+    key, query = lanes((WINDOW, QB)), rows_of((WINDOW, QB))
+    return (key > query) & (key <= query + WINDOW)
+
+
+def query_kernel(x_ref, q_ref, k_ref, v_ref, whole_ref, f_ref, o_hbm, done, obuf, sems):
     done[...] = jnp.zeros_like(done)
-    first = lax.axis_index("seq") == 0
-    earlier, key, allowed = masks()
-    bias = jnp.where(allowed & ((key >= 0) | jnp.logical_not(first)), 0.0, -jnp.inf)
-    top = slice(0, QB)
-    copies = []
-    for h in range(0, q_ref.shape[1], 2 * GROUP * WDIM):
-        blocks = []
-        for c in range(h, h + 2 * GROUP * WDIM, WDIM):
-            cols = slice(c, c + WDIM)
-            kh, vh = h_ref[:WINDOW, cols], h_ref[WINDOW:, cols]
-            k = jnp.concatenate([kh, kh, k_ref[top, cols]], axis=0)
-            v = jnp.concatenate([vh, vh, v_ref[top, cols]], axis=0)
-            blocks.append((q_ref[top, cols], k, v))
-        for n, out in enumerate(attend(blocks, earlier, bias)):
-            obuf[:, h + n * WDIM : h + (n + 1) * WDIM] = out
-        part = (pl.ds(0, QB), pl.ds(h, 2 * GROUP * WDIM))
-        copies.append(
-            pltpu.make_async_copy(obuf.at[part], o_hbm.at[part], sems.at[h // (2 * GROUP * WDIM)])
-        )
-        copies[-1].start()
+    bias = jnp.where(band(), 0.0, -jnp.inf)
+    copies = narrow(
+        q_ref, WINDOW, lambda c: k_ref[:QB, c], lambda c: v_ref[:QB, c], bias, o_hbm, obuf, sems
+    )
+    put_features(x_ref[...].astype(F32), COEF, f_ref.at[0], f_ref.at[1])
+    for copy in copies:
+        copy.wait()
+
+
+def own_kernel(f_ref, e_ref, peer_ref, num_ref, den_ref, o_ref, done, weights):
+    done[...] = jnp.zeros_like(done)
+    half = lax.axis_index("seq") % 2
+    for rows in finish_half(half, f_ref, e_ref, peer_ref, num_ref, den_ref, o_ref, weights):
+        pass
+
+
+def tail_kernel(
+    f_ref, e_ref, peer_ref, num_ref, den_ref, own_ref, q_ref, k_ref, v_ref, kh_ref, vh_ref,
+    whole_ref, lin_hbm, win_hbm, weights, obuf, wbuf, lin_sems, win_sems,
+):
+    half = lax.axis_index("seq") % 2
+
+    def put(ref, side, at, sem):
+        copy = pltpu.make_async_copy(
+            ref, lin_hbm.at[at, pl.ds(pl.multiple_of(side * 256, 256), 256)], sem
+        )
+        copy.start()
+        return copy
+
+    copies = [put(own_ref, half, pl.ds(0, f_ref.shape[1]), lin_sems.at[2])]
+    for n, rows in enumerate(
+        finish_half(1 - half, f_ref, e_ref, peer_ref, num_ref, den_ref, obuf, weights)
+    ):
+        copies.append(put(obuf.at[rows], 1 - half, rows, lin_sems.at[n]))
+    allowed = band()
+    follows = lax.axis_index("seq") > 0
+    bias = jnp.where(allowed & ((lanes(allowed.shape) >= WINDOW) | follows), 0.0, -jnp.inf)
+
+    def pair(edge, ref):
+        return lambda c: jnp.concatenate([edge[:, c], ref[:WINDOW, c]], axis=0)
+
+    copies += narrow(
+        q_ref, 0, pair(kh_ref, k_ref), pair(vh_ref, v_ref), bias, win_hbm, wbuf, win_sems
+    )
     for copy in copies:
         copy.wait()
 
@@ -311,33 +367,28 @@
     hbm = pl.BlockSpec(memory_space=pltpu.HBM)
     feats = pltpu.VMEM((tok, PAIRS * 128), BF)
 
-    edge, q_lin, k_lin, v_lin = call(
-        load_kernel,
+    state, key_edge, val_edge, q_lin, k_lin, v_lin = call(
+        state_kernel,
         (
-            shape(2 * WINDOW, wide),
+            shape(2, ROWS, 128),
+            shape(WINDOW, wide),
+            shape(WINDOW, wide),
             shape(*q_lin.shape),
             shape(*k_lin.shape),
             shape(*v_lin.shape),
         ),
         *(pltpu.with_memory_space_constraint(x, pltpu.HBM) for x in (q_lin, k_lin, v_lin, k_win, v_win)),
         in_specs=[hbm] * 5,
-        out_specs=(VMEM,) * 4,
-        scratch_shapes=[pltpu.SemaphoreType.DMA((5,))],
+        out_specs=(VMEM,) * 6,
+        scratch_shapes=[feats] * 2 + [pltpu.SemaphoreType.DMA((5,))],
+        flops=1 << 30,
         nbytes=2 << 20,
-        vmem=4,
-    )
-    edge = lax.ppermute(edge, "seq", [(i, (i + 1) % count) for i in range(count)])
-    state = call(
-        state_kernel,
-        shape(2, ROWS, 128),
-        k_lin,
-        v_lin,
-        in_specs=[VMEM] * 2,
-        out_specs=VMEM,
-        scratch_shapes=[feats] * 2,
-        flops=1 << 30,
-        nbytes=1 << 20,
-    )
+    )
+
+    def ring(x, after):
+        x, after = lax.optimization_barrier((x, after))
+        return lax.ppermute(x, "seq", [(i, (i + 1) % count) for i in range(count)]), after
+
     peer = exchange(state, 1)
     both = state.astype(F32) + peer.astype(F32)
     carried = jnp.where(bits[0], both[1], both[0])
@@ -348,7 +399,7 @@
     def local(after):
         num, den, done = call(
             local_kernel,
-            (shape(tok, HEADS * VDIM, dtype=F32),) * 2 + (token,),
+            (shape(2, tok, HEADS * VDIM // 2, dtype=F32),) * 2 + (token,),
             q_lin,
             k_lin,
             v_lin,
@@ -379,43 +430,37 @@
         )
         return win, (done,)
 
-    def rest(after, win):
-        fa, fb, first = call(
+    def query(after, win):
+        feats, win, done = call(
             query_kernel,
-            (shape(tok, PAIRS * 128),) * 2 + (token,),
+            (shape(2, tok, PAIRS * 128), shape(tok, wide), token),
             q_lin,
-            after=after,
-            in_specs=[VMEM],
-            out_specs=(VMEM,) * 3,
-            flops=1 << 28,
-            nbytes=1 << 20,
-        )
-        out, second = call(
-            edge_kernel,
-            (shape(tok, wide), token),
             q_win,
             k_win,
             v_win,
-            edge,
             win,
             after=after,
             in_specs=[VMEM] * 4 + [hbm],
-            out_specs=(hbm, VMEM),
+            out_specs=(VMEM, hbm, VMEM),
             scratch_shapes=[
-                pltpu.VMEM((QB, wide), BF),
+                pltpu.VMEM((WINDOW, wide), BF),
                 pltpu.SemaphoreType.DMA((WHEADS // (2 * GROUP),)),
             ],
-            input_output_aliases={4: 0},
-            flops=1 << 28,
-            nbytes=1 << 20,
-        )
-        return (fa, fb, out), (first, second)
+            input_output_aliases={4: 1},
+            flops=1 << 29,
+            nbytes=2 << 20,
+        )
+        return feats, win, (done,)
 
     step, turn = 2, 0
     sums = win = feats = None
     done = ()
     while step < count:
         send = carried.astype(BF)
+        if turn == 0:
+            key_edge, send = ring(key_edge, send)
+        elif turn == 1:
+            val_edge, send = ring(val_edge, send)
         got = exchange(send, step)
         after = (send,) + done
         if turn == 0:
@@ -423,8 +468,10 @@
         elif turn == 1:
             win, done = window(after)
         elif turn == 2:
-            feats, done = rest(after, win)
-        if turn < 3:
+            feats, win, done = query(after, win)
+        if turn == 2:
+            got, done, key_edge, val_edge = lax.optimization_barrier((got, done, key_edge, val_edge))
+        elif turn < 2:
             got, done = lax.optimization_barrier((got, done))
         got = got.astype(F32)
         before = before + jnp.where(bits[turn + 1], got, 0.0)
@@ -434,22 +481,50 @@
     assert turn >= 3
     own = before.astype(BF)
     other = exchange(own, 1)
-    lin_out = call(
-        finish_kernel,
-        shape(tok, HEADS * VDIM),
-        *feats[:2],
+    weights = pltpu.VMEM((PAIRS * 128, 256), BF)
+    mine, last = call(
+        own_kernel,
+        (shape(tok, HEADS * VDIM // 2), token),
+        feats,
         own,
+        peer,
+        *sums,
+        after=done,
+        in_specs=[VMEM] * 5,
+        out_specs=(VMEM, VMEM),
+        scratch_shapes=[weights],
+        flops=1 << 29,
+        nbytes=2 << 20,
+    )
+    other, last = lax.optimization_barrier((other, last))
+    return call(
+        tail_kernel,
+        (shape(tok, HEADS * VDIM), shape(tok, wide)),
+        feats,
         other,
         peer,
         *sums,
-        after=done,
-        in_specs=[VMEM] * 7,
-        out_specs=VMEM,
-        scratch_shapes=[pltpu.VMEM((PAIRS * 128, 256), BF)] * 2,
-        flops=1 << 30,
+        mine,
+        q_win,
+        k_win,
+        v_win,
+        key_edge,
+        val_edge,
+        win,
+        after=(last,),
+        in_specs=[VMEM] * 11 + [hbm],
+        out_specs=(hbm, hbm),
+        scratch_shapes=[
+            weights,
+            pltpu.VMEM((tok, HEADS * VDIM // 2), BF),
+            pltpu.VMEM((WINDOW, wide), BF),
+            pltpu.SemaphoreType.DMA((3,)),
+            pltpu.SemaphoreType.DMA((WHEADS // (2 * GROUP),)),
+        ],
+        input_output_aliases={11: 1},
+        flops=1 << 29,
         nbytes=3 << 20,
     )
-    return (lin_out, feats[2])
 
 
 def solution(mesh):

time: 32 us -> 27.4 us (0.86)
  waiting for transfers between devices: 10.8 us -> 4.01 us
  starting transfers between devices: 7.1 us -> 9.67 us
  Pallas kernels: 13 us -> 12.3 us
    ppermute x5, waiting for transfers between devices: 10.8 us -> 3.1 us  [exchange(): return lax.ppermute(x, 'seq', [(i, i ^ step) for i in range(count)])]
    ppermute x5, starting transfers between devices: 7.03 us -> 9.66 us  [exchange(): return lax.ppermute(x, 'seq', [(i, i ^ step) for i in range(count)])]
    ppermute x1 -> x2, waiting for transfers between devices: 0.01 us -> 0.91 us  [ring(): lax.ppermute(x, 'seq', [(i, (i + 1) % count) for i in range(count)])]
    pallas_call x7 -> x6, Pallas kernels: 13 us -> 12.3 us  [call(): pl.pallas_call(run, out_shape=out, in_specs=list(in_specs) + [pl.BlockSpe...]
  transfers between devices with their start and end apart: 6 -> 7, of which waited for: 5 -> 5; matrix products, arithmetic and copies ran while one was open for 0% -> 0% of each run, Pallas kernels for 25% -> 28%
where the time goes in v3:
time: 27.4 us; the launch traced here: 26.9 us
  Pallas kernels  12.3 us (45%)
  starting transfers between devices  9.67 us (35%)
  waiting for transfers between devices  4.01 us (15%)
  between operations  0.73 us (3%)
    pallas_call x6, Pallas kernels, call(): pl.pallas_call(run, out_shape=out, in_specs=list(in_specs) + [pl.BlockSpe...  12.3 us
    ppermute x5, starting transfers between devices, exchange(): return lax.ppermute(x, 'seq', [(i, i ^ step) for i in range(count)])  9.66 us
    ppermute x5, waiting for transfers between devices, exchange(): return lax.ppermute(x, 'seq', [(i, i ^ step) for i in range(count)])  3.1 us
    ppermute x2, waiting for transfers between devices, ring(): lax.ppermute(x, 'seq', [(i, (i + 1) % count) for i in range(count)])  0.91 us
  transfers between devices with their start and end apart: 7, of which 5 were waited for; matrix products, arithmetic and copies ran while one was open for 0% of the time, Pallas kernels for 28%

profile of v3, /device:TPU:0, one launch (start us, length us, event | category | flops | bytes accessed | tf_op | source)
XLA Modules:
  0.0 26.9 jit_solution(353124086770513402)
XLA Ops:
  0.6 2.8 %state_kernel.1 = (bf16[2,336,128]{2,1,0:T(8,128)(2,1)S(1)}, bf16[64,2048]{1,0:T(8,128)(2,1)S(1)}, bf16[64,2048]{1,0:T(8,128)(2,1)S(1)}, bf16[512,128]{1,0:T(8,1...) custom-call(bf16[512,128]{1,0:T(8,128)(2,1)} %refs_0_.2, bf16[512,128]{1,0:T(8,128)(2,1)} %refs_1_.2, ...), custom_call_target="tpu_custom_call" | custom-call | flops 1073741824 | bytes 2097152 | tf_op jit(solution)/shard_map/state_kernel/pallas_call | solution.py:339
  3.4 0.5 %collective-permute-start = (bf16[2,336,128]{2,1,0:T(8,128)(2,1)S(1)}, bf16[2,336,128]{2,1,0:T(8,128)(2,1)S(1)}, u32[]{:S(2)}, u32[]{:S(2)}) collective-permute-start(bf16[2,336,128]{2,1,0:T(8,128)(2,1)S(1)} %get-tuple-element.41), channel_id=1, source_target_pairs={{0,1},{1,0},{2,3},{3,2},{4,5},{5,4},{6,7},{7,6},{8,9},{9,8},{10,11... | collective-permute-start | bytes 516104 | tf_op jit(solution)/shard_map/ppermute | solution.py:352
  3.9 1.0 %collective-permute-done.refs_2_ = bf16[2,336,128]{2,1,0:T(8,128)(2,1)S(1)} collective-permute-done((bf16[2,336,128]{2,1,0:T(8,128)(2,1)S(1)}, bf16[2,336,128]{2,1,0:T(8,128)(2,1)S(1)}, u32[]{:S(2)}, u32[]{:S(2)}) %collective-permute-start) | collective-permute-done | bytes 172064 | tf_op jit(solution)/shard_map/ppermute | solution.py:352
  5.0 2.9 %collective-permute-start.1 = (bf16[336,128]{1,0:T(8,128)(2,1)S(1)}, bf16[336,128]{1,0:T(8,128)(2,1)S(1)}, u32[]{:S(2)}, u32[]{:S(2)}) collective-permute-start(bf16[336,128]{1,0:T(8,128)(2,1)S(1)} %get-tuple-element.43.refs_3_), channel_id=1, source_target_pairs={{0,2},{1,3},{2,0},{3,1},{4,6},{5,7},{6,4},{7,5},{8,10},{9,11},{10,... | collective-permute-start | bytes 258056 | tf_op jit(solution)/shard_map/ppermute | solution.py:352
  8.0 0.0 collective-permute-start.4
  8.0 2.0 %local_kernel.1 = (f32[2,512,256]{2,1,0:T(8,128)S(1)}, f32[2,512,256]{2,1,0:T(8,128)S(1)}, f32[8,128]{1,0:T(8,128)S(1)}) custom-call(bf16[512,128]{1,0:T(8,128)(2,1)S(1)} %get-tuple-element.38.refs_0_, bf16[512,128]{1,0:T(8,128)(2,1)S(1)} %get-tuple-element.44.refs_1_, bf16[512,512]{1,0:T(8,128)(2,1)S(1)} %get-tuple-element.45.refs_2_, ...), custom_call_target="tpu_custom_call" | custom-call | flops 2147483648 | bytes 3145728 | tf_op jit(solution)/shard_map/local_kernel/pallas_call | solution.py:339
  10.0 0.8 %collective-permute-done.1 = bf16[336,128]{1,0:T(8,128)(2,1)S(1)} collective-permute-done((bf16[336,128]{1,0:T(8,128)(2,1)S(1)}, bf16[336,128]{1,0:T(8,128)(2,1)S(1)}, u32[]{:S(2)}, u32[]{:S(2)}) %collective-permute-start.1) | collective-permute-done | bytes 86048 | tf_op jit(solution)/shard_map/ppermute | solution.py:352
  10.9 1.8 %collective-permute-start.2 = (bf16[336,128]{1,0:T(8,128)(2,1)S(1)}, bf16[336,128]{1,0:T(8,128)(2,1)S(1)}, u32[]{:S(2)}, u32[]{:S(2)}) collective-permute-start(bf16[336,128]{1,0:T(8,128)(2,1)S(1)} %fusion.5.refs_3_), channel_id=1, source_target_pairs={{0,4},{1,5},{2,6},{3,7},{4,0},{5,1},{6,2},{7,3},{8,12},{9,13},{10,... | collective-permute-start | bytes 258056 | tf_op jit(solution)/shard_map/ppermute | solution.py:352
  12.7 0.0 collective-permute-start.5
  12.7 0.0 copy-done
  12.7 0.0 copy-done.1
  12.7 0.0 copy-done.2
  12.7 3.0 %window_kernel.1 = (bf16[512,2048]{1,0:T(8,128)(2,1)}, f32[8,128]{1,0:T(8,128)S(1)}) custom-call(bf16[512,2048]{1,0:T(8,128)(2,1)S(1)} %copy-done.2, bf16[512,2048]{1,0:T(8,128)(2,1)S(1)} %copy-done, bf16[512,2048]{1,0:T(8,128)(2,1)S(1)} %copy-done.1, bf16[336,128]{1,0:T(8,128)(2,1)S(1)} %fusion.5.refs_3_, f32[8,128]{1,0:T(8,128)S(1)} %get-tuple-element.49.refs_4_), custom_call_target="tpu_custom_call" | custom-call | flops 2147483648 | bytes 8388608 | tf_op jit(solution)/shard_map/window_kernel/pallas_call | solution.py:339
  15.7 0.0 collective-permute-done.2
  15.8 2.7 %collective-permute-start.3 = (bf16[336,128]{1,0:T(8,128)(2,1)S(1)}, bf16[336,128]{1,0:T(8,128)(2,1)S(1)}, u32[]{:S(2)}, u32[]{:S(2)}) collective-permute-start(bf16[336,128]{1,0:T(8,128)(2,1)S(1)} %fusion.3.refs_5_), channel_id=1, source_target_pairs={{0,8},{1,9},{2,10},{3,11},{4,12},{5,13},{6,14},{7,15},{8,0},{9,1},... | collective-permute-start | bytes 258056 | tf_op jit(solution)/shard_map/ppermute | solution.py:352
  18.4 1.9 %query_kernel.1 = (bf16[2,512,640]{2,1,0:T(8,128)(2,1)S(1)}, bf16[512,2048]{1,0:T(8,128)(2,1)}, f32[8,128]{1,0:T(8,128)S(1)}) custom-call(bf16[512,128]{1,0:T(8,128)(2,1)S(1)} %get-tuple-element.38.refs_0_, bf16[512,2048]{1,0:T(8,128)(2,1)S(1)} %copy-done.2, bf16[512,2048]{1,0:T(8,128)(2,1)S(1)} %copy-done, ...), custom_call_target="tpu_custom_call", output_to_operand_aliasing={{1}: (4, {})} | custom-call | flops 536870912 | bytes 2097152 | tf_op jit(solution)/shard_map/query_kernel/pallas_call | solution.py:339
  20.3 0.9 %collective-permute-done.3 = bf16[336,128]{1,0:T(8,128)(2,1)S(1)} collective-permute-done((bf16[336,128]{1,0:T(8,128)(2,1)S(1)}, bf16[336,128]{1,0:T(8,128)(2,1)S(1)}, u32[]{:S(2)}, u32[]{:S(2)}) %collective-permute-start.3) | collective-permute-done | bytes 86048 | tf_op jit(solution)/shard_map/ppermute | solution.py:352
  21.2 0.0 collective-permute-done.4.refs_9_
  21.2 0.9 %collective-permute-done.5.refs_10_ = bf16[64,2048]{1,0:T(8,128)(2,1)S(1)} collective-permute-done((bf16[64,2048]{1,0:T(8,128)(2,1)S(1)}, bf16[64,2048]{1,0:T(8,128)(2,1)S(1)}, u32[]{:S(2)}, u32[]{:S(2)}) %collective-permute-start.5) | collective-permute-done | bytes 262176 | tf_op jit(solution)/shard_map/ppermute | solution.py:390
  22.2 0.1 fusion.2.refs_1_
  22.2 1.7 %collective-permute-start.6 = (bf16[336,128]{1,0:T(8,128)(2,1)S(1)}, bf16[336,128]{1,0:T(8,128)(2,1)S(1)}, u32[]{:S(2)}, u32[]{:S(2)}) collective-permute-start(bf16[336,128]{1,0:T(8,128)(2,1)S(1)} %fusion.2.refs_1_), channel_id=1, source_target_pairs={{0,1},{1,0},{2,3},{3,2},{4,5},{5,4},{6,7},{7,6},{8,9},{9,8},{10,11... | collective-permute-start | bytes 258056 | tf_op jit(solution)/shard_map/ppermute | solution.py:352
  23.9 0.6 %own_kernel.1 = (bf16[512,256]{1,0:T(8,128)(2,1)S(1)}, f32[8,128]{1,0:T(8,128)S(1)}) custom-call(bf16[2,512,640]{2,1,0:T(8,128)(2,1)S(1)} %get-tuple-element.54.refs_0_, bf16[336,128]{1,0:T(8,128)(2,1)S(1)} %fusion.2.refs_1_, bf16[2,336,128]{2,1,0:T(8,128)(2,1)S(1)} %collective-permute-done.refs_2_, f32[2,512,256]{2,1,0:T(8,128)S(1)} %get-tuple-element.62.refs_3_, ...), custom_call_target="tpu_custom_call" | custom-call | flops 536870912 | bytes 2097152 | tf_op jit(solution)/shard_map/own_kernel/pallas_call | solution.py:339
  24.6 0.3 %collective-permute-done.6.refs_1_ = bf16[336,128]{1,0:T(8,128)(2,1)S(1)} collective-permute-done((bf16[336,128]{1,0:T(8,128)(2,1)S(1)}, bf16[336,128]{1,0:T(8,128)(2,1)S(1)}, u32[]{:S(2)}, u32[]{:S(2)}) %collective-permute-start.6) | collective-permute-done | bytes 86048 | tf_op jit(solution)/shard_map/ppermute | solution.py:352
  24.9 2.0 %tail_kernel.1 = (bf16[512,512]{1,0:T(8,128)(2,1)}, bf16[512,2048]{1,0:T(8,128)(2,1)}) custom-call(bf16[2,512,640]{2,1,0:T(8,128)(2,1)S(1)} %get-tuple-element.54.refs_0_, bf16[336,128]{1,0:T(8,128)(2,1)S(1)} %collective-permute-done.6.refs_1_, bf16[2,336,128]{2,1,0:T(8,128)(2,1)S(1)} %collective-permute-done.refs_2_, ...), custom_call_target="tpu_custom_call", output_to_operand_aliasing={{1}: (11, {})} | custom-call | flops 536870912 | bytes 3145728 | tf_op jit(solution)/shard_map/tail_kernel/pallas_call | solution.py:339
  (7 shorter events, 0.1 us)
Async XLA Ops:
  3.4 1.6 %collective-permute-start = (bf16[2,336,128]{2,1,0:T(8,128)(2,1)S(1)}, bf16[2,336,128]{2,1,0:T(8,128)(2,1)S(1)}, u32[]{:S(2)}, u32[]{:S(2)}) collective-permute-start(bf16[2,336,128]{2,1,0:T(8,128)(2,1)S(1)} %get-tuple-element.41), channel_id=1, source_target_pairs={{0,1},{1,0},{2,3},{3,2},{4,5},{5,4},{6,7},{7,6},{8,9},{9,8},{10,11... | collective-permute-start | bytes 516104 | tf_op jit(solution)/shard_map/ppermute | solution.py:352
  5.0 5.8 %collective-permute-start.1 = (bf16[336,128]{1,0:T(8,128)(2,1)S(1)}, bf16[336,128]{1,0:T(8,128)(2,1)S(1)}, u32[]{:S(2)}, u32[]{:S(2)}) collective-permute-start(bf16[336,128]{1,0:T(8,128)(2,1)S(1)} %get-tuple-element.43.refs_3_), channel_id=1, source_target_pairs={{0,2},{1,3},{2,0},{3,1},{4,6},{5,7},{6,4},{7,5},{8,10},{9,11},{10,... | collective-permute-start | bytes 258056 | tf_op jit(solution)/shard_map/ppermute | solution.py:352
  8.0 13.3 %collective-permute-start.4 = (bf16[64,2048]{1,0:T(8,128)(2,1)S(1)}, bf16[64,2048]{1,0:T(8,128)(2,1)S(1)}, u32[]{:S(2)}, u32[]{:S(2)}) collective-permute-start(bf16[64,2048]{1,0:T(8,128)(2,1)S(1)} %get-tuple-element.59), channel_id=1, source_target_pairs={{0,1},{1,2},{2,3},{3,4},{4,5},{5,6},{6,7},{7,8},{8,9},{9,10},{10,1... | collective-permute-start | bytes 786440 | tf_op jit(solution)/shard_map/ppermute | solution.py:390
  8.0 4.8 %copy-start = (bf16[512,2048]{1,0:T(8,128)(2,1)S(1)}, bf16[512,2048]{1,0:T(8,128)(2,1)}, u32[]{:S(2)}) copy-start(bf16[512,2048]{1,0:T(8,128)(2,1)} %refs_7_.1) | copy-start | bytes 6291460
  8.0 4.8 %copy-start.1 = (bf16[512,2048]{1,0:T(8,128)(2,1)S(1)}, bf16[512,2048]{1,0:T(8,128)(2,1)}, u32[]{:S(2)}) copy-start(bf16[512,2048]{1,0:T(8,128)(2,1)} %refs_8_.1) | copy-start | bytes 6291460
  8.0 4.8 %copy-start.2 = (bf16[512,2048]{1,0:T(8,128)(2,1)S(1)}, bf16[512,2048]{1,0:T(8,128)(2,1)}, u32[]{:S(2)}) copy-start(bf16[512,2048]{1,0:T(8,128)(2,1)} %refs_6_.1) | copy-start | bytes 6291460
  10.9 4.8 %collective-permute-start.2 = (bf16[336,128]{1,0:T(8,128)(2,1)S(1)}, bf16[336,128]{1,0:T(8,128)(2,1)S(1)}, u32[]{:S(2)}, u32[]{:S(2)}) collective-permute-start(bf16[336,128]{1,0:T(8,128)(2,1)S(1)} %fusion.5.refs_3_), channel_id=1, source_target_pairs={{0,4},{1,5},{2,6},{3,7},{4,0},{5,1},{6,2},{7,3},{8,12},{9,13},{10,... | collective-permute-start | bytes 258056 | tf_op jit(solution)/shard_map/ppermute | solution.py:352
  12.7 9.4 %collective-permute-start.5 = (bf16[64,2048]{1,0:T(8,128)(2,1)S(1)}, bf16[64,2048]{1,0:T(8,128)(2,1)S(1)}, u32[]{:S(2)}, u32[]{:S(2)}) collective-permute-start(bf16[64,2048]{1,0:T(8,128)(2,1)S(1)} %get-tuple-element.60), channel_id=1, source_target_pairs={{0,1},{1,2},{2,3},{3,4},{4,5},{5,6},{6,7},{7,8},{8,9},{9,10},{10,1... | collective-permute-start | bytes 786440 | tf_op jit(solution)/shard_map/ppermute | solution.py:390
  15.8 5.5 %collective-permute-start.3 = (bf16[336,128]{1,0:T(8,128)(2,1)S(1)}, bf16[336,128]{1,0:T(8,128)(2,1)S(1)}, u32[]{:S(2)}, u32[]{:S(2)}) collective-permute-start(bf16[336,128]{1,0:T(8,128)(2,1)S(1)} %fusion.3.refs_5_), channel_id=1, source_target_pairs={{0,8},{1,9},{2,10},{3,11},{4,12},{5,13},{6,14},{7,15},{8,0},{9,1},... | collective-permute-start | bytes 258056 | tf_op jit(solution)/shard_map/ppermute | solution.py:352
  22.2 2.7 %collective-permute-start.6 = (bf16[336,128]{1,0:T(8,128)(2,1)S(1)}, bf16[336,128]{1,0:T(8,128)(2,1)S(1)}, u32[]{:S(2)}, u32[]{:S(2)}) collective-permute-start(bf16[336,128]{1,0:T(8,128)(2,1)S(1)} %fusion.2.refs_1_), channel_id=1, source_target_pairs={{0,1},{1,0},{2,3},{3,2},{4,5},{5,4},{6,7},{7,6},{8,9},{9,8},{10,11... | collective-permute-start | bytes 258056 | tf_op jit(solution)/shard_map/ppermute | solution.py:352

commit v4 on v3

--- a/solution.py
+++ b/solution.py
@@ -34,37 +34,31 @@
     return lax.broadcasted_iota(jnp.int32, shape, len(shape) - 2)
 
 
-def feature(x, d):
-    if d == 9:
-        return x
-    if d == 0:
-        return x * x
-    low = lanes(x.shape) % KDIM < KDIM - d
-    other = jnp.where(low, pltpu.roll(x, 128 - d, 1), pltpu.roll(x, KDIM - d, 1))
-    return x * other
-
-
-def halves(first, second):
-    left = lanes(first.shape) < 64
-    return (
-        jnp.where(left, first, pltpu.roll(second, 64, 1)),
-        jnp.where(left, pltpu.roll(first, 64, 1), second),
-    )
-
-
-def put_features(x, coef, fa, fb):
-    sums = []
+def feature_pairs(x, coef):
+    src, dst = rows_of((128, 256)), lanes((128, 256))
+    order = (src // KDIM == dst // 128 * 4 + dst % 4) & (src % KDIM == dst % 64 // 4)
+    y = jnp.dot(x, order.astype(BF), preferred_element_type=F32)
+    left = lanes((x.shape[0], 128)) < 64
     for p in range(PAIRS):
-        blocks = [feature(x, d) * coef[d] for d in (2 * p, 2 * p + 1)]
-        sums.append([jnp.sum(b, axis=0, keepdims=True) for b in blocks])
-        a, b = halves(*blocks)
-        fa[:, p * 128 : (p + 1) * 128] = a.astype(BF)
-        fb[:, p * 128 : (p + 1) * 128] = b.astype(BF)
-    return sums
+        pair = []
+        for half in range(2):
+            own = y[:, half * 128 : (half + 1) * 128]
+            others = []
+            for d in (2 * p, 2 * p + 1):
+                if d == 9:
+                    others.append(jnp.ones_like(own))
+                else:
+                    others.append(pltpu.roll(own, 128 - 4 * d, 1) if d else own)
+            f = own * jnp.where(left, *others)
+            if coef is not None:
+                low, high = coef[2 * p : 2 * p + 2]
+                f = f * (low if low == high else jnp.where(left, low, high))
+            pair.append(f)
+        yield pair
 
 
 def state_kernel(
-    q_hbm, k_hbm, v_hbm, kw_hbm, vw_hbm, s_ref, ke_ref, ve_ref, q_ref, k_ref, v_ref, fa, fb, sems
+    q_hbm, k_hbm, v_hbm, kw_hbm, vw_hbm, s_ref, ke_ref, ve_ref, q_ref, k_ref, v_ref, f_ref, sems
 ):
     last = pl.ds(kw_hbm.shape[0] - WINDOW, WINDOW)
     moves = (
@@ -78,16 +72,19 @@
     for copy in copies:
         copy.start()
     copies[0].wait()
-    sums = put_features(k_ref[...].astype(F32), (1.0,) * BLOCKS, fa, fb)
+    sums = []
+    for p, pair in enumerate(feature_pairs(k_ref[...], None)):
+        sums.append([jnp.sum(f, axis=0, keepdims=True) for f in pair])
+        for half, f in enumerate(pair):
+            f_ref[half, :, p * 128 : (p + 1) * 128] = f.astype(BF)
     copies[1].wait()
-    zs = [halves(*pair) for pair in sums]
     v = v_ref[...]
     vsum = jnp.sum(v.astype(F32), axis=0, keepdims=True)
     left = lanes((64, 128)) < 64
-    even = (rows_of((64, 128)) // KDIM) % 2 == 0
-    for half, f in ((0, fa), (1, fb)):
+    head = rows_of((64, 128)) % 4
+    for half in range(2):
         r = lax.dot_general(
-            f[...],
+            f_ref[half],
             v[:, half * 256 : (half + 1) * 256],
             (((0,), (0,)), ((), ())),
             preferred_element_type=F32,
@@ -96,13 +93,10 @@
             pieces = []
             for par in range(2):
                 at = p * 128 + par * 64
-                z = jnp.concatenate(
-                    [r[at : at + 32, :128], r[at + 32 : at + 64, 128:]], axis=0
-                )
-                keep = even if par == 0 else jnp.logical_not(even)
-                pieces.append(jnp.where(keep, z, pltpu.roll(z, 64, 1)))
+                z = jnp.where(head < 2, r[at : at + 64, :128], r[at : at + 64, 128:])
+                pieces.append(jnp.where(head % 2 == par, z, pltpu.roll(z, 64, 1)))
             s_ref[half, p * 64 : (p + 1) * 64, :] = jnp.where(left, *pieces).astype(BF)
-        aux = [z[half] for z in zs]
+        aux = [total[half] for total in sums]
         aux += [vsum[:, half * 256 + t * 128 : half * 256 + (t + 1) * 128] for t in range(2)]
         aux.append(jnp.zeros((ROWS - MAIN - PAIRS - 2, 128), F32))
         s_ref[half, MAIN:, :] = jnp.concatenate(aux, axis=0).astype(BF)
@@ -153,9 +147,9 @@
     me = lax.axis_index("seq")
     core = me % 2
     left = lanes((64, 128)) < 64
-    row = rows_of((64, 128)) // KDIM
+    row = rows_of((64, 128)) % 4
     col = lanes((64, 128)) // VDIM
-    span = ((rows_of((256, 256)) // KDIM) % 4 == lanes((256, 256)) // VDIM).astype(BF)
+    span = (rows_of((256, 256)) % 4 == lanes((256, 256)) // VDIM).astype(BF)
     count = (me * tok).astype(F32)
     state = e_ref[...].astype(F32) + jnp.where(core == 1, peer_ref[half].astype(F32), 0.0)
     for p in range(PAIRS):
@@ -245,8 +239,8 @@
         copy.wait()
 
 
-def narrow(q_ref, first_row, k_of, v_of, bias, o_hbm, obuf, sems):
-    copies, group = [], 2 * GROUP * WDIM
+def narrow_weights(q_ref, first_row, k_of, bias, put):
+    group = 2 * GROUP * WDIM
     rows = slice(first_row, first_row + WINDOW)
     for h in range(0, q_ref.shape[1], group):
         places = [slice(c, c + WDIM) for c in range(h, h + group, WDIM)]
@@ -260,19 +254,9 @@
         )
         s = s * SCALE + bias
         e = jnp.exp2(s - jnp.max(s, axis=2, keepdims=True))
-        inverse = 1.0 / jnp.sum(e, axis=2, keepdims=True)
-        e = e.astype(BF)
+        e = (e * (1.0 / jnp.sum(e, axis=2, keepdims=True))).astype(BF)
         for n, c in enumerate(places):
-            o = jnp.dot(e[n], v_of(c), preferred_element_type=F32) * inverse[n]
-            obuf[:, c] = o.astype(BF)
-        cols = pl.ds(h, group)
-        copies.append(
-            pltpu.make_async_copy(
-                obuf.at[:, cols], o_hbm.at[pl.ds(first_row, WINDOW), cols], sems.at[h // group]
-            )
-        )
-        copies[-1].start()
-    return copies
+            put(c, e[n])
 
 
 def band():
@@ -280,27 +264,52 @@
     return (key > query) & (key <= query + WINDOW)
 
 
-def query_kernel(x_ref, q_ref, k_ref, v_ref, whole_ref, f_ref, o_hbm, done, obuf, sems):
+def query_kernel(x_ref, f_ref, done):
     done[...] = jnp.zeros_like(done)
-    bias = jnp.where(band(), 0.0, -jnp.inf)
-    copies = narrow(
-        q_ref, WINDOW, lambda c: k_ref[:QB, c], lambda c: v_ref[:QB, c], bias, o_hbm, obuf, sems
-    )
-    put_features(x_ref[...].astype(F32), COEF, f_ref.at[0], f_ref.at[1])
-    for copy in copies:
-        copy.wait()
-
-
-def own_kernel(f_ref, e_ref, peer_ref, num_ref, den_ref, o_ref, done, weights):
+    for p, pair in enumerate(feature_pairs(x_ref[...], COEF)):
+        for half, f in enumerate(pair):
+            f_ref[half, :, p * 128 : (p + 1) * 128] = f.astype(BF)
+
+
+def top_kernel(q_ref, k_ref, v_ref, kh_ref, whole_ref, w_ref, o_hbm, done, obuf, sem):
     done[...] = jnp.zeros_like(done)
+    allowed = band()
+
+    def put(c, w):
+        obuf[:, c] = jnp.dot(w, v_ref[:QB, c], preferred_element_type=F32).astype(BF)
+
+    narrow_weights(
+        q_ref, WINDOW, lambda c: k_ref[:QB, c], jnp.where(allowed, 0.0, -jnp.inf), put
+    )
+    copy = pltpu.make_async_copy(obuf, o_hbm.at[pl.ds(WINDOW, WINDOW)], sem)
+    copy.start()
+    follows = lax.axis_index("seq") > 0
+    bias = jnp.where(allowed & ((lanes(allowed.shape) >= WINDOW) | follows), 0.0, -jnp.inf)
+
+    def keep(c, w):
+        w_ref[:, c] = w
+
+    narrow_weights(
+        q_ref, 0, lambda c: jnp.concatenate([kh_ref[:, c], k_ref[:WINDOW, c]], axis=0), bias, keep
+    )
+    copy.wait()
+
+
+def own_kernel(
+    f_ref, e_ref, peer_ref, num_ref, den_ref, w_ref, v_ref, vh_ref, o_ref, top_ref, weights
+):
     half = lax.axis_index("seq") % 2
     for rows in finish_half(half, f_ref, e_ref, peer_ref, num_ref, den_ref, o_ref, weights):
         pass
+    for c in range(0, w_ref.shape[1], WDIM):
+        c = slice(c, c + WDIM)
+        v = jnp.concatenate([vh_ref[:, c], v_ref[:WINDOW, c]], axis=0)
+        top_ref[:, c] = jnp.dot(w_ref[:, c], v, preferred_element_type=F32).astype(BF)
 
 
 def tail_kernel(
-    f_ref, e_ref, peer_ref, num_ref, den_ref, own_ref, q_ref, k_ref, v_ref, kh_ref, vh_ref,
-    whole_ref, lin_hbm, win_hbm, weights, obuf, wbuf, lin_sems, win_sems,
+    f_ref, e_ref, peer_ref, num_ref, den_ref, own_ref, top_ref, whole_ref,
+    lin_hbm, win_hbm, weights, obuf, sems,
 ):
     half = lax.axis_index("seq") % 2
 
@@ -311,21 +320,15 @@
         copy.start()
         return copy
 
-    copies = [put(own_ref, half, pl.ds(0, f_ref.shape[1]), lin_sems.at[2])]
+    copies = [
+        pltpu.make_async_copy(top_ref, win_hbm.at[pl.ds(0, WINDOW)], sems.at[3]),
+        put(own_ref, half, pl.ds(0, f_ref.shape[1]), sems.at[2]),
+    ]
+    copies[0].start()
     for n, rows in enumerate(
         finish_half(1 - half, f_ref, e_ref, peer_ref, num_ref, den_ref, obuf, weights)
     ):
-        copies.append(put(obuf.at[rows], 1 - half, rows, lin_sems.at[n]))
-    allowed = band()
-    follows = lax.axis_index("seq") > 0
-    bias = jnp.where(allowed & ((lanes(allowed.shape) >= WINDOW) | follows), 0.0, -jnp.inf)
-
-    def pair(edge, ref):
-        return lambda c: jnp.concatenate([edge[:, c], ref[:WINDOW, c]], axis=0)
-
-    copies += narrow(
-        q_ref, 0, pair(kh_ref, k_ref), pair(vh_ref, v_ref), bias, win_hbm, wbuf, win_sems
-    )
+        copies.append(put(obuf.at[rows], 1 - half, rows, sems.at[n]))
     for copy in copies:
         copy.wait()
 
@@ -365,7 +368,6 @@
     bits, k_lin = lax.optimization_barrier((bits, k_lin))
     wide = WHEADS * WDIM
     hbm = pl.BlockSpec(memory_space=pltpu.HBM)
-    feats = pltpu.VMEM((tok, PAIRS * 128), BF)
 
     state, key_edge, val_edge, q_lin, k_lin, v_lin = call(
         state_kernel,
@@ -380,7 +382,7 @@
         *(pltpu.with_memory_space_constraint(x, pltpu.HBM) for x in (q_lin, k_lin, v_lin, k_win, v_win)),
         in_specs=[hbm] * 5,
         out_specs=(VMEM,) * 6,
-        scratch_shapes=[feats] * 2 + [pltpu.SemaphoreType.DMA((5,))],
+        scratch_shapes=[pltpu.VMEM((2, tok, PAIRS * 128), BF), pltpu.SemaphoreType.DMA((5,))],
         flops=1 << 30,
         nbytes=2 << 20,
     )
@@ -390,11 +392,22 @@
         return lax.ppermute(x, "seq", [(i, (i + 1) % count) for i in range(count)]), after
 
     peer = exchange(state, 1)
+    token = shape(8, 128, dtype=F32)
+    feats, first = call(
+        query_kernel,
+        (shape(2, tok, PAIRS * 128), token),
+        q_lin,
+        after=(state,),
+        in_specs=[VMEM],
+        out_specs=(VMEM, VMEM),
+        flops=1 << 28,
+        nbytes=2 << 20,
+    )
+    done = (first,)
+    peer, done = lax.optimization_barrier((peer, done))
     both = state.astype(F32) + peer.astype(F32)
     carried = jnp.where(bits[0], both[1], both[0])
     before = jnp.zeros_like(carried)
-
-    token = shape(8, 128, dtype=F32)
 
     def local(after):
         num, den, done = call(
@@ -430,47 +443,43 @@
         )
         return win, (done,)
 
-    def query(after, win):
-        feats, win, done = call(
-            query_kernel,
-            (shape(2, tok, PAIRS * 128), shape(tok, wide), token),
-            q_lin,
+    def top(after, win):
+        shares, win, done = call(
+            top_kernel,
+            (shape(WINDOW, wide), shape(tok, wide), token),
             q_win,
             k_win,
             v_win,
+            key_edge,
             win,
             after=after,
             in_specs=[VMEM] * 4 + [hbm],
             out_specs=(VMEM, hbm, VMEM),
-            scratch_shapes=[
-                pltpu.VMEM((WINDOW, wide), BF),
-                pltpu.SemaphoreType.DMA((WHEADS // (2 * GROUP),)),
-            ],
+            scratch_shapes=[pltpu.VMEM((WINDOW, wide), BF), pltpu.SemaphoreType.DMA],
             input_output_aliases={4: 1},
-            flops=1 << 29,
+            flops=1 << 30,
             nbytes=2 << 20,
         )
-        return feats, win, (done,)
+        return shares, win, (done,)
 
     step, turn = 2, 0
-    sums = win = feats = None
-    done = ()
+    sums = win = shares = None
     while step < count:
         send = carried.astype(BF)
         if turn == 0:
             key_edge, send = ring(key_edge, send)
         elif turn == 1:
             val_edge, send = ring(val_edge, send)
-        got = exchange(send, step)
+        got = exchange(send, step + step // 2 if 2 * step == count else step)
         after = (send,) + done
         if turn == 0:
             sums, done = local(after)
         elif turn == 1:
             win, done = window(after)
         elif turn == 2:
-            feats, win, done = query(after, win)
+            shares, win, done = top(after, win)
         if turn == 2:
-            got, done, key_edge, val_edge = lax.optimization_barrier((got, done, key_edge, val_edge))
+            got, done, val_edge = lax.optimization_barrier((got, done, val_edge))
         elif turn < 2:
             got, done = lax.optimization_barrier((got, done))
         got = got.astype(F32)
@@ -482,21 +491,24 @@
     own = before.astype(BF)
     other = exchange(own, 1)
     weights = pltpu.VMEM((PAIRS * 128, 256), BF)
-    mine, last = call(
+    mine, top = call(
         own_kernel,
-        (shape(tok, HEADS * VDIM // 2), token),
+        (shape(tok, HEADS * VDIM // 2), shape(WINDOW, wide)),
         feats,
         own,
         peer,
         *sums,
+        shares,
+        v_win,
+        val_edge,
         after=done,
-        in_specs=[VMEM] * 5,
+        in_specs=[VMEM] * 8,
         out_specs=(VMEM, VMEM),
         scratch_shapes=[weights],
-        flops=1 << 29,
-        nbytes=2 << 20,
-    )
-    other, last = lax.optimization_barrier((other, last))
+        flops=1 << 30,
+        nbytes=3 << 20,
+    )
+    other, mine, top = lax.optimization_barrier((other, mine, top))
     return call(
         tail_kernel,
         (shape(tok, HEADS * VDIM), shape(tok, wide)),
@@ -505,25 +517,18 @@
         peer,
         *sums,
         mine,
-        q_win,
-        k_win,
-        v_win,
-        key_edge,
-        val_edge,
+        top,
         win,
-        after=(last,),
-        in_specs=[VMEM] * 11 + [hbm],
+        in_specs=[VMEM] * 7 + [hbm],
         out_specs=(hbm, hbm),
         scratch_shapes=[
             weights,
             pltpu.VMEM((tok, HEADS * VDIM // 2), BF),
-            pltpu.VMEM((WINDOW, wide), BF),
-            pltpu.SemaphoreType.DMA((3,)),
-            pltpu.SemaphoreType.DMA((WHEADS // (2 * GROUP),)),
+            pltpu.SemaphoreType.DMA((4,)),
         ],
-        input_output_aliases={11: 1},
+        input_output_aliases={7: 1},
         flops=1 << 29,
-        nbytes=3 << 20,
+        nbytes=2 << 20,
     )
 
 

time: 27.4 us -> 26.2 us (0.956); the launches traced: 26.9 us -> 26 us
  waiting for transfers between devices: 4.01 us -> 2.14 us
  Pallas kernels: 12.3 us -> 13.3 us
    pallas_call x6 -> x7, Pallas kernels: 12.3 us -> 13.3 us  [call(): pl.pallas_call(run, out_shape=out, in_specs=list(in_specs) + [pl.BlockSpe...]
    ppermute x5, waiting for transfers between devices: 3.1 us -> 2.14 us  [exchange(): return lax.ppermute(x, 'seq', [(i, i ^ step) for i in range(count)])]
    ppermute x2, waiting for transfers between devices: 0.91 us -> 0.01 us  [ring(): lax.ppermute(x, 'seq', [(i, (i + 1) % count) for i in range(count)])]
  transfers between devices with their start and end apart: 7 -> 7, of which waited for: 5 -> 3; matrix products, arithmetic and copies ran while one was open for 0% -> 0% of each run, Pallas kernels for 28% -> 35%
where the time goes in v4:
time: 26.2 us; the launch traced here: 26 us
  Pallas kernels  13.3 us (51%)
  starting transfers between devices  9.64 us (37%)
  waiting for transfers between devices  2.14 us (8%)
  between operations  0.74 us (3%)
    pallas_call x7, Pallas kernels, call(): pl.pallas_call(run, out_shape=out, in_specs=list(in_specs) + [pl.BlockSpe...  13.3 us
    ppermute x5, starting transfers between devices, exchange(): return lax.ppermute(x, 'seq', [(i, i ^ step) for i in range(count)])  9.48 us
    ppermute x5, waiting for transfers between devices, exchange(): return lax.ppermute(x, 'seq', [(i, i ^ step) for i in range(count)])  2.14 us
  transfers between devices with their start and end apart: 7, of which 3 were waited for; matrix products, arithmetic and copies ran while one was open for 0% of the time, Pallas kernels for 35%

profile of v4, /device:TPU:0, one launch (start us, length us, event | category | flops | bytes accessed | tf_op | source)
XLA Modules:
  0.0 26.0 jit_solution(12470101433605034670)
XLA Ops:
  0.6 2.9 %state_kernel.1 = (bf16[2,336,128]{2,1,0:T(8,128)(2,1)S(1)}, bf16[64,2048]{1,0:T(8,128)(2,1)S(1)}, bf16[64,2048]{1,0:T(8,128)(2,1)S(1)}, bf16[512,128]{1,0:T(8,1...) custom-call(bf16[512,128]{1,0:T(8,128)(2,1)} %refs_0_.3, bf16[512,128]{1,0:T(8,128)(2,1)} %refs_1_.2, ...), custom_call_target="tpu_custom_call" | custom-call | flops 1073741824 | bytes 2097152 | tf_op jit(solution)/shard_map/state_kernel/pallas_call | solution.py:342
  3.6 0.5 %collective-permute-start = (bf16[2,336,128]{2,1,0:T(8,128)(2,1)S(1)}, bf16[2,336,128]{2,1,0:T(8,128)(2,1)S(1)}, u32[]{:S(2)}, u32[]{:S(2)}) collective-permute-start(bf16[2,336,128]{2,1,0:T(8,128)(2,1)S(1)} %get-tuple-element.43.refs_1_), channel_id=1, source_target_pairs={{0,1},{1,0},{2,3},{3,2},{4,5},{5,4},{6,7},{7,6},{8,9},{9,8},{10,11... | collective-permute-start | bytes 516104 | tf_op jit(solution)/shard_map/ppermute | solution.py:355
  4.1 1.3 %query_kernel.1 = (bf16[2,512,640]{2,1,0:T(8,128)(2,1)S(1)}, f32[8,128]{1,0:T(8,128)S(1)}) custom-call(bf16[512,128]{1,0:T(8,128)(2,1)S(1)} %get-tuple-element.42.refs_0_, bf16[2,336,128]{2,1,0:T(8,128)(2,1)S(1)} %get-tuple-element.43.refs_1_), custom_call_target="tpu_custom_call" | custom-call | flops 268435456 | bytes 2097152 | tf_op jit(solution)/shard_map/query_kernel/pallas_call | solution.py:342
  5.4 0.0 collective-permute-done.refs_2_
  5.5 2.6 %collective-permute-start.1 = (bf16[336,128]{1,0:T(8,128)(2,1)S(1)}, bf16[336,128]{1,0:T(8,128)(2,1)S(1)}, u32[]{:S(2)}, u32[]{:S(2)}) collective-permute-start(bf16[336,128]{1,0:T(8,128)(2,1)S(1)} %get-tuple-element.50.refs_3_), channel_id=1, source_target_pairs={{0,2},{1,3},{2,0},{3,1},{4,6},{5,7},{6,4},{7,5},{8,10},{9,11},{10,... | collective-permute-start | bytes 258056 | tf_op jit(solution)/shard_map/ppermute | solution.py:355
  8.1 0.2 collective-permute-start.4
  8.3 2.0 %local_kernel.1 = (f32[2,512,256]{2,1,0:T(8,128)S(1)}, f32[2,512,256]{2,1,0:T(8,128)S(1)}, f32[8,128]{1,0:T(8,128)S(1)}) custom-call(bf16[512,128]{1,0:T(8,128)(2,1)S(1)} %get-tuple-element.42.refs_0_, bf16[512,128]{1,0:T(8,128)(2,1)S(1)} %get-tuple-element.51.refs_1_, bf16[512,512]{1,0:T(8,128)(2,1)S(1)} %get-tuple-element.52.refs_2_, ...), custom_call_target="tpu_custom_call" | custom-call | flops 2147483648 | bytes 3145728 | tf_op jit(solution)/shard_map/local_kernel/pallas_call | solution.py:342
  10.3 0.9 %collective-permute-done.1 = bf16[336,128]{1,0:T(8,128)(2,1)S(1)} collective-permute-done((bf16[336,128]{1,0:T(8,128)(2,1)S(1)}, bf16[336,128]{1,0:T(8,128)(2,1)S(1)}, u32[]{:S(2)}, u32[]{:S(2)}) %collective-permute-start.1) | collective-permute-done | bytes 86048 | tf_op jit(solution)/shard_map/ppermute | solution.py:355
  11.3 1.9 %collective-permute-start.2 = (bf16[336,128]{1,0:T(8,128)(2,1)S(1)}, bf16[336,128]{1,0:T(8,128)(2,1)S(1)}, u32[]{:S(2)}, u32[]{:S(2)}) collective-permute-start(bf16[336,128]{1,0:T(8,128)(2,1)S(1)} %fusion.5.refs_3_), channel_id=1, source_target_pairs={{0,4},{1,5},{2,6},{3,7},{4,0},{5,1},{6,2},{7,3},{8,12},{9,13},{10,... | collective-permute-start | bytes 258056 | tf_op jit(solution)/shard_map/ppermute | solution.py:355
  13.2 0.0 collective-permute-start.5
  13.2 0.0 copy-done
  13.2 0.0 copy-done.1
  13.2 3.0 %window_kernel.1 = (bf16[512,2048]{1,0:T(8,128)(2,1)}, f32[8,128]{1,0:T(8,128)S(1)}) custom-call(bf16[512,2048]{1,0:T(8,128)(2,1)S(1)} %copy-done.2, bf16[512,2048]{1,0:T(8,128)(2,1)S(1)} %copy-done.1, bf16[512,2048]{1,0:T(8,128)(2,1)S(1)} %copy-done, bf16[336,128]{1,0:T(8,128)(2,1)S(1)} %fusion.5.refs_3_, f32[8,128]{1,0:T(8,128)S(1)} %get-tuple-element.59.refs_4_), custom_call_target="tpu_custom_call" | custom-call | flops 2147483648 | bytes 8388608 | tf_op jit(solution)/shard_map/window_kernel/pallas_call | solution.py:342
  16.2 0.0 collective-permute-done.2
  16.3 3.5 %collective-permute-start.3 = (bf16[336,128]{1,0:T(8,128)(2,1)S(1)}, bf16[336,128]{1,0:T(8,128)(2,1)S(1)}, u32[]{:S(2)}, u32[]{:S(2)}) collective-permute-start(bf16[336,128]{1,0:T(8,128)(2,1)S(1)} %fusion.3.refs_5_), channel_id=1, source_target_pairs={{0,12},{1,13},{2,14},{3,15},{4,8},{5,9},{6,10},{7,11},{8,4},{9,5},... | collective-permute-start | bytes 258056 | tf_op jit(solution)/shard_map/ppermute | solution.py:355
  19.8 0.0 collective-permute-done.4.refs_3_
  19.8 1.9 %top_kernel.1 = (bf16[64,2048]{1,0:T(8,128)(2,1)S(1)}, bf16[512,2048]{1,0:T(8,128)(2,1)}, f32[8,128]{1,0:T(8,128)S(1)}) custom-call(bf16[512,2048]{1,0:T(8,128)(2,1)S(1)} %copy-done.2, bf16[512,2048]{1,0:T(8,128)(2,1)S(1)} %copy-done.1, bf16[512,2048]{1,0:T(8,128)(2,1)S(1)} %copy-done, ...), custom_call_target="tpu_custom_call", output_to_operand_aliasing={{1}: (4, {})} | custom-call | flops 1073741824 | bytes 2097152 | tf_op jit(solution)/shard_map/top_kernel/pallas_call | solution.py:342
  21.7 1.1 %collective-permute-done.3 = bf16[336,128]{1,0:T(8,128)(2,1)S(1)} collective-permute-done((bf16[336,128]{1,0:T(8,128)(2,1)S(1)}, bf16[336,128]{1,0:T(8,128)(2,1)S(1)}, u32[]{:S(2)}, u32[]{:S(2)}) %collective-permute-start.3) | collective-permute-done | bytes 86048 | tf_op jit(solution)/shard_map/ppermute | solution.py:355
  22.7 0.0 collective-permute-done.5.refs_7_
  22.7 0.1 fusion.2.refs_1_
  22.8 0.9 %collective-permute-start.6 = (bf16[336,128]{1,0:T(8,128)(2,1)S(1)}, bf16[336,128]{1,0:T(8,128)(2,1)S(1)}, u32[]{:S(2)}, u32[]{:S(2)}) collective-permute-start(bf16[336,128]{1,0:T(8,128)(2,1)S(1)} %fusion.2.refs_1_), channel_id=1, source_target_pairs={{0,1},{1,0},{2,3},{3,2},{4,5},{5,4},{6,7},{7,6},{8,9},{9,8},{10,11... | collective-permute-start | bytes 258056 | tf_op jit(solution)/shard_map/ppermute | solution.py:355
  23.7 0.8 %own_kernel.1 = (bf16[512,256]{1,0:T(8,128)(2,1)S(1)}, bf16[64,2048]{1,0:T(8,128)(2,1)S(1)}) custom-call(bf16[2,512,640]{2,1,0:T(8,128)(2,1)S(1)} %get-tuple-element.44.refs_0_, bf16[336,128]{1,0:T(8,128)(2,1)S(1)} %fusion.2.refs_1_, bf16[2,336,128]{2,1,0:T(8,128)(2,1)S(1)} %collective-permute-done.refs_2_, f32[2,512,256]{2,1,0:T(8,128)S(1)} %get-tuple-element.69.refs_3_, ...), custom_call_target="tpu_custom_call" | custom-call | flops 1073741824 | bytes 3145728 | tf_op jit(solution)/shard_map/own_kernel/pallas_call | solution.py:342
  24.5 0.1 collective-permute-done.6.refs_1_
  24.7 1.4 %tail_kernel.1 = (bf16[512,512]{1,0:T(8,128)(2,1)}, bf16[512,2048]{1,0:T(8,128)(2,1)}) custom-call(bf16[2,512,640]{2,1,0:T(8,128)(2,1)S(1)} %get-tuple-element.44.refs_0_, bf16[336,128]{1,0:T(8,128)(2,1)S(1)} %collective-permute-done.6.refs_1_, bf16[2,336,128]{2,1,0:T(8,128)(2,1)S(1)} %collective-permute-done.refs_2_, ...), custom_call_target="tpu_custom_call", output_to_operand_aliasing={{1}: (7, {})} | custom-call | flops 536870912 | bytes 2097152 | tf_op jit(solution)/shard_map/tail_kernel/pallas_call | solution.py:342
  (8 shorter events, 0.1 us)
Async XLA Ops:
  3.6 1.8 %collective-permute-start = (bf16[2,336,128]{2,1,0:T(8,128)(2,1)S(1)}, bf16[2,336,128]{2,1,0:T(8,128)(2,1)S(1)}, u32[]{:S(2)}, u32[]{:S(2)}) collective-permute-start(bf16[2,336,128]{2,1,0:T(8,128)(2,1)S(1)} %get-tuple-element.43.refs_1_), channel_id=1, source_target_pairs={{0,1},{1,0},{2,3},{3,2},{4,5},{5,4},{6,7},{7,6},{8,9},{9,8},{10,11... | collective-permute-start | bytes 516104 | tf_op jit(solution)/shard_map/ppermute | solution.py:355
  5.5 5.8 %collective-permute-start.1 = (bf16[336,128]{1,0:T(8,128)(2,1)S(1)}, bf16[336,128]{1,0:T(8,128)(2,1)S(1)}, u32[]{:S(2)}, u32[]{:S(2)}) collective-permute-start(bf16[336,128]{1,0:T(8,128)(2,1)S(1)} %get-tuple-element.50.refs_3_), channel_id=1, source_target_pairs={{0,2},{1,3},{2,0},{3,1},{4,6},{5,7},{6,4},{7,5},{8,10},{9,11},{10,... | collective-permute-start | bytes 258056 | tf_op jit(solution)/shard_map/ppermute | solution.py:355
  8.1 11.7 %collective-permute-start.4 = (bf16[64,2048]{1,0:T(8,128)(2,1)S(1)}, bf16[64,2048]{1,0:T(8,128)(2,1)S(1)}, u32[]{:S(2)}, u32[]{:S(2)}) collective-permute-start(bf16[64,2048]{1,0:T(8,128)(2,1)S(1)} %get-tuple-element.63), channel_id=1, source_target_pairs={{0,1},{1,2},{2,3},{3,4},{4,5},{5,6},{6,7},{7,8},{8,9},{9,10},{10,1... | collective-permute-start | bytes 786440 | tf_op jit(solution)/shard_map/ppermute | solution.py:392
  8.3 4.9 %copy-start = (bf16[512,2048]{1,0:T(8,128)(2,1)S(1)}, bf16[512,2048]{1,0:T(8,128)(2,1)}, u32[]{:S(2)}) copy-start(bf16[512,2048]{1,0:T(8,128)(2,1)} %refs_6_.1) | copy-start | bytes 6291460
  8.3 4.9 %copy-start.1 = (bf16[512,2048]{1,0:T(8,128)(2,1)S(1)}, bf16[512,2048]{1,0:T(8,128)(2,1)}, u32[]{:S(2)}) copy-start(bf16[512,2048]{1,0:T(8,128)(2,1)} %refs_1_.4) | copy-start | bytes 6291460
  8.3 4.9 %copy-start.2 = (bf16[512,2048]{1,0:T(8,128)(2,1)S(1)}, bf16[512,2048]{1,0:T(8,128)(2,1)}, u32[]{:S(2)}) copy-start(bf16[512,2048]{1,0:T(8,128)(2,1)} %refs_0_.5) | copy-start | bytes 6291460
  11.3 5.0 %collective-permute-start.2 = (bf16[336,128]{1,0:T(8,128)(2,1)S(1)}, bf16[336,128]{1,0:T(8,128)(2,1)S(1)}, u32[]{:S(2)}, u32[]{:S(2)}) collective-permute-start(bf16[336,128]{1,0:T(8,128)(2,1)S(1)} %fusion.5.refs_3_), channel_id=1, source_target_pairs={{0,4},{1,5},{2,6},{3,7},{4,0},{5,1},{6,2},{7,3},{8,12},{9,13},{10,... | collective-permute-start | bytes 258056 | tf_op jit(solution)/shard_map/ppermute | solution.py:355
  13.2 9.6 %collective-permute-start.5 = (bf16[64,2048]{1,0:T(8,128)(2,1)S(1)}, bf16[64,2048]{1,0:T(8,128)(2,1)S(1)}, u32[]{:S(2)}, u32[]{:S(2)}) collective-permute-start(bf16[64,2048]{1,0:T(8,128)(2,1)S(1)} %get-tuple-element.67), channel_id=1, source_target_pairs={{0,1},{1,2},{2,3},{3,4},{4,5},{5,6},{6,7},{7,8},{8,9},{9,10},{10,1... | collective-permute-start | bytes 786440 | tf_op jit(solution)/shard_map/ppermute | solution.py:392
  16.3 6.4 %collective-permute-start.3 = (bf16[336,128]{1,0:T(8,128)(2,1)S(1)}, bf16[336,128]{1,0:T(8,128)(2,1)S(1)}, u32[]{:S(2)}, u32[]{:S(2)}) collective-permute-start(bf16[336,128]{1,0:T(8,128)(2,1)S(1)} %fusion.3.refs_5_), channel_id=1, source_target_pairs={{0,12},{1,13},{2,14},{3,15},{4,8},{5,9},{6,10},{7,11},{8,4},{9,5},... | collective-permute-start | bytes 258056 | tf_op jit(solution)/shard_map/ppermute | solution.py:355
  22.8 1.9 %collective-permute-start.6 = (bf16[336,128]{1,0:T(8,128)(2,1)S(1)}, bf16[336,128]{1,0:T(8,128)(2,1)S(1)}, u32[]{:S(2)}, u32[]{:S(2)}) collective-permute-start(bf16[336,128]{1,0:T(8,128)(2,1)S(1)} %fusion.2.refs_1_), channel_id=1, source_target_pairs={{0,1},{1,0},{2,3},{3,2},{4,5},{5,4},{6,7},{7,6},{8,9},{9,8},{10,11... | collective-permute-start | bytes 258056 | tf_op jit(solution)/shard_map/ppermute | solution.py:355

commit v5 on v4

--- a/solution.py
+++ b/solution.py
@@ -34,31 +34,36 @@
     return lax.broadcasted_iota(jnp.int32, shape, len(shape) - 2)
 
 
-def feature_pairs(x, coef):
-    src, dst = rows_of((128, 256)), lanes((128, 256))
-    order = (src // KDIM == dst // 128 * 4 + dst % 4) & (src % KDIM == dst % 64 // 4)
-    y = jnp.dot(x, order.astype(BF), preferred_element_type=F32)
+def orders():
+    dims = (128, (1 + PAIRS) * 256)
+    src, dst = rows_of(dims), lanes(dims)
+    d = jnp.where(dst < 256, 0, dst // 256 * 2 - 2 + dst % 128 // 64)
+    head, entry = dst % 256 // 128 * 4 + dst % 4, (dst % 64 // 4 + d) % KDIM
+    return (src == head * KDIM + entry).astype(BF)
+
+
+def feature_pairs(x, order, coef):
+    own = jnp.dot(x, order[:, :256], preferred_element_type=F32)
+    others = jnp.dot(x, order[:, 256:], preferred_element_type=F32)
     left = lanes((x.shape[0], 128)) < 64
     for p in range(PAIRS):
         pair = []
         for half in range(2):
-            own = y[:, half * 128 : (half + 1) * 128]
-            others = []
-            for d in (2 * p, 2 * p + 1):
-                if d == 9:
-                    others.append(jnp.ones_like(own))
-                else:
-                    others.append(pltpu.roll(own, 128 - 4 * d, 1) if d else own)
-            f = own * jnp.where(left, *others)
+            at = p * 256 + half * 128
+            other = others[:, at : at + 128]
+            if p == PAIRS - 1:
+                other = jnp.where(left, other, 1.0)
+            f = own[:, half * 128 : (half + 1) * 128] * other
             if coef is not None:
                 low, high = coef[2 * p : 2 * p + 2]
-                f = f * (low if low == high else jnp.where(left, low, high))
+                f = f * (low if low == high else jnp.where(left[:1], low, high))
             pair.append(f)
         yield pair
 
 
 def state_kernel(
-    q_hbm, k_hbm, v_hbm, kw_hbm, vw_hbm, s_ref, ke_ref, ve_ref, q_ref, k_ref, v_ref, f_ref, sems
+    q_hbm, k_hbm, v_hbm, kw_hbm, vw_hbm,
+    s_ref, ke_ref, ve_ref, q_ref, k_ref, v_ref, order_ref, f_ref, sems,
 ):
     last = pl.ds(kw_hbm.shape[0] - WINDOW, WINDOW)
     moves = (
@@ -71,9 +76,10 @@
     copies = [pltpu.make_async_copy(src, dst, sems.at[n]) for n, (src, dst) in enumerate(moves)]
     for copy in copies:
         copy.start()
+    order_ref[...] = orders()
     copies[0].wait()
     sums = []
-    for p, pair in enumerate(feature_pairs(k_ref[...], None)):
+    for p, pair in enumerate(feature_pairs(k_ref[...], order_ref[...], None)):
         sums.append([jnp.sum(f, axis=0, keepdims=True) for f in pair])
         for half, f in enumerate(pair):
             f_ref[half, :, p * 128 : (p + 1) * 128] = f.astype(BF)
@@ -164,8 +170,8 @@
                 ).astype(BF)
     at = MAIN + PAIRS
     vsum = jnp.concatenate([state[at : at + 1, :], state[at + 1 : at + 2, :]], axis=1)
-    step = tok // 2
-    for n in range(2):
+    step = tok // 4
+    for n in range(tok // step):
         rows = slice(n * step, (n + 1) * step)
         f = f_ref[half, rows, :]
         acc = jnp.zeros((step, 128), F32)
@@ -208,35 +214,24 @@
     ]
 
 
-def window_kernel(q_ref, k_ref, v_ref, o_hbm, done, obuf, sems):
+def window_kernel(q_ref, k_ref, v_ref, o_ref, done):
     done[...] = jnp.zeros_like(done)
     earlier, allowed = masks()
     bias = jnp.where(allowed, 0.0, -jnp.inf)
     tok, wide = q_ref.shape
-    copies = []
     for h in range(0, wide, GROUP * WDIM):
         places = [
-            (at, slice(c, c + WDIM))
+            (slice(at, at + QB), slice(at - QB, at + QB), slice(c, c + WDIM))
             for c in range(h, h + GROUP * WDIM, WDIM)
             for at in range(QB, tok, QB)
         ]
         outs = attend(
-            [
-                (q_ref[at : at + QB, c], k_ref[at - QB : at + QB, c], v_ref[at - QB : at + QB, c])
-                for at, c in places
-            ],
+            [(q_ref[rows, c], k_ref[keys, c], v_ref[keys, c]) for rows, keys, c in places],
             earlier,
             bias,
         )
-        for (at, c), out in zip(places, outs):
-            obuf[at : at + QB, c] = out
-        part = (pl.ds(QB, tok - QB), pl.ds(h, GROUP * WDIM))
-        copies.append(
-            pltpu.make_async_copy(obuf.at[part], o_hbm.at[part], sems.at[h // (GROUP * WDIM)])
-        )
-        copies[-1].start()
-    for copy in copies:
-        copy.wait()
+        for (rows, _, c), out in zip(places, outs):
+            o_ref[rows, c] = out
 
 
 def narrow_weights(q_ref, first_row, k_of, bias, put):
@@ -264,16 +259,19 @@
     return (key > query) & (key <= query + WINDOW)
 
 
-def query_kernel(x_ref, f_ref, done):
+def query_kernel(x_ref, order_ref, f_ref, done):
     done[...] = jnp.zeros_like(done)
-    for p, pair in enumerate(feature_pairs(x_ref[...], COEF)):
+    for p, pair in enumerate(feature_pairs(x_ref[...], order_ref[...], COEF)):
         for half, f in enumerate(pair):
             f_ref[half, :, p * 128 : (p + 1) * 128] = f.astype(BF)
 
 
-def top_kernel(q_ref, k_ref, v_ref, kh_ref, whole_ref, w_ref, o_hbm, done, obuf, sem):
+def top_kernel(q_ref, k_ref, v_ref, kh_ref, rest_ref, w_ref, o_hbm, done, obuf, sems):
     done[...] = jnp.zeros_like(done)
     allowed = band()
+    rows = pl.ds(QB, q_ref.shape[0] - QB)
+    copies = [pltpu.make_async_copy(rest_ref.at[rows], o_hbm.at[rows], sems.at[0])]
+    copies[0].start()
 
     def put(c, w):
         obuf[:, c] = jnp.dot(w, v_ref[:QB, c], preferred_element_type=F32).astype(BF)
@@ -281,8 +279,8 @@
     narrow_weights(
         q_ref, WINDOW, lambda c: k_ref[:QB, c], jnp.where(allowed, 0.0, -jnp.inf), put
     )
-    copy = pltpu.make_async_copy(obuf, o_hbm.at[pl.ds(WINDOW, WINDOW)], sem)
-    copy.start()
+    copies.append(pltpu.make_async_copy(obuf, o_hbm.at[pl.ds(WINDOW, WINDOW)], sems.at[1]))
+    copies[1].start()
     follows = lax.axis_index("seq") > 0
     bias = jnp.where(allowed & ((lanes(allowed.shape) >= WINDOW) | follows), 0.0, -jnp.inf)
 
@@ -292,7 +290,8 @@
     narrow_weights(
         q_ref, 0, lambda c: jnp.concatenate([kh_ref[:, c], k_ref[:WINDOW, c]], axis=0), bias, keep
     )
-    copy.wait()
+    for copy in copies:
+        copy.wait()
 
 
 def own_kernel(
@@ -321,8 +320,8 @@
         return copy
 
     copies = [
-        pltpu.make_async_copy(top_ref, win_hbm.at[pl.ds(0, WINDOW)], sems.at[3]),
-        put(own_ref, half, pl.ds(0, f_ref.shape[1]), sems.at[2]),
+        pltpu.make_async_copy(top_ref, win_hbm.at[pl.ds(0, WINDOW)], sems.at[5]),
+        put(own_ref, half, pl.ds(0, f_ref.shape[1]), sems.at[4]),
     ]
     copies[0].start()
     for n, rows in enumerate(
@@ -369,7 +368,7 @@
     wide = WHEADS * WDIM
     hbm = pl.BlockSpec(memory_space=pltpu.HBM)
 
-    state, key_edge, val_edge, q_lin, k_lin, v_lin = call(
+    state, key_edge, val_edge, q_lin, k_lin, v_lin, order = call(
         state_kernel,
         (
             shape(2, ROWS, 128),
@@ -378,10 +377,11 @@
             shape(*q_lin.shape),
             shape(*k_lin.shape),
             shape(*v_lin.shape),
+            shape(128, (1 + PAIRS) * 256),
         ),
         *(pltpu.with_memory_space_constraint(x, pltpu.HBM) for x in (q_lin, k_lin, v_lin, k_win, v_win)),
         in_specs=[hbm] * 5,
-        out_specs=(VMEM,) * 6,
+        out_specs=(VMEM,) * 7,
         scratch_shapes=[pltpu.VMEM((2, tok, PAIRS * 128), BF), pltpu.SemaphoreType.DMA((5,))],
         flops=1 << 30,
         nbytes=2 << 20,
@@ -397,8 +397,9 @@
         query_kernel,
         (shape(2, tok, PAIRS * 128), token),
         q_lin,
+        order,
         after=(state,),
-        in_specs=[VMEM],
+        in_specs=[VMEM] * 2,
         out_specs=(VMEM, VMEM),
         flops=1 << 28,
         nbytes=2 << 20,
@@ -433,11 +434,7 @@
             v_win,
             after=after,
             in_specs=[VMEM] * 3,
-            out_specs=(hbm, VMEM),
-            scratch_shapes=[
-                pltpu.VMEM((tok, wide), BF),
-                pltpu.SemaphoreType.DMA((WHEADS // GROUP,)),
-            ],
+            out_specs=(VMEM, VMEM),
             flops=1 << 31,
             nbytes=8 << 20,
         )
@@ -453,10 +450,12 @@
             key_edge,
             win,
             after=after,
-            in_specs=[VMEM] * 4 + [hbm],
+            in_specs=[VMEM] * 5,
             out_specs=(VMEM, hbm, VMEM),
-            scratch_shapes=[pltpu.VMEM((WINDOW, wide), BF), pltpu.SemaphoreType.DMA],
-            input_output_aliases={4: 1},
+            scratch_shapes=[
+                pltpu.VMEM((WINDOW, wide), BF),
+                pltpu.SemaphoreType.DMA((2,)),
+            ],
             flops=1 << 30,
             nbytes=2 << 20,
         )
@@ -524,7 +523,7 @@
         scratch_shapes=[
             weights,
             pltpu.VMEM((tok, HEADS * VDIM // 2), BF),
-            pltpu.SemaphoreType.DMA((4,)),
+            pltpu.SemaphoreType.DMA((6,)),
         ],
         input_output_aliases={7: 1},
         flops=1 << 29,

time: 26.2 us -> 25 us (0.954)
  the two profiles are of different devices: /device:TPU:0 before, /device:TPU:15 now
where the time goes in v5:
time: 25 us; the launch traced here: 24.9 us
  Pallas kernels  10.9 us (44%)
  starting transfers between devices  8.05 us (32%)
  waiting for transfers between devices  4.97 us (20%)
  between operations  0.72 us (3%)
    pallas_call x7, Pallas kernels, call(): pl.pallas_call(run, out_shape=out, in_specs=list(in_specs) + [pl.BlockSpe...  10.9 us
    ppermute x2, starting transfers between devices, ring(): lax.ppermute(x, 'seq', [(i, (i + 1) % count) for i in range(count)])  5.21 us
    ppermute x5, waiting for transfers between devices, exchange(): return lax.ppermute(x, 'seq', [(i, i ^ step) for i in range(count)])  4.96 us
    ppermute x5, starting transfers between devices, exchange(): return lax.ppermute(x, 'seq', [(i, i ^ step) for i in range(count)])  2.83 us
  transfers between devices with their start and end apart: 7, of which 3 were waited for; matrix products, arithmetic and copies ran while one was open for 0% of the time, Pallas kernels for 30%

profile of v5, /device:TPU:15, one launch (start us, length us, event | category | flops | bytes accessed | tf_op | source)
XLA Modules:
  0.0 24.9 jit_solution(4782710960563693228)
XLA Ops:
  0.6 2.2 %state_kernel.1 = (bf16[2,336,128]{2,1,0:T(8,128)(2,1)S(1)}, bf16[64,2048]{1,0:T(8,128)(2,1)S(1)}, bf16[64,2048]{1,0:T(8,128)(2,1)S(1)}, bf16[512,128]{1,0:T(8,1...) custom-call(bf16[512,128]{1,0:T(8,128)(2,1)} %refs_0_.3, ...), custom_call_target="tpu_custom_call" | custom-call | flops 1073741824 | bytes 2097152 | tf_op jit(solution)/shard_map/state_kernel/pallas_call | solution.py:341
  2.8 0.7 %collective-permute-start = (bf16[2,336,128]{2,1,0:T(8,128)(2,1)S(1)}, bf16[2,336,128]{2,1,0:T(8,128)(2,1)S(1)}, u32[]{:S(2)}, u32[]{:S(2)}) collective-permute-start(bf16[2,336,128]{2,1,0:T(8,128)(2,1)S(1)} %get-tuple-element.45.refs_2_), channel_id=1, source_target_pairs={{0,1},{1,0},{2,3},{3,2},{4,5},{5,4},{6,7},{7,6},{8,9},{9,8},{10,11... | collective-permute-start | bytes 516104 | tf_op jit(solution)/shard_map/ppermute | solution.py:354
  3.5 0.6 %query_kernel.1 = (bf16[2,512,640]{2,1,0:T(8,128)(2,1)S(1)}, f32[8,128]{1,0:T(8,128)S(1)}) custom-call(bf16[512,128]{1,0:T(8,128)(2,1)S(1)} %get-tuple-element.43.refs_0_, bf16[128,1536]{1,0:T(8,128)(2,1)S(1)} %get-tuple-element.44.refs_1_, bf16[2,336,128]{2,1,0:T(8,128)(2,1)S(1)} %get-tuple-element.45.refs_2_), custom_call_target="tpu_custom_call" | custom-call | flops 268435456 | bytes 2097152 | tf_op jit(solution)/shard_map/query_kernel/pallas_call | solution.py:341
  4.1 0.5 %collective-permute-done.refs_2_ = bf16[2,336,128]{2,1,0:T(8,128)(2,1)S(1)} collective-permute-done((bf16[2,336,128]{2,1,0:T(8,128)(2,1)S(1)}, bf16[2,336,128]{2,1,0:T(8,128)(2,1)S(1)}, u32[]{:S(2)}, u32[]{:S(2)}) %collective-permute-start) | collective-permute-done | bytes 172064 | tf_op jit(solution)/shard_map/ppermute | solution.py:354
  4.7 0.3 %collective-permute-start.1 = (bf16[336,128]{1,0:T(8,128)(2,1)S(1)}, bf16[336,128]{1,0:T(8,128)(2,1)S(1)}, u32[]{:S(2)}, u32[]{:S(2)}) collective-permute-start(bf16[336,128]{1,0:T(8,128)(2,1)S(1)} %get-tuple-element.52.refs_3_), channel_id=1, source_target_pairs={{0,2},{1,3},{2,0},{3,1},{4,6},{5,7},{6,4},{7,5},{8,10},{9,11},{10,... | collective-permute-start | bytes 258056 | tf_op jit(solution)/shard_map/ppermute | solution.py:354
  5.0 2.8 %collective-permute-start.4 = (bf16[64,2048]{1,0:T(8,128)(2,1)S(1)}, bf16[64,2048]{1,0:T(8,128)(2,1)S(1)}, u32[]{:S(2)}, u32[]{:S(2)}) collective-permute-start(bf16[64,2048]{1,0:T(8,128)(2,1)S(1)} %get-tuple-element.65), channel_id=1, source_target_pairs={{0,1},{1,2},{2,3},{3,4},{4,5},{5,6},{6,7},{7,8},{8,9},{9,10},{10,1... | collective-permute-start | bytes 786440 | tf_op jit(solution)/shard_map/ppermute | solution.py:392
  7.7 2.0 %local_kernel.1 = (f32[2,512,256]{2,1,0:T(8,128)S(1)}, f32[2,512,256]{2,1,0:T(8,128)S(1)}, f32[8,128]{1,0:T(8,128)S(1)}) custom-call(bf16[512,128]{1,0:T(8,128)(2,1)S(1)} %get-tuple-element.43.refs_0_, bf16[512,128]{1,0:T(8,128)(2,1)S(1)} %get-tuple-element.53.refs_1_, bf16[512,512]{1,0:T(8,128)(2,1)S(1)} %get-tuple-element.54.refs_2_, ...), custom_call_target="tpu_custom_call" | custom-call | flops 2147483648 | bytes 3145728 | tf_op jit(solution)/shard_map/local_kernel/pallas_call | solution.py:341
  9.8 0.0 collective-permute-done.1
  9.8 0.2 collective-permute-start.2
  10.0 2.5 %collective-permute-start.5 = (bf16[64,2048]{1,0:T(8,128)(2,1)S(1)}, bf16[64,2048]{1,0:T(8,128)(2,1)S(1)}, u32[]{:S(2)}, u32[]{:S(2)}) collective-permute-start(bf16[64,2048]{1,0:T(8,128)(2,1)S(1)} %get-tuple-element.69), channel_id=1, source_target_pairs={{0,1},{1,2},{2,3},{3,4},{4,5},{5,6},{6,7},{7,8},{8,9},{9,10},{10,1... | collective-permute-start | bytes 786440 | tf_op jit(solution)/shard_map/ppermute | solution.py:392
  12.5 0.0 copy-done
  12.5 0.0 copy-done.1
  12.5 2.3 %window_kernel.1 = (bf16[512,2048]{1,0:T(8,128)(2,1)S(1)}, f32[8,128]{1,0:T(8,128)S(1)}) custom-call(bf16[512,2048]{1,0:T(8,128)(2,1)S(1)} %copy-done.2, bf16[512,2048]{1,0:T(8,128)(2,1)S(1)} %copy-done.1, bf16[512,2048]{1,0:T(8,128)(2,1)S(1)} %copy-done, bf16[336,128]{1,0:T(8,128)(2,1)S(1)} %fusion.5.refs_3_, f32[8,128]{1,0:T(8,128)S(1)} %get-tuple-element.61.refs_4_), custom_call_target="tpu_custom_call" | custom-call | flops 2147483648 | bytes 8388608 | tf_op jit(solution)/shard_map/window_kernel/pallas_call | solution.py:341
  14.8 0.0 collective-permute-done.2
  14.8 0.2 collective-permute-start.3
  15.1 0.0 collective-permute-done.4.refs_3_
  15.1 1.9 %top_kernel.1 = (bf16[64,2048]{1,0:T(8,128)(2,1)S(1)}, bf16[512,2048]{1,0:T(8,128)(2,1)}, f32[8,128]{1,0:T(8,128)S(1)}) custom-call(bf16[512,2048]{1,0:T(8,128)(2,1)S(1)} %copy-done.2, bf16[512,2048]{1,0:T(8,128)(2,1)S(1)} %copy-done.1, bf16[512,2048]{1,0:T(8,128)(2,1)S(1)} %copy-done, bf16[64,2048]{1,0:T(8,128)(2,1)S(1)} %collective-permute-done.4.refs_3_, ...), custom_call_target="tpu_custom_call" | custom-call | flops 1073741824 | bytes 2097152 | tf_op jit(solution)/shard_map/top_kernel/pallas_call | solution.py:341
  17.0 4.3 %collective-permute-done.3 = bf16[336,128]{1,0:T(8,128)(2,1)S(1)} collective-permute-done((bf16[336,128]{1,0:T(8,128)(2,1)S(1)}, bf16[336,128]{1,0:T(8,128)(2,1)S(1)}, u32[]{:S(2)}, u32[]{:S(2)}) %collective-permute-start.3) | collective-permute-done | bytes 86048 | tf_op jit(solution)/shard_map/ppermute | solution.py:354
  21.3 0.0 collective-permute-done.5.refs_7_
  21.3 0.1 fusion.2.refs_1_
  21.3 1.3 %collective-permute-start.6 = (bf16[336,128]{1,0:T(8,128)(2,1)S(1)}, bf16[336,128]{1,0:T(8,128)(2,1)S(1)}, u32[]{:S(2)}, u32[]{:S(2)}) collective-permute-start(bf16[336,128]{1,0:T(8,128)(2,1)S(1)} %fusion.2.refs_1_), channel_id=1, source_target_pairs={{0,1},{1,0},{2,3},{3,2},{4,5},{5,4},{6,7},{7,6},{8,9},{9,8},{10,11... | collective-permute-start | bytes 258056 | tf_op jit(solution)/shard_map/ppermute | solution.py:354
  22.6 0.8 %own_kernel.1 = (bf16[512,256]{1,0:T(8,128)(2,1)S(1)}, bf16[64,2048]{1,0:T(8,128)(2,1)S(1)}) custom-call(bf16[2,512,640]{2,1,0:T(8,128)(2,1)S(1)} %get-tuple-element.46.refs_0_, bf16[336,128]{1,0:T(8,128)(2,1)S(1)} %fusion.2.refs_1_, bf16[2,336,128]{2,1,0:T(8,128)(2,1)S(1)} %collective-permute-done.refs_2_, f32[2,512,256]{2,1,0:T(8,128)S(1)} %get-tuple-element.71.refs_3_, ...), custom_call_target="tpu_custom_call" | custom-call | flops 1073741824 | bytes 3145728 | tf_op jit(solution)/shard_map/own_kernel/pallas_call | solution.py:341
  23.4 0.2 collective-permute-done.6.refs_1_
  23.6 1.3 %tail_kernel.1 = (bf16[512,512]{1,0:T(8,128)(2,1)}, bf16[512,2048]{1,0:T(8,128)(2,1)}) custom-call(bf16[2,512,640]{2,1,0:T(8,128)(2,1)S(1)} %get-tuple-element.46.refs_0_, bf16[336,128]{1,0:T(8,128)(2,1)S(1)} %collective-permute-done.6.refs_1_, bf16[2,336,128]{2,1,0:T(8,128)(2,1)S(1)} %collective-permute-done.refs_2_, ...), custom_call_target="tpu_custom_call", output_to_operand_aliasing={{1}: (7, {})} | custom-call | flops 536870912 | bytes 2097152 | tf_op jit(solution)/shard_map/tail_kernel/pallas_call | solution.py:341
  (8 shorter events, 0.1 us)
Async XLA Ops:
  2.8 1.8 %collective-permute-start = (bf16[2,336,128]{2,1,0:T(8,128)(2,1)S(1)}, bf16[2,336,128]{2,1,0:T(8,128)(2,1)S(1)}, u32[]{:S(2)}, u32[]{:S(2)}) collective-permute-start(bf16[2,336,128]{2,1,0:T(8,128)(2,1)S(1)} %get-tuple-element.45.refs_2_), channel_id=1, source_target_pairs={{0,1},{1,0},{2,3},{3,2},{4,5},{5,4},{6,7},{7,6},{8,9},{9,8},{10,11... | collective-permute-start | bytes 516104 | tf_op jit(solution)/shard_map/ppermute | solution.py:354
  4.7 5.1 %collective-permute-start.1 = (bf16[336,128]{1,0:T(8,128)(2,1)S(1)}, bf16[336,128]{1,0:T(8,128)(2,1)S(1)}, u32[]{:S(2)}, u32[]{:S(2)}) collective-permute-start(bf16[336,128]{1,0:T(8,128)(2,1)S(1)} %get-tuple-element.52.refs_3_), channel_id=1, source_target_pairs={{0,2},{1,3},{2,0},{3,1},{4,6},{5,7},{6,4},{7,5},{8,10},{9,11},{10,... | collective-permute-start | bytes 258056 | tf_op jit(solution)/shard_map/ppermute | solution.py:354
  5.0 10.1 %collective-permute-start.4 = (bf16[64,2048]{1,0:T(8,128)(2,1)S(1)}, bf16[64,2048]{1,0:T(8,128)(2,1)S(1)}, u32[]{:S(2)}, u32[]{:S(2)}) collective-permute-start(bf16[64,2048]{1,0:T(8,128)(2,1)S(1)} %get-tuple-element.65), channel_id=1, source_target_pairs={{0,1},{1,2},{2,3},{3,4},{4,5},{5,6},{6,7},{7,8},{8,9},{9,10},{10,1... | collective-permute-start | bytes 786440 | tf_op jit(solution)/shard_map/ppermute | solution.py:392
  7.7 4.8 %copy-start = (bf16[512,2048]{1,0:T(8,128)(2,1)S(1)}, bf16[512,2048]{1,0:T(8,128)(2,1)}, u32[]{:S(2)}) copy-start(bf16[512,2048]{1,0:T(8,128)(2,1)} %refs_6_.1) | copy-start | bytes 6291460
  7.7 4.8 %copy-start.1 = (bf16[512,2048]{1,0:T(8,128)(2,1)S(1)}, bf16[512,2048]{1,0:T(8,128)(2,1)}, u32[]{:S(2)}) copy-start(bf16[512,2048]{1,0:T(8,128)(2,1)} %refs_1_.4) | copy-start | bytes 6291460
  7.7 4.8 %copy-start.2 = (bf16[512,2048]{1,0:T(8,128)(2,1)S(1)}, bf16[512,2048]{1,0:T(8,128)(2,1)}, u32[]{:S(2)}) copy-start(bf16[512,2048]{1,0:T(8,128)(2,1)} %refs_0_.5) | copy-start | bytes 6291460
  9.8 5.0 %collective-permute-start.2 = (bf16[336,128]{1,0:T(8,128)(2,1)S(1)}, bf16[336,128]{1,0:T(8,128)(2,1)S(1)}, u32[]{:S(2)}, u32[]{:S(2)}) collective-permute-start(bf16[336,128]{1,0:T(8,128)(2,1)S(1)} %fusion.5.refs_3_), channel_id=1, source_target_pairs={{0,4},{1,5},{2,6},{3,7},{4,0},{5,1},{6,2},{7,3},{8,12},{9,13},{10,... | collective-permute-start | bytes 258056 | tf_op jit(solution)/shard_map/ppermute | solution.py:354
  10.0 11.2 %collective-permute-start.5 = (bf16[64,2048]{1,0:T(8,128)(2,1)S(1)}, bf16[64,2048]{1,0:T(8,128)(2,1)S(1)}, u32[]{:S(2)}, u32[]{:S(2)}) collective-permute-start(bf16[64,2048]{1,0:T(8,128)(2,1)S(1)} %get-tuple-element.69), channel_id=1, source_target_pairs={{0,1},{1,2},{2,3},{3,4},{4,5},{5,6},{6,7},{7,8},{8,9},{9,10},{10,1... | collective-permute-start | bytes 786440 | tf_op jit(solution)/shard_map/ppermute | solution.py:392
  14.8 6.4 %collective-permute-start.3 = (bf16[336,128]{1,0:T(8,128)(2,1)S(1)}, bf16[336,128]{1,0:T(8,128)(2,1)S(1)}, u32[]{:S(2)}, u32[]{:S(2)}) collective-permute-start(bf16[336,128]{1,0:T(8,128)(2,1)S(1)} %fusion.3.refs_5_), channel_id=1, source_target_pairs={{0,12},{1,13},{2,14},{3,15},{4,8},{5,9},{6,10},{7,11},{8,4},{9,5},... | collective-permute-start | bytes 258056 | tf_op jit(solution)/shard_map/ppermute | solution.py:354
  21.3 2.2 %collective-permute-start.6 = (bf16[336,128]{1,0:T(8,128)(2,1)S(1)}, bf16[336,128]{1,0:T(8,128)(2,1)S(1)}, u32[]{:S(2)}, u32[]{:S(2)}) collective-permute-start(bf16[336,128]{1,0:T(8,128)(2,1)S(1)} %fusion.2.refs_1_), channel_id=1, source_target_pairs={{0,1},{1,0},{2,3},{3,2},{4,5},{5,4},{6,7},{7,6},{8,9},{9,8},{10,11... | collective-permute-start | bytes 258056 | tf_op jit(solution)/shard_map/ppermute | solution.py:354

commit v6 on v5

--- a/solution.py
+++ b/solution.py
@@ -77,6 +77,7 @@
     for copy in copies:
         copy.start()
     order_ref[...] = orders()
+    core = lax.axis_index("seq") % 2
     copies[0].wait()
     sums = []
     for p, pair in enumerate(feature_pairs(k_ref[...], order_ref[...], None)):
@@ -89,6 +90,7 @@
     left = lanes((64, 128)) < 64
     head = rows_of((64, 128)) % 4
     for half in range(2):
+        slot = (core + half) % 2
         r = lax.dot_general(
             f_ref[half],
             v[:, half * 256 : (half + 1) * 256],
@@ -101,11 +103,11 @@
                 at = p * 128 + par * 64
                 z = jnp.where(head < 2, r[at : at + 64, :128], r[at : at + 64, 128:])
                 pieces.append(jnp.where(head % 2 == par, z, pltpu.roll(z, 64, 1)))
-            s_ref[half, p * 64 : (p + 1) * 64, :] = jnp.where(left, *pieces).astype(BF)
+            s_ref[slot, p * 64 : (p + 1) * 64, :] = jnp.where(left, *pieces).astype(BF)
         aux = [total[half] for total in sums]
         aux += [vsum[:, half * 256 + t * 128 : half * 256 + (t + 1) * 128] for t in range(2)]
         aux.append(jnp.zeros((ROWS - MAIN - PAIRS - 2, 128), F32))
-        s_ref[half, MAIN:, :] = jnp.concatenate(aux, axis=0).astype(BF)
+        s_ref[slot, MAIN:, :] = jnp.concatenate(aux, axis=0).astype(BF)
     for copy in copies[2:]:
         copy.wait()
 
@@ -148,16 +150,15 @@
                 den_ref[half, rows, cols] = pltpu.roll(jnp.where(left, b, a), 64, 1)
 
 
-def finish_half(half, f_ref, e_ref, peer_ref, num_ref, den_ref, obuf, weights):
+def finish_half(half, f_ref, e_ref, num_ref, den_ref, obuf, weights):
     tok = f_ref.shape[1]
     me = lax.axis_index("seq")
-    core = me % 2
     left = lanes((64, 128)) < 64
     row = rows_of((64, 128)) % 4
     col = lanes((64, 128)) // VDIM
     span = (rows_of((256, 256)) % 4 == lanes((256, 256)) // VDIM).astype(BF)
     count = (me * tok).astype(F32)
-    state = e_ref[...].astype(F32) + jnp.where(core == 1, peer_ref[half].astype(F32), 0.0)
+    state = e_ref[...].astype(F32)
     for p in range(PAIRS):
         c = state[p * 64 : (p + 1) * 64, :]
         turned = pltpu.roll(c, 64, 1)
@@ -295,10 +296,10 @@
 
 
 def own_kernel(
-    f_ref, e_ref, peer_ref, num_ref, den_ref, w_ref, v_ref, vh_ref, o_ref, top_ref, weights
+    f_ref, e_ref, num_ref, den_ref, w_ref, v_ref, vh_ref, o_ref, top_ref, weights
 ):
     half = lax.axis_index("seq") % 2
-    for rows in finish_half(half, f_ref, e_ref, peer_ref, num_ref, den_ref, o_ref, weights):
+    for rows in finish_half(half, f_ref, e_ref, num_ref, den_ref, o_ref, weights):
         pass
     for c in range(0, w_ref.shape[1], WDIM):
         c = slice(c, c + WDIM)
@@ -307,7 +308,7 @@
 
 
 def tail_kernel(
-    f_ref, e_ref, peer_ref, num_ref, den_ref, own_ref, top_ref, whole_ref,
+    f_ref, e_ref, num_ref, den_ref, own_ref, top_ref, whole_ref,
     lin_hbm, win_hbm, weights, obuf, sems,
 ):
     half = lax.axis_index("seq") % 2
@@ -325,7 +326,7 @@
     ]
     copies[0].start()
     for n, rows in enumerate(
-        finish_half(1 - half, f_ref, e_ref, peer_ref, num_ref, den_ref, obuf, weights)
+        finish_half(1 - half, f_ref, e_ref, num_ref, den_ref, obuf, weights)
     ):
         copies.append(put(obuf.at[rows], 1 - half, rows, sems.at[n]))
     for copy in copies:
@@ -391,7 +392,7 @@
         x, after = lax.optimization_barrier((x, after))
         return lax.ppermute(x, "seq", [(i, (i + 1) % count) for i in range(count)]), after
 
-    peer = exchange(state, 1)
+    peer = exchange(state[1], 1)
     token = shape(8, 128, dtype=F32)
     feats, first = call(
         query_kernel,
@@ -406,8 +407,8 @@
     )
     done = (first,)
     peer, done = lax.optimization_barrier((peer, done))
-    both = state.astype(F32) + peer.astype(F32)
-    carried = jnp.where(bits[0], both[1], both[0])
+    mine, peer = state[0].astype(F32), peer.astype(F32)
+    carried = mine + peer
     before = jnp.zeros_like(carried)
 
     def local(after):
@@ -487,21 +488,20 @@
         step *= 2
         turn += 1
     assert turn >= 3
-    own = before.astype(BF)
-    other = exchange(own, 1)
+    own = (before + jnp.where(bits[0], peer, 0.0)).astype(BF)
+    other = exchange((before + jnp.where(bits[0], 0.0, mine)).astype(BF), 1)
     weights = pltpu.VMEM((PAIRS * 128, 256), BF)
     mine, top = call(
         own_kernel,
         (shape(tok, HEADS * VDIM // 2), shape(WINDOW, wide)),
         feats,
         own,
-        peer,
         *sums,
         shares,
         v_win,
         val_edge,
         after=done,
-        in_specs=[VMEM] * 8,
+        in_specs=[VMEM] * 7,
         out_specs=(VMEM, VMEM),
         scratch_shapes=[weights],
         flops=1 << 30,
@@ -513,19 +513,18 @@
         (shape(tok, HEADS * VDIM), shape(tok, wide)),
         feats,
         other,
-        peer,
         *sums,
         mine,
         top,
         win,
-        in_specs=[VMEM] * 7 + [hbm],
+        in_specs=[VMEM] * 6 + [hbm],
         out_specs=(hbm, hbm),
         scratch_shapes=[
             weights,
             pltpu.VMEM((tok, HEADS * VDIM // 2), BF),
             pltpu.SemaphoreType.DMA((6,)),
         ],
-        input_output_aliases={7: 1},
+        input_output_aliases={6: 1},
         flops=1 << 29,
         nbytes=2 << 20,
     )

time: 25 us -> 24.9 us (level)
  the two profiles are of different devices: /device:TPU:15 before, /device:TPU:11 now
where the time goes in v6:
time: 24.9 us; the launch traced here: 24.7 us
  Pallas kernels  10.9 us (44%)
  starting transfers between devices  8.04 us (32%)
  waiting for transfers between devices  4.85 us (19%)
  between operations  0.73 us (3%)
    pallas_call x7, Pallas kernels, call(): pl.pallas_call(run, out_shape=out, in_specs=list(in_specs) + [pl.BlockSpe...  10.9 us
    ppermute x2, starting transfers between devices, ring(): lax.ppermute(x, 'seq', [(i, (i + 1) % count) for i in range(count)])  5.22 us
    ppermute x5, waiting for transfers between devices, exchange(): return lax.ppermute(x, 'seq', [(i, i ^ step) for i in range(count)])  4.85 us
    ppermute x5, starting transfers between devices, exchange(): return lax.ppermute(x, 'seq', [(i, i ^ step) for i in range(count)])  2.82 us
  transfers between devices with their start and end apart: 7, of which 3 were waited for; matrix products, arithmetic and copies ran while one was open for 0% of the time, Pallas kernels for 30%

profile of v6, /device:TPU:11, one launch (start us, length us, event | category | flops | bytes accessed | tf_op | source)
XLA Modules:
  0.0 24.7 jit_solution(3516089027641610376)
XLA Ops:
  0.6 2.1 %state_kernel.1 = (bf16[2,336,128]{2,1,0:T(8,128)(2,1)S(1)}, bf16[64,2048]{1,0:T(8,128)(2,1)S(1)}, bf16[64,2048]{1,0:T(8,128)(2,1)S(1)}, bf16[512,128]{1,0:T(8,1...) custom-call(bf16[512,128]{1,0:T(8,128)(2,1)} %refs_0_.3, ...), custom_call_target="tpu_custom_call" | custom-call | flops 1073741824 | bytes 2097152 | tf_op jit(solution)/shard_map/state_kernel/pallas_call | solution.py:342
  2.8 0.7 %collective-permute-start = (bf16[336,128]{1,0:T(8,128)(2,1)S(1)}, bf16[336,128]{1,0:T(8,128)(2,1)S(1)}, u32[]{:S(2)}, u32[]{:S(2)}) collective-permute-start(bf16[336,128]{1,0:T(8,128)(2,1)S(1)} %slice_bitcast_fusion), channel_id=1, source_target_pairs={{0,1},{1,0},{2,3},{3,2},{4,5},{5,4},{6,7},{7,6},{8,9},{9,8},{10,11... | collective-permute-start | bytes 258056 | tf_op jit(solution)/shard_map/ppermute | solution.py:355
  3.6 0.6 %query_kernel.1 = (bf16[2,512,640]{2,1,0:T(8,128)(2,1)S(1)}, f32[8,128]{1,0:T(8,128)S(1)}) custom-call(bf16[512,128]{1,0:T(8,128)(2,1)S(1)} %get-tuple-element.43.refs_0_, bf16[128,1536]{1,0:T(8,128)(2,1)S(1)} %get-tuple-element.44.refs_1_, bf16[2,336,128]{2,1,0:T(8,128)(2,1)S(1)} %get-tuple-element.45.refs_2_), custom_call_target="tpu_custom_call" | custom-call | flops 268435456 | bytes 2097152 | tf_op jit(solution)/shard_map/query_kernel/pallas_call | solution.py:342
  4.1 0.4 %collective-permute-done = bf16[336,128]{1,0:T(8,128)(2,1)S(1)} collective-permute-done((bf16[336,128]{1,0:T(8,128)(2,1)S(1)}, bf16[336,128]{1,0:T(8,128)(2,1)S(1)}, u32[]{:S(2)}, u32[]{:S(2)}) %collective-permute-start) | collective-permute-done | bytes 86048 | tf_op jit(solution)/shard_map/ppermute | solution.py:355
  4.5 0.3 %collective-permute-start.1 = (bf16[336,128]{1,0:T(8,128)(2,1)S(1)}, bf16[336,128]{1,0:T(8,128)(2,1)S(1)}, u32[]{:S(2)}, u32[]{:S(2)}) collective-permute-start(bf16[336,128]{1,0:T(8,128)(2,1)S(1)} %fusion.7.refs_3_), channel_id=1, source_target_pairs={{0,2},{1,3},{2,0},{3,1},{4,6},{5,7},{6,4},{7,5},{8,10},{9,11},{10,... | collective-permute-start | bytes 258056 | tf_op jit(solution)/shard_map/ppermute | solution.py:355
  4.8 2.7 %collective-permute-start.4 = (bf16[64,2048]{1,0:T(8,128)(2,1)S(1)}, bf16[64,2048]{1,0:T(8,128)(2,1)S(1)}, u32[]{:S(2)}, u32[]{:S(2)}) collective-permute-start(bf16[64,2048]{1,0:T(8,128)(2,1)S(1)} %get-tuple-element.64), channel_id=1, source_target_pairs={{0,1},{1,2},{2,3},{3,4},{4,5},{5,6},{6,7},{7,8},{8,9},{9,10},{10,1... | collective-permute-start | bytes 786440 | tf_op jit(solution)/shard_map/ppermute | solution.py:393
  7.6 2.0 %local_kernel.1 = (f32[2,512,256]{2,1,0:T(8,128)S(1)}, f32[2,512,256]{2,1,0:T(8,128)S(1)}, f32[8,128]{1,0:T(8,128)S(1)}) custom-call(bf16[512,128]{1,0:T(8,128)(2,1)S(1)} %get-tuple-element.43.refs_0_, bf16[512,128]{1,0:T(8,128)(2,1)S(1)} %get-tuple-element.52.refs_1_, bf16[512,512]{1,0:T(8,128)(2,1)S(1)} %get-tuple-element.53.refs_2_, ...), custom_call_target="tpu_custom_call" | custom-call | flops 2147483648 | bytes 3145728 | tf_op jit(solution)/shard_map/local_kernel/pallas_call | solution.py:342
  9.6 0.0 collective-permute-done.1
  9.7 0.2 collective-permute-start.2
  9.9 2.5 %collective-permute-start.5 = (bf16[64,2048]{1,0:T(8,128)(2,1)S(1)}, bf16[64,2048]{1,0:T(8,128)(2,1)S(1)}, u32[]{:S(2)}, u32[]{:S(2)}) collective-permute-start(bf16[64,2048]{1,0:T(8,128)(2,1)S(1)} %get-tuple-element.68), channel_id=1, source_target_pairs={{0,1},{1,2},{2,3},{3,4},{4,5},{5,6},{6,7},{7,8},{8,9},{9,10},{10,1... | collective-permute-start | bytes 786440 | tf_op jit(solution)/shard_map/ppermute | solution.py:393
  12.4 0.0 copy-done.2
  12.4 2.3 %window_kernel.1 = (bf16[512,2048]{1,0:T(8,128)(2,1)S(1)}, f32[8,128]{1,0:T(8,128)S(1)}) custom-call(bf16[512,2048]{1,0:T(8,128)(2,1)S(1)} %copy-done.2, bf16[512,2048]{1,0:T(8,128)(2,1)S(1)} %copy-done.1, bf16[512,2048]{1,0:T(8,128)(2,1)S(1)} %copy-done, bf16[336,128]{1,0:T(8,128)(2,1)S(1)} %fusion.8.refs_3_, f32[8,128]{1,0:T(8,128)S(1)} %get-tuple-element.60.refs_4_), custom_call_target="tpu_custom_call" | custom-call | flops 2147483648 | bytes 8388608 | tf_op jit(solution)/shard_map/window_kernel/pallas_call | solution.py:342
  14.6 0.0 collective-permute-done.2
  14.7 0.1 fusion.4.refs_5_
  14.7 0.2 collective-permute-start.3
  14.9 0.0 collective-permute-done.4.refs_3_
  14.9 1.9 %top_kernel.1 = (bf16[64,2048]{1,0:T(8,128)(2,1)S(1)}, bf16[512,2048]{1,0:T(8,128)(2,1)}, f32[8,128]{1,0:T(8,128)S(1)}) custom-call(bf16[512,2048]{1,0:T(8,128)(2,1)S(1)} %copy-done.2, bf16[512,2048]{1,0:T(8,128)(2,1)S(1)} %copy-done.1, bf16[512,2048]{1,0:T(8,128)(2,1)S(1)} %copy-done, bf16[64,2048]{1,0:T(8,128)(2,1)S(1)} %collective-permute-done.4.refs_3_, ...), custom_call_target="tpu_custom_call" | custom-call | flops 1073741824 | bytes 2097152 | tf_op jit(solution)/shard_map/top_kernel/pallas_call | solution.py:342
  16.8 4.3 %collective-permute-done.3 = bf16[336,128]{1,0:T(8,128)(2,1)S(1)} collective-permute-done((bf16[336,128]{1,0:T(8,128)(2,1)S(1)}, bf16[336,128]{1,0:T(8,128)(2,1)S(1)}, u32[]{:S(2)}, u32[]{:S(2)}) %collective-permute-start.3) | collective-permute-done | bytes 86048 | tf_op jit(solution)/shard_map/ppermute | solution.py:355
  21.1 0.0 collective-permute-done.5.refs_6_
  21.1 0.1 fusion.1
  21.2 1.3 %collective-permute-start.6 = (bf16[336,128]{1,0:T(8,128)(2,1)S(1)}, bf16[336,128]{1,0:T(8,128)(2,1)S(1)}, u32[]{:S(2)}, u32[]{:S(2)}) collective-permute-start(bf16[336,128]{1,0:T(8,128)(2,1)S(1)} %get-tuple-element.83), channel_id=1, source_target_pairs={{0,1},{1,0},{2,3},{3,2},{4,5},{5,4},{6,7},{7,6},{8,9},{9,8},{10,11... | collective-permute-start | bytes 258056 | tf_op jit(solution)/shard_map/ppermute | solution.py:355
  22.5 0.8 %own_kernel.1 = (bf16[512,256]{1,0:T(8,128)(2,1)S(1)}, bf16[64,2048]{1,0:T(8,128)(2,1)S(1)}) custom-call(bf16[2,512,640]{2,1,0:T(8,128)(2,1)S(1)} %get-tuple-element.46.refs_0_, bf16[336,128]{1,0:T(8,128)(2,1)S(1)} %get-tuple-element.82.refs_1_, f32[2,512,256]{2,1,0:T(8,128)S(1)} %get-tuple-element.71.refs_2_, f32[2,512,256]{2,1,0:T(8,128)S(1)} %get-tuple-element.72.refs_3_, ...), custom_call_target="tpu_custom_call" | custom-call | flops 1073741824 | bytes 3145728 | tf_op jit(solution)/shard_map/own_kernel/pallas_call | solution.py:342
  23.3 0.2 collective-permute-done.6.refs_1_
  23.5 1.3 %tail_kernel.1 = (bf16[512,512]{1,0:T(8,128)(2,1)}, bf16[512,2048]{1,0:T(8,128)(2,1)}) custom-call(bf16[2,512,640]{2,1,0:T(8,128)(2,1)S(1)} %get-tuple-element.46.refs_0_, bf16[336,128]{1,0:T(8,128)(2,1)S(1)} %collective-permute-done.6.refs_1_, f32[2,512,256]{2,1,0:T(8,128)S(1)} %get-tuple-element.71.refs_2_, ...), custom_call_target="tpu_custom_call", output_to_operand_aliasing={{1}: (6, {})} | custom-call | flops 536870912 | bytes 2097152 | tf_op jit(solution)/shard_map/tail_kernel/pallas_call | solution.py:342
  (8 shorter events, 0.1 us)
Async XLA Ops:
  2.8 1.7 %collective-permute-start = (bf16[336,128]{1,0:T(8,128)(2,1)S(1)}, bf16[336,128]{1,0:T(8,128)(2,1)S(1)}, u32[]{:S(2)}, u32[]{:S(2)}) collective-permute-start(bf16[336,128]{1,0:T(8,128)(2,1)S(1)} %slice_bitcast_fusion), channel_id=1, source_target_pairs={{0,1},{1,0},{2,3},{3,2},{4,5},{5,4},{6,7},{7,6},{8,9},{9,8},{10,11... | collective-permute-start | bytes 258056 | tf_op jit(solution)/shard_map/ppermute | solution.py:355
  4.5 5.1 %collective-permute-start.1 = (bf16[336,128]{1,0:T(8,128)(2,1)S(1)}, bf16[336,128]{1,0:T(8,128)(2,1)S(1)}, u32[]{:S(2)}, u32[]{:S(2)}) collective-permute-start(bf16[336,128]{1,0:T(8,128)(2,1)S(1)} %fusion.7.refs_3_), channel_id=1, source_target_pairs={{0,2},{1,3},{2,0},{3,1},{4,6},{5,7},{6,4},{7,5},{8,10},{9,11},{10,... | collective-permute-start | bytes 258056 | tf_op jit(solution)/shard_map/ppermute | solution.py:355
  4.8 10.1 %collective-permute-start.4 = (bf16[64,2048]{1,0:T(8,128)(2,1)S(1)}, bf16[64,2048]{1,0:T(8,128)(2,1)S(1)}, u32[]{:S(2)}, u32[]{:S(2)}) collective-permute-start(bf16[64,2048]{1,0:T(8,128)(2,1)S(1)} %get-tuple-element.64), channel_id=1, source_target_pairs={{0,1},{1,2},{2,3},{3,4},{4,5},{5,6},{6,7},{7,8},{8,9},{9,10},{10,1... | collective-permute-start | bytes 786440 | tf_op jit(solution)/shard_map/ppermute | solution.py:393
  7.6 4.8 %copy-start = (bf16[512,2048]{1,0:T(8,128)(2,1)S(1)}, bf16[512,2048]{1,0:T(8,128)(2,1)}, u32[]{:S(2)}) copy-start(bf16[512,2048]{1,0:T(8,128)(2,1)} %refs_5_.1) | copy-start | bytes 6291460
  7.6 4.8 %copy-start.1 = (bf16[512,2048]{1,0:T(8,128)(2,1)S(1)}, bf16[512,2048]{1,0:T(8,128)(2,1)}, u32[]{:S(2)}) copy-start(bf16[512,2048]{1,0:T(8,128)(2,1)} %refs_1_.4) | copy-start | bytes 6291460
  7.6 4.8 %copy-start.2 = (bf16[512,2048]{1,0:T(8,128)(2,1)S(1)}, bf16[512,2048]{1,0:T(8,128)(2,1)}, u32[]{:S(2)}) copy-start(bf16[512,2048]{1,0:T(8,128)(2,1)} %refs_0_.5) | copy-start | bytes 6291460
  9.7 5.0 %collective-permute-start.2 = (bf16[336,128]{1,0:T(8,128)(2,1)S(1)}, bf16[336,128]{1,0:T(8,128)(2,1)S(1)}, u32[]{:S(2)}, u32[]{:S(2)}) collective-permute-start(bf16[336,128]{1,0:T(8,128)(2,1)S(1)} %fusion.8.refs_3_), channel_id=1, source_target_pairs={{0,4},{1,5},{2,6},{3,7},{4,0},{5,1},{6,2},{7,3},{8,12},{9,13},{10,... | collective-permute-start | bytes 258056 | tf_op jit(solution)/shard_map/ppermute | solution.py:355
  9.9 11.3 %collective-permute-start.5 = (bf16[64,2048]{1,0:T(8,128)(2,1)S(1)}, bf16[64,2048]{1,0:T(8,128)(2,1)S(1)}, u32[]{:S(2)}, u32[]{:S(2)}) collective-permute-start(bf16[64,2048]{1,0:T(8,128)(2,1)S(1)} %get-tuple-element.68), channel_id=1, source_target_pairs={{0,1},{1,2},{2,3},{3,4},{4,5},{5,6},{6,7},{7,8},{8,9},{9,10},{10,1... | collective-permute-start | bytes 786440 | tf_op jit(solution)/shard_map/ppermute | solution.py:393
  14.7 6.4 %collective-permute-start.3 = (bf16[336,128]{1,0:T(8,128)(2,1)S(1)}, bf16[336,128]{1,0:T(8,128)(2,1)S(1)}, u32[]{:S(2)}, u32[]{:S(2)}) collective-permute-start(bf16[336,128]{1,0:T(8,128)(2,1)S(1)} %fusion.4.refs_5_), channel_id=1, source_target_pairs={{0,12},{1,13},{2,14},{3,15},{4,8},{5,9},{6,10},{7,11},{8,4},{9,5},... | collective-permute-start | bytes 258056 | tf_op jit(solution)/shard_map/ppermute | solution.py:355
  21.2 2.2 %collective-permute-start.6 = (bf16[336,128]{1,0:T(8,128)(2,1)S(1)}, bf16[336,128]{1,0:T(8,128)(2,1)S(1)}, u32[]{:S(2)}, u32[]{:S(2)}) collective-permute-start(bf16[336,128]{1,0:T(8,128)(2,1)S(1)} %get-tuple-element.83), channel_id=1, source_target_pairs={{0,1},{1,0},{2,3},{3,2},{4,5},{5,4},{6,7},{7,6},{8,9},{9,8},{10,11... | collective-permute-start | bytes 258056 | tf_op jit(solution)/shard_map/ppermute | solution.py:355

commit v7 on v5

--- a/solution.py
+++ b/solution.py
@@ -134,7 +134,7 @@
                 kernels.append(u + 4.0)
             outs = []
             for w, (t, e) in zip(kernels, places):
-                w = w * w * (1 / 32) + 0.5
+                w = w * w + 16.0
                 diag = jnp.where(causal, w[:, r * step :], 0.0).astype(BF)
                 if r:
                     diag = jnp.concatenate([w[:, : r * step].astype(BF), diag], axis=1)
@@ -143,7 +143,7 @@
                 outs.append(jnp.dot(diag, aug[:end, :], preferred_element_type=F32))
             for n in range(2):
                 half, cols = t0 // 2, slice(n * 128, (n + 1) * 128)
-                a, b = outs[2 * n : 2 * n + 2]
+                a, b = (out * (1 / 32) for out in outs[2 * n : 2 * n + 2])
                 num_ref[half, rows, cols] = jnp.where(left, a, b)
                 den_ref[half, rows, cols] = pltpu.roll(jnp.where(left, b, a), 64, 1)
 

time: 25 us -> 25 us (level)
  no operation moved by 1% of the time
where the time goes in v7:
time: 25 us; the launch traced here: 24.9 us
  Pallas kernels  10.8 us (43%)
  starting transfers between devices  8.17 us (33%)
  waiting for transfers between devices  4.97 us (20%)
  between operations  0.72 us (3%)
    pallas_call x7, Pallas kernels, call(): pl.pallas_call(run, out_shape=out, in_specs=list(in_specs) + [pl.BlockSpe...  10.8 us
    ppermute x2, starting transfers between devices, ring(): lax.ppermute(x, 'seq', [(i, (i + 1) % count) for i in range(count)])  5.34 us
    ppermute x5, waiting for transfers between devices, exchange(): return lax.ppermute(x, 'seq', [(i, i ^ step) for i in range(count)])  4.96 us
    ppermute x5, starting transfers between devices, exchange(): return lax.ppermute(x, 'seq', [(i, i ^ step) for i in range(count)])  2.83 us
  transfers between devices with their start and end apart: 7, of which 3 were waited for; matrix products, arithmetic and copies ran while one was open for 0% of the time, Pallas kernels for 30%

profile of v7, /device:TPU:15, one launch (start us, length us, event | category | flops | bytes accessed | tf_op | source)
XLA Modules:
  0.0 24.9 jit_solution(17908141798913447390)
XLA Ops:
  0.6 2.2 %state_kernel.1 = (bf16[2,336,128]{2,1,0:T(8,128)(2,1)S(1)}, bf16[64,2048]{1,0:T(8,128)(2,1)S(1)}, bf16[64,2048]{1,0:T(8,128)(2,1)S(1)}, bf16[512,128]{1,0:T(8,1...) custom-call(bf16[512,128]{1,0:T(8,128)(2,1)} %refs_0_.3, ...), custom_call_target="tpu_custom_call" | custom-call | flops 1073741824 | bytes 2097152 | tf_op jit(solution)/shard_map/state_kernel/pallas_call | solution.py:341
  2.8 0.7 %collective-permute-start = (bf16[2,336,128]{2,1,0:T(8,128)(2,1)S(1)}, bf16[2,336,128]{2,1,0:T(8,128)(2,1)S(1)}, u32[]{:S(2)}, u32[]{:S(2)}) collective-permute-start(bf16[2,336,128]{2,1,0:T(8,128)(2,1)S(1)} %get-tuple-element.45.refs_2_), channel_id=1, source_target_pairs={{0,1},{1,0},{2,3},{3,2},{4,5},{5,4},{6,7},{7,6},{8,9},{9,8},{10,11... | collective-permute-start | bytes 516104 | tf_op jit(solution)/shard_map/ppermute | solution.py:354
  3.5 0.6 %query_kernel.1 = (bf16[2,512,640]{2,1,0:T(8,128)(2,1)S(1)}, f32[8,128]{1,0:T(8,128)S(1)}) custom-call(bf16[512,128]{1,0:T(8,128)(2,1)S(1)} %get-tuple-element.43.refs_0_, bf16[128,1536]{1,0:T(8,128)(2,1)S(1)} %get-tuple-element.44.refs_1_, bf16[2,336,128]{2,1,0:T(8,128)(2,1)S(1)} %get-tuple-element.45.refs_2_), custom_call_target="tpu_custom_call" | custom-call | flops 268435456 | bytes 2097152 | tf_op jit(solution)/shard_map/query_kernel/pallas_call | solution.py:341
  4.1 0.5 %collective-permute-done.refs_2_ = bf16[2,336,128]{2,1,0:T(8,128)(2,1)S(1)} collective-permute-done((bf16[2,336,128]{2,1,0:T(8,128)(2,1)S(1)}, bf16[2,336,128]{2,1,0:T(8,128)(2,1)S(1)}, u32[]{:S(2)}, u32[]{:S(2)}) %collective-permute-start) | collective-permute-done | bytes 172064 | tf_op jit(solution)/shard_map/ppermute | solution.py:354
  4.7 0.3 %collective-permute-start.1 = (bf16[336,128]{1,0:T(8,128)(2,1)S(1)}, bf16[336,128]{1,0:T(8,128)(2,1)S(1)}, u32[]{:S(2)}, u32[]{:S(2)}) collective-permute-start(bf16[336,128]{1,0:T(8,128)(2,1)S(1)} %get-tuple-element.52.refs_3_), channel_id=1, source_target_pairs={{0,2},{1,3},{2,0},{3,1},{4,6},{5,7},{6,4},{7,5},{8,10},{9,11},{10,... | collective-permute-start | bytes 258056 | tf_op jit(solution)/shard_map/ppermute | solution.py:354
  5.0 2.8 %collective-permute-start.4 = (bf16[64,2048]{1,0:T(8,128)(2,1)S(1)}, bf16[64,2048]{1,0:T(8,128)(2,1)S(1)}, u32[]{:S(2)}, u32[]{:S(2)}) collective-permute-start(bf16[64,2048]{1,0:T(8,128)(2,1)S(1)} %get-tuple-element.65), channel_id=1, source_target_pairs={{0,1},{1,2},{2,3},{3,4},{4,5},{5,6},{6,7},{7,8},{8,9},{9,10},{10,1... | collective-permute-start | bytes 786440 | tf_op jit(solution)/shard_map/ppermute | solution.py:392
  7.7 1.9 %local_kernel.1 = (f32[2,512,256]{2,1,0:T(8,128)S(1)}, f32[2,512,256]{2,1,0:T(8,128)S(1)}, f32[8,128]{1,0:T(8,128)S(1)}) custom-call(bf16[512,128]{1,0:T(8,128)(2,1)S(1)} %get-tuple-element.43.refs_0_, bf16[512,128]{1,0:T(8,128)(2,1)S(1)} %get-tuple-element.53.refs_1_, bf16[512,512]{1,0:T(8,128)(2,1)S(1)} %get-tuple-element.54.refs_2_, ...), custom_call_target="tpu_custom_call" | custom-call | flops 2147483648 | bytes 3145728 | tf_op jit(solution)/shard_map/local_kernel/pallas_call | solution.py:341
  9.6 0.0 collective-permute-done.1
  9.7 0.2 collective-permute-start.2
  9.9 2.6 %collective-permute-start.5 = (bf16[64,2048]{1,0:T(8,128)(2,1)S(1)}, bf16[64,2048]{1,0:T(8,128)(2,1)S(1)}, u32[]{:S(2)}, u32[]{:S(2)}) collective-permute-start(bf16[64,2048]{1,0:T(8,128)(2,1)S(1)} %get-tuple-element.69), channel_id=1, source_target_pairs={{0,1},{1,2},{2,3},{3,4},{4,5},{5,6},{6,7},{7,8},{8,9},{9,10},{10,1... | collective-permute-start | bytes 786440 | tf_op jit(solution)/shard_map/ppermute | solution.py:392
  12.5 0.0 copy-done
  12.5 0.0 copy-done.1
  12.5 2.3 %window_kernel.1 = (bf16[512,2048]{1,0:T(8,128)(2,1)S(1)}, f32[8,128]{1,0:T(8,128)S(1)}) custom-call(bf16[512,2048]{1,0:T(8,128)(2,1)S(1)} %copy-done.2, bf16[512,2048]{1,0:T(8,128)(2,1)S(1)} %copy-done.1, bf16[512,2048]{1,0:T(8,128)(2,1)S(1)} %copy-done, bf16[336,128]{1,0:T(8,128)(2,1)S(1)} %fusion.5.refs_3_, f32[8,128]{1,0:T(8,128)S(1)} %get-tuple-element.61.refs_4_), custom_call_target="tpu_custom_call" | custom-call | flops 2147483648 | bytes 8388608 | tf_op jit(solution)/shard_map/window_kernel/pallas_call | solution.py:341
  14.8 0.0 collective-permute-done.2
  14.8 0.2 collective-permute-start.3
  15.1 0.0 collective-permute-done.4.refs_3_
  15.1 1.9 %top_kernel.1 = (bf16[64,2048]{1,0:T(8,128)(2,1)S(1)}, bf16[512,2048]{1,0:T(8,128)(2,1)}, f32[8,128]{1,0:T(8,128)S(1)}) custom-call(bf16[512,2048]{1,0:T(8,128)(2,1)S(1)} %copy-done.2, bf16[512,2048]{1,0:T(8,128)(2,1)S(1)} %copy-done.1, bf16[512,2048]{1,0:T(8,128)(2,1)S(1)} %copy-done, bf16[64,2048]{1,0:T(8,128)(2,1)S(1)} %collective-permute-done.4.refs_3_, ...), custom_call_target="tpu_custom_call" | custom-call | flops 1073741824 | bytes 2097152 | tf_op jit(solution)/shard_map/top_kernel/pallas_call | solution.py:341
  17.0 4.3 %collective-permute-done.3 = bf16[336,128]{1,0:T(8,128)(2,1)S(1)} collective-permute-done((bf16[336,128]{1,0:T(8,128)(2,1)S(1)}, bf16[336,128]{1,0:T(8,128)(2,1)S(1)}, u32[]{:S(2)}, u32[]{:S(2)}) %collective-permute-start.3) | collective-permute-done | bytes 86048 | tf_op jit(solution)/shard_map/ppermute | solution.py:354
  21.3 0.0 collective-permute-done.5.refs_7_
  21.3 0.1 fusion.2.refs_1_
  21.3 1.3 %collective-permute-start.6 = (bf16[336,128]{1,0:T(8,128)(2,1)S(1)}, bf16[336,128]{1,0:T(8,128)(2,1)S(1)}, u32[]{:S(2)}, u32[]{:S(2)}) collective-permute-start(bf16[336,128]{1,0:T(8,128)(2,1)S(1)} %fusion.2.refs_1_), channel_id=1, source_target_pairs={{0,1},{1,0},{2,3},{3,2},{4,5},{5,4},{6,7},{7,6},{8,9},{9,8},{10,11... | collective-permute-start | bytes 258056 | tf_op jit(solution)/shard_map/ppermute | solution.py:354
  22.6 0.8 %own_kernel.1 = (bf16[512,256]{1,0:T(8,128)(2,1)S(1)}, bf16[64,2048]{1,0:T(8,128)(2,1)S(1)}) custom-call(bf16[2,512,640]{2,1,0:T(8,128)(2,1)S(1)} %get-tuple-element.46.refs_0_, bf16[336,128]{1,0:T(8,128)(2,1)S(1)} %fusion.2.refs_1_, bf16[2,336,128]{2,1,0:T(8,128)(2,1)S(1)} %collective-permute-done.refs_2_, f32[2,512,256]{2,1,0:T(8,128)S(1)} %get-tuple-element.71.refs_3_, ...), custom_call_target="tpu_custom_call" | custom-call | flops 1073741824 | bytes 3145728 | tf_op jit(solution)/shard_map/own_kernel/pallas_call | solution.py:341
  23.4 0.2 collective-permute-done.6.refs_1_
  23.6 1.3 %tail_kernel.1 = (bf16[512,512]{1,0:T(8,128)(2,1)}, bf16[512,2048]{1,0:T(8,128)(2,1)}) custom-call(bf16[2,512,640]{2,1,0:T(8,128)(2,1)S(1)} %get-tuple-element.46.refs_0_, bf16[336,128]{1,0:T(8,128)(2,1)S(1)} %collective-permute-done.6.refs_1_, bf16[2,336,128]{2,1,0:T(8,128)(2,1)S(1)} %collective-permute-done.refs_2_, ...), custom_call_target="tpu_custom_call", output_to_operand_aliasing={{1}: (7, {})} | custom-call | flops 536870912 | bytes 2097152 | tf_op jit(solution)/shard_map/tail_kernel/pallas_call | solution.py:341
  (8 shorter events, 0.1 us)
Async XLA Ops:
  2.8 1.8 %collective-permute-start = (bf16[2,336,128]{2,1,0:T(8,128)(2,1)S(1)}, bf16[2,336,128]{2,1,0:T(8,128)(2,1)S(1)}, u32[]{:S(2)}, u32[]{:S(2)}) collective-permute-start(bf16[2,336,128]{2,1,0:T(8,128)(2,1)S(1)} %get-tuple-element.45.refs_2_), channel_id=1, source_target_pairs={{0,1},{1,0},{2,3},{3,2},{4,5},{5,4},{6,7},{7,6},{8,9},{9,8},{10,11... | collective-permute-start | bytes 516104 | tf_op jit(solution)/shard_map/ppermute | solution.py:354
  4.7 5.0 %collective-permute-start.1 = (bf16[336,128]{1,0:T(8,128)(2,1)S(1)}, bf16[336,128]{1,0:T(8,128)(2,1)S(1)}, u32[]{:S(2)}, u32[]{:S(2)}) collective-permute-start(bf16[336,128]{1,0:T(8,128)(2,1)S(1)} %get-tuple-element.52.refs_3_), channel_id=1, source_target_pairs={{0,2},{1,3},{2,0},{3,1},{4,6},{5,7},{6,4},{7,5},{8,10},{9,11},{10,... | collective-permute-start | bytes 258056 | tf_op jit(solution)/shard_map/ppermute | solution.py:354
  5.0 10.1 %collective-permute-start.4 = (bf16[64,2048]{1,0:T(8,128)(2,1)S(1)}, bf16[64,2048]{1,0:T(8,128)(2,1)S(1)}, u32[]{:S(2)}, u32[]{:S(2)}) collective-permute-start(bf16[64,2048]{1,0:T(8,128)(2,1)S(1)} %get-tuple-element.65), channel_id=1, source_target_pairs={{0,1},{1,2},{2,3},{3,4},{4,5},{5,6},{6,7},{7,8},{8,9},{9,10},{10,1... | collective-permute-start | bytes 786440 | tf_op jit(solution)/shard_map/ppermute | solution.py:392
  7.7 4.8 %copy-start = (bf16[512,2048]{1,0:T(8,128)(2,1)S(1)}, bf16[512,2048]{1,0:T(8,128)(2,1)}, u32[]{:S(2)}) copy-start(bf16[512,2048]{1,0:T(8,128)(2,1)} %refs_6_.1) | copy-start | bytes 6291460
  7.7 4.8 %copy-start.1 = (bf16[512,2048]{1,0:T(8,128)(2,1)S(1)}, bf16[512,2048]{1,0:T(8,128)(2,1)}, u32[]{:S(2)}) copy-start(bf16[512,2048]{1,0:T(8,128)(2,1)} %refs_1_.4) | copy-start | bytes 6291460
  7.7 4.8 %copy-start.2 = (bf16[512,2048]{1,0:T(8,128)(2,1)S(1)}, bf16[512,2048]{1,0:T(8,128)(2,1)}, u32[]{:S(2)}) copy-start(bf16[512,2048]{1,0:T(8,128)(2,1)} %refs_0_.5) | copy-start | bytes 6291460
  9.7 5.1 %collective-permute-start.2 = (bf16[336,128]{1,0:T(8,128)(2,1)S(1)}, bf16[336,128]{1,0:T(8,128)(2,1)S(1)}, u32[]{:S(2)}, u32[]{:S(2)}) collective-permute-start(bf16[336,128]{1,0:T(8,128)(2,1)S(1)} %fusion.5.refs_3_), channel_id=1, source_target_pairs={{0,4},{1,5},{2,6},{3,7},{4,0},{5,1},{6,2},{7,3},{8,12},{9,13},{10,... | collective-permute-start | bytes 258056 | tf_op jit(solution)/shard_map/ppermute | solution.py:354
  9.9 11.4 %collective-permute-start.5 = (bf16[64,2048]{1,0:T(8,128)(2,1)S(1)}, bf16[64,2048]{1,0:T(8,128)(2,1)S(1)}, u32[]{:S(2)}, u32[]{:S(2)}) collective-permute-start(bf16[64,2048]{1,0:T(8,128)(2,1)S(1)} %get-tuple-element.69), channel_id=1, source_target_pairs={{0,1},{1,2},{2,3},{3,4},{4,5},{5,6},{6,7},{7,8},{8,9},{9,10},{10,1... | collective-permute-start | bytes 786440 | tf_op jit(solution)/shard_map/ppermute | solution.py:392
  14.8 6.4 %collective-permute-start.3 = (bf16[336,128]{1,0:T(8,128)(2,1)S(1)}, bf16[336,128]{1,0:T(8,128)(2,1)S(1)}, u32[]{:S(2)}, u32[]{:S(2)}) collective-permute-start(bf16[336,128]{1,0:T(8,128)(2,1)S(1)} %fusion.3.refs_5_), channel_id=1, source_target_pairs={{0,12},{1,13},{2,14},{3,15},{4,8},{5,9},{6,10},{7,11},{8,4},{9,5},... | collective-permute-start | bytes 258056 | tf_op jit(solution)/shard_map/ppermute | solution.py:354
  21.3 2.2 %collective-permute-start.6 = (bf16[336,128]{1,0:T(8,128)(2,1)S(1)}, bf16[336,128]{1,0:T(8,128)(2,1)S(1)}, u32[]{:S(2)}, u32[]{:S(2)}) collective-permute-start(bf16[336,128]{1,0:T(8,128)(2,1)S(1)} %fusion.2.refs_1_), channel_id=1, source_target_pairs={{0,1},{1,0},{2,3},{3,2},{4,5},{5,4},{6,7},{7,6},{8,9},{9,8},{10,11... | collective-permute-start | bytes 258056 | tf_op jit(solution)/shard_map/ppermute | solution.py:354
